TPU v7x, 256 devices: a whole 4x4x8 slice. The times are simulated.
256 devices in a mesh: leaf: 128 (over y, x, z_lo, core), player: 2 (over z_hi).
Axes of the slice: x: 4, y: 4, z: 8 (z_hi: 2, z_lo: 4; z = z_hi * 4 + z_lo), core: 2. Of those that a mesh axis runs over, the one named last changes fastest.
Arguments:
- chance_reach: float32 [2, 4096, 1326], P('player', 'leaf'), may hold values from 0.02 to 1
- regrets_start: float32 [2, 4096, 1326], P('player', 'leaf'), may hold values from -6 to 6
- pot: float32 [4096], P('leaf'), may hold values from 1 to 8
- parent: int32 [2, 4096], P('player'), may hold values from 0 to 2047, never falling along the last dimension, each value on 1 to 6 neighbouring positions
- hand_cards: int32 [1326, 2], replicated, may hold values from 0 to 51, as said below
- board_cards: int32 [512, 5], P('leaf'), may hold values from 0 to 51, as said below
- hand_rank: int32 [512, 1326], P('leaf'), may hold values from 0 to 1999
Outputs:
- regrets: float32 [2, 4096, 1326], P('player', 'leaf')
- values: float32 [2, 4096, 1326], P('player', 'leaf')
Inputs may be any that keep to these rules, and one draw needn't show every extreme that they name: `parent`: along each row the node ids never fall; each node owns 1 to 6 consecutive leaves, one exactly 6; every id up to 2047 occurs. `hand_cards`: distinct pairs of two different cards, the smaller card first. `board_cards`: five different cards on each board.
All inputs are finite; a program needn't handle non-finite values.
Results may differ from a plain program's by a relative error of at most 0.0003.
Values sent between devices are 32-bit elements; how exact they have to be, the bound alone decides.
No kernel may reach another device: no remote copies, remote signals or barrier semaphores. Data moves between devices by JAX's collectives and lax.ppermute only.
A program may use at most 128 MiB of HBM per device.

v0:
```python
import functools

import jax
import jax.numpy as jnp
from jax import lax
from jax.sharding import Mesh
from jax.sharding import PartitionSpec as P

ITERS = 2
LEAF = ("leaf_0", "leaf_1", "leaf_2", "leaf_3")


DELTA = 0.05
EPSILON = 1e-06
DECK_SIZE = 52


def extended(array, sides, width):
    for axis, dim in sides:
        size, length = (lax.axis_size(axis), array.shape[dim])
        up = [(i, (i + 1) % size) for i in range(size - 1)]
        down = [(j, i) for i, j in up]
        last = lax.slice_in_dim(array, length - width, length, axis=dim)
        first = lax.slice_in_dim(array, 0, width, axis=dim)
        before = lax.ppermute(last, axis, up)
        after = lax.ppermute(first, axis, down)
        array = jnp.concatenate([before, array, after], axis=dim)
    return array


def partner(array, axis, stride):
    return lax.ppermute(array, axis, [(i, i ^ 1 << stride) for i in range(lax.axis_size(axis))])


def over_axes(array, axes):
    return functools.reduce(lax.psum, axes, array)


def holding_table(hand_cards):
    deck_cards = jnp.arange(DECK_SIZE, dtype=jnp.int32)
    holding = (hand_cards[:, 0:1] == deck_cards[None, :]) | (
        hand_cards[:, 1:2] == deck_cards[None, :]
    )
    return holding.astype(jnp.float32)


def board_free(board_cards, holding):
    deck_cards = jnp.arange(DECK_SIZE, dtype=jnp.int32)
    on_board = jnp.any(board_cards[:, :, None] == deck_cards[None, None, :], axis=1).astype(
        jnp.float32
    )
    touched = jnp.dot(on_board, holding.T, precision=lax.Precision.HIGHEST)
    return (touched < 0.5).astype(jnp.float32)


def payoff_matrix(rank_row, free_row, apart_mask):
    ranked = rank_row.astype(jnp.float32)
    sign_table = jnp.sign(ranked[:, None] - ranked[None, :])
    return sign_table * apart_mask * free_row[:, None] * free_row[None, :]


def showdown(opposed, pot, matrices):
    board_count = matrices.shape[0]
    hand_count = opposed.shape[1]
    blocks = opposed.reshape(board_count, -1, hand_count)
    pot_rows = pot.reshape(board_count, -1)

    def one_board(board_items):
        matrix, opp_block, pot_row = board_items
        summed = jnp.dot(opp_block, matrix.T, precision=lax.Precision.HIGHEST)
        return summed * (pot_row[:, None] * (1.0 / hand_count))

    return lax.map(one_board, (matrices, blocks, pot_rows)).reshape(opposed.shape)


def local(chance_reach, regrets_start, pot, parent, hand_cards, board_cards, hand_rank):
    chance = chance_reach[0]
    regrets = regrets_start[0]
    parents = parent[0]
    leaf_rows = chance.shape[0]
    hand_count = chance.shape[1]
    leaf_count = parents.shape[0]
    holding = holding_table(hand_cards)
    apart_mask = (jnp.dot(holding, holding.T, precision=lax.Precision.HIGHEST) < 0.5).astype(
        jnp.float32
    )
    free_rows = board_free(board_cards, holding)
    matrices = lax.map(
        lambda items: payoff_matrix(items[0], items[1], apart_mask), (hand_rank, free_rows)
    )
    first_leaf = lax.axis_index(LEAF) * leaf_rows
    local_parent = lax.dynamic_slice_in_dim(parents, first_leaf, leaf_rows)
    local_ids = local_parent - local_parent[0]
    last_id = local_ids[leaf_rows - 1]
    before_id = parents[jnp.maximum(first_leaf - 1, 0)]
    after_id = parents[jnp.minimum(first_leaf + leaf_rows, leaf_count - 1)]
    joins_before = (first_leaf > 0) & (before_id == local_parent[0])
    joins_after = (first_leaf + leaf_rows < leaf_count) & (after_id == local_parent[leaf_rows - 1])

    def node_totals(values):
        segment_sums = jax.ops.segment_sum(values, local_ids, num_segments=leaf_rows)
        edge_sums = jnp.stack([segment_sums[0], segment_sums[last_id]])
        padded = extended(edge_sums, ((LEAF, 0),), 1)
        segment_sums = segment_sums.at[0].add(jnp.where(joins_before, padded[0], 0.0))
        segment_sums = segment_sums.at[last_id].add(jnp.where(joins_after, padded[3], 0.0))
        return segment_sums[local_ids]

    values = jnp.zeros((leaf_rows, hand_count), jnp.float32)
    for iteration in range(ITERS):
        positive = jnp.maximum(regrets, 0.0) + DELTA
        policy = positive / node_totals(positive)
        own_reach = chance * policy
        opposed = partner(own_reach, "player", 0)
        values = showdown(opposed, pot, matrices)
        instant = values - node_totals(policy * values)
        squares = over_axes(jnp.sum(instant * instant), LEAF)
        norm_scale = jnp.sqrt(squares / (leaf_count * hand_count) + EPSILON)
        regrets = regrets + instant / norm_scale
    return (regrets[None], values[None])


def solution(mesh):
    split = Mesh(
        mesh.devices.reshape(4, 4, 4, 2, mesh.shape["player"]),
        ("leaf_0", "leaf_1", "leaf_2", "leaf_3", "player"),
    )
    placed = (
        P("player", LEAF, None),
        P("player", LEAF, None),
        P(LEAF),
        P("player", None),
        P(),
        P(LEAF, None),
        P(LEAF, None),
    )
    return jax.shard_map(
        local,
        mesh=split,
        in_specs=placed,
        out_specs=(P("player", LEAF, None), P("player", LEAF, None)),
        check_vma=False,
    )
```

profile of v0, /device:TPU:1, one launch (start us, length us, event | category | flops | bytes accessed | tf_op | source)
XLA Modules:
  0.0 263.4 jit_solution(3531040054646606058)
XLA Ops:
  7.4 4.9 %collective-permute-start = (f32[1,1326]{1,0:T(1,128)S(1)}, f32[1,1326]{1,0:T(1,128)S(1)}, u32[]{:S(2)}, u32[]{:S(2)}) collective-permute-start(f32[1,1326]{1,0:T(1,128)S(1)} %constant_dynamic-slice_fusion.6), channel_id=1, source_target_pairs={{0,2},{2,4},{4,6},{6,8},{8,10},{10,12},{12,14},{14,16},{16,18},{18... | collective-permute-start | bytes 15920 | tf_op jit(solution)/shard_map/ppermute | solution.py:25
  14.1 4.5 %fusion.37 = f32[1326,1326]{1,0:T(8,128)} fusion(s32[1326]{0:T(1024)S(1)} %get-tuple-element.183, s32[1326]{0:T(1024)S(1)} %get-tuple-element.182), kind=kOutput, calls=%fused_computation.39 | convolution fusion | flops 186584096 | bytes 7043712 | tf_op jit(solution)/shard_map/dot_general | solution.py:84
  28.8 6.1 %collective-permute-start.2 = (f32[32,1326]{1,0:T(8,128)S(1)}, f32[32,1326]{1,0:T(8,128)S(1)}, u32[]{:S(2)}, u32[]{:S(2)}) collective-permute-start(f32[32,1326]{1,0:T(8,128)S(1)} %bitcast_multiply_fusion.6), channel_id=1, source_target_pairs={{0,1},{1,0},{2,3},{3,2},{4,5},{5,4},{6,7},{7,6},{8,9},{9,8},{10,11... | collective-permute-start | bytes 509192 | tf_op jit(solution)/shard_map/ppermute | solution.py:32
  34.9 30.6 %while.38 = (s32[]{:T(128)}, f32[4,1326,1326]{2,1,0:T(8,128)}, s32[4,1326]{1,0:T(4,128)}, f32[1326,1326]{1,0:T(8,128)}, f32[4,1326]{1,0:T(4,128)S(1)}, /*index=5*/s32[]{:T(128)}) while((s32[]{:T(128)}, f32[4,1326,1326]{2,1,0:T(8,128)}, s32[4,1326]{1,0:T(4,128)}, f32[1326,1326]{1,0:T(8,128)}, f32[4,1326]{1,0:T(4,128)S(1)}, ...), condition=%wide.region_2.3_spmd, body=%wide.region_1.2_spmd.sunk | while | flops 8792708 | bytes 15013161 | solution.py:88
  35.7 6.8 %fusion.91 = f32[4,1326,1326]{2,1,0:T(8,128)} fusion(f32[4,1326,1326]{2,1,0:T(8,128)} %get-tuple-element.336, s32[]{:T(128)} %get-tuple-element.335, f32[1326,1326]{1,0:T(8,128)} %get-tuple-element.344, f32[1326]{0:T(1024)S(1)} %get-tuple-element.317, f32[1326]{0:T(1024)S(1)} %get-tuple-element.318), kind=kLoop, calls=%fused_computation.35.clone.1 | loop fusion | flops 8791380 | bytes 14991872 | tf_op jit(solution)/shard_map/while/body/jit(dynamic_update_index_in_dim)/dynamic_update_slice | solution.py:88
  43.3 6.9 %fusion.91 = f32[4,1326,1326]{2,1,0:T(8,128)} fusion(f32[4,1326,1326]{2,1,0:T(8,128)} %get-tuple-element.336, s32[]{:T(128)} %get-tuple-element.335, f32[1326,1326]{1,0:T(8,128)} %get-tuple-element.344, f32[1326]{0:T(1024)S(1)} %get-tuple-element.317, f32[1326]{0:T(1024)S(1)} %get-tuple-element.318), kind=kLoop, calls=%fused_computation.35.clone.1 | loop fusion | flops 8791380 | bytes 14991872 | tf_op jit(solution)/shard_map/while/body/jit(dynamic_update_index_in_dim)/dynamic_update_slice | solution.py:88
  51.0 6.9 %fusion.91 = f32[4,1326,1326]{2,1,0:T(8,128)} fusion(f32[4,1326,1326]{2,1,0:T(8,128)} %get-tuple-element.336, s32[]{:T(128)} %get-tuple-element.335, f32[1326,1326]{1,0:T(8,128)} %get-tuple-element.344, f32[1326]{0:T(1024)S(1)} %get-tuple-element.317, f32[1326]{0:T(1024)S(1)} %get-tuple-element.318), kind=kLoop, calls=%fused_computation.35.clone.1 | loop fusion | flops 8791380 | bytes 14991872 | tf_op jit(solution)/shard_map/while/body/jit(dynamic_update_index_in_dim)/dynamic_update_slice | solution.py:88
  58.7 6.8 %fusion.91 = f32[4,1326,1326]{2,1,0:T(8,128)} fusion(f32[4,1326,1326]{2,1,0:T(8,128)} %get-tuple-element.336, s32[]{:T(128)} %get-tuple-element.335, f32[1326,1326]{1,0:T(8,128)} %get-tuple-element.344, f32[1326]{0:T(1024)S(1)} %get-tuple-element.317, f32[1326]{0:T(1024)S(1)} %get-tuple-element.318), kind=kLoop, calls=%fused_computation.35.clone.1 | loop fusion | flops 8791380 | bytes 14991872 | tf_op jit(solution)/shard_map/while/body/jit(dynamic_update_index_in_dim)/dynamic_update_slice | solution.py:88
  65.6 36.1 %while.39 = (s32[]{:T(128)}, f32[4,8,1326]{2,1,0:T(8,128)S(1)}, f32[4,8,1326]{2,1,0:T(8,128)S(1)}, f32[4,1326,1326]{2,1,0:T(8,128)}, f32[4,8]{1,0:T(4,128)S(1)}, /*index=5*/s32[]{:T(128)}) while((s32[]{:T(128)}, f32[4,8,1326]{2,1,0:T(8,128)S(1)}, f32[4,8,1326]{2,1,0:T(8,128)S(1)}, f32[4,1326,1326]{2,1,0:T(8,128)}, f32[4,8]{1,0:T(4,128)S(1)}, ...), condition=%wide.region_6.7_spmd, body=%wide.region_5.6_spmd.sunk | while | flops 168805120 | bytes 7571593 | solution.py:73
  65.7 9.0 %fusion.95 = f32[4,8,1326]{2,1,0:T(8,128)S(1)} fusion(f32[4,8,1326]{2,1,0:T(8,128)S(1)} %get-tuple-element.354, s32[]{:T(128)} %get-tuple-element.353, f32[4,1326,1326]{2,1,0:T(8,128)} %get-tuple-element.362, f32[4,8,1326]{2,1,0:T(8,128)S(1)} %get-tuple-element.361, f32[8]{0:T(128)S(1)} %fusion.94), kind=kOutput, calls=%fused_computation.13.clone.1 | convolution fusion | flops 168805104 | bytes 7571456 | tf_op jit(solution)/shard_map/while/body/eval_jaxpr/dot_general | solution.py:70
  74.7 9.0 %fusion.95 = f32[4,8,1326]{2,1,0:T(8,128)S(1)} fusion(f32[4,8,1326]{2,1,0:T(8,128)S(1)} %get-tuple-element.354, s32[]{:T(128)} %get-tuple-element.353, f32[4,1326,1326]{2,1,0:T(8,128)} %get-tuple-element.362, f32[4,8,1326]{2,1,0:T(8,128)S(1)} %get-tuple-element.361, f32[8]{0:T(128)S(1)} %fusion.94), kind=kOutput, calls=%fused_computation.13.clone.1 | convolution fusion | flops 168805104 | bytes 7571456 | tf_op jit(solution)/shard_map/while/body/eval_jaxpr/dot_general | solution.py:70
  83.7 9.0 %fusion.95 = f32[4,8,1326]{2,1,0:T(8,128)S(1)} fusion(f32[4,8,1326]{2,1,0:T(8,128)S(1)} %get-tuple-element.354, s32[]{:T(128)} %get-tuple-element.353, f32[4,1326,1326]{2,1,0:T(8,128)} %get-tuple-element.362, f32[4,8,1326]{2,1,0:T(8,128)S(1)} %get-tuple-element.361, f32[8]{0:T(128)S(1)} %fusion.94), kind=kOutput, calls=%fused_computation.13.clone.1 | convolution fusion | flops 168805104 | bytes 7571456 | tf_op jit(solution)/shard_map/while/body/eval_jaxpr/dot_general | solution.py:70
  92.7 9.0 %fusion.95 = f32[4,8,1326]{2,1,0:T(8,128)S(1)} fusion(f32[4,8,1326]{2,1,0:T(8,128)S(1)} %get-tuple-element.354, s32[]{:T(128)} %get-tuple-element.353, f32[4,1326,1326]{2,1,0:T(8,128)} %get-tuple-element.362, f32[4,8,1326]{2,1,0:T(8,128)S(1)} %get-tuple-element.361, f32[8]{0:T(128)S(1)} %fusion.94), kind=kOutput, calls=%fused_computation.13.clone.1 | convolution fusion | flops 168805104 | bytes 7571456 | tf_op jit(solution)/shard_map/while/body/eval_jaxpr/dot_general | solution.py:70
  102.7 2.4 collective-permute-start.3
  108.0 3.3 %collective-permute-done.4 = f32[1,1326]{1,0:T(1,128)S(1)} collective-permute-done((f32[1,1326]{1,0:T(1,128)S(1)}, f32[1,1326]{1,0:T(1,128)S(1)}, u32[]{:S(2)}, u32[]{:S(2)}) %collective-permute-start.4) | collective-permute-done | bytes 5336 | tf_op jit(solution)/shard_map/ppermute | solution.py:26
  113.4 17.8 %psum.56 = f32[]{:T(128)} all-reduce(f32[]{:T(128)} %fusion.52), channel_id=1, replica_groups=mesh['leaf_0'=4,'leaf_1'=4,'leaf_2'=4,'leaf_3'=2,'player'=2] {'leaf_0'}, use_global_device_ids=true, to_apply=%region_9.10 | all-reduce | flops 1 | bytes 8 | tf_op jit(solution)/shard_map/psum | solution.py:36
  131.2 6.6 %psum.57 = f32[]{:T(128)} all-reduce(f32[]{:T(128)} %psum.56), channel_id=1, replica_groups=mesh['leaf_0'=4,'leaf_1'=4,'leaf_2'=4,'leaf_3'=2,'player'=2] {'leaf_1'}, use_global_device_ids=true, to_apply=%region_10.11 | all-reduce | flops 1 | bytes 8 | tf_op jit(solution)/shard_map/psum | solution.py:36
  137.8 12.9 %psum.58 = f32[]{:T(128)} all-reduce(f32[]{:T(128)} %psum.57), channel_id=1, replica_groups=mesh['leaf_0'=4,'leaf_1'=4,'leaf_2'=4,'leaf_3'=2,'player'=2] {'leaf_2'}, use_global_device_ids=true, to_apply=%region_11.12 | all-reduce | flops 1 | bytes 8 | tf_op jit(solution)/shard_map/psum | solution.py:36
  150.6 3.1 %psum.59 = f32[]{:T(128)} all-reduce(f32[]{:T(128)} %psum.58), channel_id=1, replica_groups=mesh['leaf_0'=4,'leaf_1'=4,'leaf_2'=4,'leaf_3'=2,'player'=2] {'leaf_3'}, use_global_device_ids=true, to_apply=%region_12.13 | all-reduce | flops 1 | bytes 8 | tf_op jit(solution)/shard_map/psum | solution.py:36
  155.5 3.8 %collective-permute-start.5 = (f32[1,1326]{1,0:T(1,128)S(1)}, f32[1,1326]{1,0:T(1,128)S(1)}, u32[]{:S(2)}, u32[]{:S(2)}) collective-permute-start(f32[1,1326]{1,0:T(1,128)S(1)} %constant_dynamic-slice_fusion.3), channel_id=1, source_target_pairs={{0,2},{2,4},{4,6},{6,8},{8,10},{10,12},{12,14},{14,16},{16,18},{18... | collective-permute-start | bytes 15920 | tf_op jit(solution)/shard_map/ppermute | solution.py:25
  162.1 3.4 %collective-permute-done.6 = f32[1,1326]{1,0:T(1,128)S(1)} collective-permute-done((f32[1,1326]{1,0:T(1,128)S(1)}, f32[1,1326]{1,0:T(1,128)S(1)}, u32[]{:S(2)}, u32[]{:S(2)}) %collective-permute-start.6) | collective-permute-done | bytes 5336 | tf_op jit(solution)/shard_map/ppermute | solution.py:26
  167.3 12.1 %collective-permute-done.7 = f32[32,1326]{1,0:T(8,128)S(1)} collective-permute-done((f32[32,1326]{1,0:T(8,128)S(1)}, f32[32,1326]{1,0:T(8,128)S(1)}, u32[]{:S(2)}, u32[]{:S(2)}) %collective-permute-start.7) | collective-permute-done | bytes 169760 | tf_op jit(solution)/shard_map/ppermute | solution.py:32
  179.3 36.1 %while.40 = (s32[]{:T(128)}, f32[4,8,1326]{2,1,0:T(8,128)S(1)}, f32[4,8,1326]{2,1,0:T(8,128)S(1)}, f32[4,1326,1326]{2,1,0:T(8,128)}, f32[4,8]{1,0:T(4,128)S(1)}, /*index=5*/s32[]{:T(128)}) while((s32[]{:T(128)}, f32[4,8,1326]{2,1,0:T(8,128)S(1)}, f32[4,8,1326]{2,1,0:T(8,128)S(1)}, f32[4,1326,1326]{2,1,0:T(8,128)}, f32[4,8]{1,0:T(4,128)S(1)}, ...), condition=%wide.region_15.16_spmd, body=%wide.region_14.15_spmd.sunk | while | flops 168805120 | bytes 7571593 | solution.py:73
  179.4 9.0 %fusion.99 = f32[4,8,1326]{2,1,0:T(8,128)S(1)} fusion(f32[4,8,1326]{2,1,0:T(8,128)S(1)} %get-tuple-element.372, s32[]{:T(128)} %get-tuple-element.371, f32[4,1326,1326]{2,1,0:T(8,128)} %get-tuple-element.380, f32[4,8,1326]{2,1,0:T(8,128)S(1)} %get-tuple-element.379, f32[8]{0:T(128)S(1)} %fusion.98), kind=kOutput, calls=%fused_computation.25.clone.1 | convolution fusion | flops 168805104 | bytes 7571456 | tf_op jit(solution)/shard_map/while/body/eval_jaxpr/dot_general | solution.py:70
  188.4 9.0 %fusion.99 = f32[4,8,1326]{2,1,0:T(8,128)S(1)} fusion(f32[4,8,1326]{2,1,0:T(8,128)S(1)} %get-tuple-element.372, s32[]{:T(128)} %get-tuple-element.371, f32[4,1326,1326]{2,1,0:T(8,128)} %get-tuple-element.380, f32[4,8,1326]{2,1,0:T(8,128)S(1)} %get-tuple-element.379, f32[8]{0:T(128)S(1)} %fusion.98), kind=kOutput, calls=%fused_computation.25.clone.1 | convolution fusion | flops 168805104 | bytes 7571456 | tf_op jit(solution)/shard_map/while/body/eval_jaxpr/dot_general | solution.py:70
  197.4 9.0 %fusion.99 = f32[4,8,1326]{2,1,0:T(8,128)S(1)} fusion(f32[4,8,1326]{2,1,0:T(8,128)S(1)} %get-tuple-element.372, s32[]{:T(128)} %get-tuple-element.371, f32[4,1326,1326]{2,1,0:T(8,128)} %get-tuple-element.380, f32[4,8,1326]{2,1,0:T(8,128)S(1)} %get-tuple-element.379, f32[8]{0:T(128)S(1)} %fusion.98), kind=kOutput, calls=%fused_computation.25.clone.1 | convolution fusion | flops 168805104 | bytes 7571456 | tf_op jit(solution)/shard_map/while/body/eval_jaxpr/dot_general | solution.py:70
  206.4 9.0 %fusion.99 = f32[4,8,1326]{2,1,0:T(8,128)S(1)} fusion(f32[4,8,1326]{2,1,0:T(8,128)S(1)} %get-tuple-element.372, s32[]{:T(128)} %get-tuple-element.371, f32[4,1326,1326]{2,1,0:T(8,128)} %get-tuple-element.380, f32[4,8,1326]{2,1,0:T(8,128)S(1)} %get-tuple-element.379, f32[8]{0:T(128)S(1)} %fusion.98), kind=kOutput, calls=%fused_computation.25.clone.1 | convolution fusion | flops 168805104 | bytes 7571456 | tf_op jit(solution)/shard_map/while/body/eval_jaxpr/dot_general | solution.py:70
  221.7 3.0 %collective-permute-done.9 = f32[1,1326]{1,0:T(1,128)S(1)} collective-permute-done((f32[1,1326]{1,0:T(1,128)S(1)}, f32[1,1326]{1,0:T(1,128)S(1)}, u32[]{:S(2)}, u32[]{:S(2)}) %collective-permute-start.9) | collective-permute-done | bytes 5336 | tf_op jit(solution)/shard_map/ppermute | solution.py:26
  226.8 12.4 %psum.60 = f32[]{:T(128)} all-reduce(f32[]{:T(128)} %fusion.47), channel_id=1, replica_groups=mesh['leaf_0'=4,'leaf_1'=4,'leaf_2'=4,'leaf_3'=2,'player'=2] {'leaf_0'}, use_global_device_ids=true, to_apply=%region_18.19 | all-reduce | flops 1 | bytes 8 | tf_op jit(solution)/shard_map/psum | solution.py:36
  239.2 6.6 %psum.61 = f32[]{:T(128)} all-reduce(f32[]{:T(128)} %psum.60), channel_id=1, replica_groups=mesh['leaf_0'=4,'leaf_1'=4,'leaf_2'=4,'leaf_3'=2,'player'=2] {'leaf_1'}, use_global_device_ids=true, to_apply=%region_19.20 | all-reduce | flops 1 | bytes 8 | tf_op jit(solution)/shard_map/psum | solution.py:36
  245.8 13.1 %psum.62 = f32[]{:T(128)} all-reduce(f32[]{:T(128)} %psum.61), channel_id=1, replica_groups=mesh['leaf_0'=4,'leaf_1'=4,'leaf_2'=4,'leaf_3'=2,'player'=2] {'leaf_2'}, use_global_device_ids=true, to_apply=%region_20.21 | all-reduce | flops 1 | bytes 8 | tf_op jit(solution)/shard_map/psum | solution.py:36
  258.9 3.1 %psum.63 = f32[]{:T(128)} all-reduce(f32[]{:T(128)} %psum.62), channel_id=1, replica_groups=mesh['leaf_0'=4,'leaf_1'=4,'leaf_2'=4,'leaf_3'=2,'player'=2] {'leaf_3'}, use_global_device_ids=true, to_apply=%region_21.22 | all-reduce | flops 1 | bytes 8 | tf_op jit(solution)/shard_map/psum | solution.py:36
  (83 shorter events, 37.7 us)
Async XLA Ops:
  7.4 15.0 %collective-permute-start = (f32[1,1326]{1,0:T(1,128)S(1)}, f32[1,1326]{1,0:T(1,128)S(1)}, u32[]{:S(2)}, u32[]{:S(2)}) collective-permute-start(f32[1,1326]{1,0:T(1,128)S(1)} %constant_dynamic-slice_fusion.6), channel_id=1, source_target_pairs={{0,2},{2,4},{4,6},{6,8},{8,10},{10,12},{12,14},{14,16},{16,18},{18... | collective-permute-start | bytes 15920 | tf_op jit(solution)/shard_map/ppermute | solution.py:25
  14.1 5.1 %copy-start.4 = (s32[2]{0:T(128)S(1)}, s32[2]{0:T(128)}, u32[]{:S(2)}) copy-start(s32[2]{0:T(128)} %constant.258.clone.1) | copy-start | bytes 28
  14.1 14.7 %copy-start = (f32[1,32,1326]{2,1,0:T(8,128)S(1)}, f32[1,32,1326]{2,1,0:T(8,128)}, u32[]{:S(2)}) copy-start(f32[1,32,1326]{2,1,0:T(8,128)} %param.30) | copy-start | bytes 509188
  14.1 14.7 %copy-start.2 = (f32[1,32,1326]{2,1,0:T(8,128)S(1)}, f32[1,32,1326]{2,1,0:T(8,128)}, u32[]{:S(2)}) copy-start(f32[1,32,1326]{2,1,0:T(8,128)} %param.29) | copy-start | bytes 509188
  22.4 4.9 %collective-permute-start.1 = (f32[1,1326]{1,0:T(1,128)S(1)}, f32[1,1326]{1,0:T(1,128)S(1)}, u32[]{:S(2)}, u32[]{:S(2)}) collective-permute-start(f32[1,1326]{1,0:T(1,128)S(1)} %get-tuple-element.226), channel_id=1, source_target_pairs={{2,0},{4,2},{6,4},{8,6},{10,8},{12,10},{14,12},{16,14},{18,16},{20... | collective-permute-start | bytes 15920 | tf_op jit(solution)/shard_map/ppermute | solution.py:26
  28.8 36.8 %collective-permute-start.2 = (f32[32,1326]{1,0:T(8,128)S(1)}, f32[32,1326]{1,0:T(8,128)S(1)}, u32[]{:S(2)}, u32[]{:S(2)}) collective-permute-start(f32[32,1326]{1,0:T(8,128)S(1)} %bitcast_multiply_fusion.6), channel_id=1, source_target_pairs={{0,1},{1,0},{2,3},{3,2},{4,5},{5,4},{6,7},{7,6},{8,9},{9,8},{10,11... | collective-permute-start | bytes 509192 | tf_op jit(solution)/shard_map/ppermute | solution.py:32
  34.9 30.6 %copy-start.3 = (f32[32]{0:T(128)S(1)}, f32[32]{0:T(128)}, u32[]{:S(2)}) copy-start(f32[32]{0:T(128)} %param.31) | copy-start | bytes 388
  102.7 3.1 %collective-permute-start.3 = (f32[1,1326]{1,0:T(1,128)S(1)}, f32[1,1326]{1,0:T(1,128)S(1)}, u32[]{:S(2)}, u32[]{:S(2)}) collective-permute-start(f32[1,1326]{1,0:T(1,128)S(1)} %constant_dynamic-slice_fusion.4), channel_id=1, source_target_pairs={{0,2},{2,4},{4,6},{6,8},{8,10},{10,12},{12,14},{14,16},{16,18},{18... | collective-permute-start | bytes 15920 | tf_op jit(solution)/shard_map/ppermute | solution.py:25
  105.9 5.5 %collective-permute-start.4 = (f32[1,1326]{1,0:T(1,128)S(1)}, f32[1,1326]{1,0:T(1,128)S(1)}, u32[]{:S(2)}, u32[]{:S(2)}) collective-permute-start(f32[1,1326]{1,0:T(1,128)S(1)} %get-tuple-element.224), channel_id=1, source_target_pairs={{2,0},{4,2},{6,4},{8,6},{10,8},{12,10},{14,12},{16,14},{18,16},{20... | collective-permute-start | bytes 15920 | tf_op jit(solution)/shard_map/ppermute | solution.py:26
  155.5 4.6 %collective-permute-start.5 = (f32[1,1326]{1,0:T(1,128)S(1)}, f32[1,1326]{1,0:T(1,128)S(1)}, u32[]{:S(2)}, u32[]{:S(2)}) collective-permute-start(f32[1,1326]{1,0:T(1,128)S(1)} %constant_dynamic-slice_fusion.3), channel_id=1, source_target_pairs={{0,2},{2,4},{4,6},{6,8},{8,10},{10,12},{12,14},{14,16},{16,18},{18... | collective-permute-start | bytes 15920 | tf_op jit(solution)/shard_map/ppermute | solution.py:25
  160.1 5.5 %collective-permute-start.6 = (f32[1,1326]{1,0:T(1,128)S(1)}, f32[1,1326]{1,0:T(1,128)S(1)}, u32[]{:S(2)}, u32[]{:S(2)}) collective-permute-start(f32[1,1326]{1,0:T(1,128)S(1)} %get-tuple-element.222), channel_id=1, source_target_pairs={{2,0},{4,2},{6,4},{8,6},{10,8},{12,10},{14,12},{16,14},{18,16},{20... | collective-permute-start | bytes 15920 | tf_op jit(solution)/shard_map/ppermute | solution.py:26
  167.0 12.3 %collective-permute-start.7 = (f32[32,1326]{1,0:T(8,128)S(1)}, f32[32,1326]{1,0:T(8,128)S(1)}, u32[]{:S(2)}, u32[]{:S(2)}) collective-permute-start(f32[32,1326]{1,0:T(8,128)S(1)} %get-tuple-element.214), channel_id=1, source_target_pairs={{0,1},{1,0},{2,3},{3,2},{4,5},{5,4},{6,7},{7,6},{8,9},{9,8},{10,11... | collective-permute-start | bytes 509192 | tf_op jit(solution)/shard_map/ppermute | solution.py:32
  215.4 48.0 %copy-start.1 = (f32[4,8,1326]{2,1,0:T(8,128)}, f32[4,8,1326]{2,1,0:T(8,128)S(1)}, u32[]{:S(2)}) copy-start(f32[4,8,1326]{2,1,0:T(8,128)S(1)} %get-tuple-element.181) | copy-start | bytes 509188
  216.4 3.1 %collective-permute-start.8 = (f32[1,1326]{1,0:T(1,128)S(1)}, f32[1,1326]{1,0:T(1,128)S(1)}, u32[]{:S(2)}, u32[]{:S(2)}) collective-permute-start(f32[1,1326]{1,0:T(1,128)S(1)} %constant_dynamic-slice_fusion.2), channel_id=1, source_target_pairs={{0,2},{2,4},{4,6},{6,8},{8,10},{10,12},{12,14},{14,16},{16,18},{18... | collective-permute-start | bytes 15920 | tf_op jit(solution)/shard_map/ppermute | solution.py:25
  219.5 5.3 %collective-permute-start.9 = (f32[1,1326]{1,0:T(1,128)S(1)}, f32[1,1326]{1,0:T(1,128)S(1)}, u32[]{:S(2)}, u32[]{:S(2)}) collective-permute-start(f32[1,1326]{1,0:T(1,128)S(1)} %get-tuple-element.220), channel_id=1, source_target_pairs={{2,0},{4,2},{6,4},{8,6},{10,8},{12,10},{14,12},{16,14},{18,16},{20... | collective-permute-start | bytes 15920 | tf_op jit(solution)/shard_map/ppermute | solution.py:26
where the time goes:
time: 264 us; the launch traced here: 263 us
  matrix products  76.9 us (29%)
  blocking collectives  75.5 us (29%)
  other arithmetic  41.5 us (16%)
  starting transfers between devices  27.5 us (10%)
  waiting for transfers between devices  25.8 us (10%)
  local copies, waits for them, and re-layouts  8.85 us (3%)
  between operations  7 us (3%)
    psum x8, blocking collectives, over_axes(): return functools.reduce(lax.psum, axes, array)  75.5 us
    dot_general x8, matrix products, one_board(): summed = jnp.dot(opp_block, matrix.T, precision=lax.Precision.HIGHEST)  71.9 us
    dynamic_update_slice x4, other arithmetic, local(): lax.map(lambda items: payoff_matrix(items[0], items[1], apart_mask), (han...  27.5 us
    ppermute x4, starting transfers between devices, extended(): before = lax.ppermute(last, axis, up)  13.2 us
    ppermute x2, waiting for transfers between devices, partner(): lax.ppermute(array, axis, [(i, i ^ 1 << stride) for i in range(lax.axis_s...  12.1 us
    ppermute x4, waiting for transfers between devices, extended(): after = lax.ppermute(first, axis, down)  11.3 us
    ppermute x4, starting transfers between devices, extended(): after = lax.ppermute(first, axis, down)  7.91 us
    ppermute x2, starting transfers between devices, partner(): lax.ppermute(array, axis, [(i, i ^ 1 << stride) for i in range(lax.axis_s...  6.37 us
  transfers between devices with their start and end apart: 10, of which 8 were waited for; matrix products, arithmetic and copies ran while one was open for 15% of the time, Pallas kernels for 0%

commit v1 on v0

v1 whole, which is shorter than its diff:
```python
import functools

import jax
import jax.numpy as jnp
from jax import lax
from jax.experimental import pallas as pl
from jax.experimental.pallas import tpu as pltpu
from jax.sharding import Mesh
from jax.sharding import PartitionSpec as P

LEAF = ("leaf_0", "leaf_1", "leaf_2", "leaf_3")
DELTA = 0.05
EPSILON = 1e-06
DECK_SIZE = 52

HANDS = 1326
WIDE = 1408
OWN = 32
SIDE = 16
WINDOW = OWN + 2 * SIDE
BOARD_LEAVES = 8
PIECES = 2
BF16 = jnp.bfloat16
F32 = jnp.float32
VMEM = functools.partial(pl.BlockSpec, memory_space=pltpu.VMEM)


def holding_table(hand_cards):
    deck_cards = jnp.arange(128, dtype=jnp.int32)
    holding = (hand_cards[:, 0:1] == deck_cards[None, :]) | (
        hand_cards[:, 1:2] == deck_cards[None, :]
    )
    return jnp.pad(holding, ((0, WIDE - HANDS), (0, 0))).astype(BF16)


ROWS = 32


def build_kernel(holding_ref, rank_ref, matrix_ref, apart_ref, column_ref, *, boards):
    @pl.loop(0, WIDE // 128)
    def _(i):
        rows = pl.ds(pl.multiple_of(i * 128, 128), 128)
        shared = lax.dot_general(
            holding_ref[rows, :],
            holding_ref[...],
            (((1,), (1,)), ((), ())),
            preferred_element_type=F32,
        )
        apart_ref[rows, :] = (1.0 - jnp.minimum(shared, 1.0)).astype(BF16)

    ranks = rank_ref[...]
    for t in range(WIDE // 128):
        lanes = slice(t * 128, (t + 1) * 128)
        tile = jnp.concatenate([ranks[:, lanes], jnp.zeros((120, 128), F32)], axis=0)
        column_ref[lanes, :] = tile.T

    @pl.loop(0, WIDE // ROWS)
    def _(i):
        rows = pl.ds(pl.multiple_of(i * ROWS, ROWS), ROWS)
        column = column_ref[rows, :]
        own = [jnp.broadcast_to(column[:, b : b + 1], (ROWS, 128)) for b in range(boards)]
        for t in range(WIDE // 128):
            lanes = slice(t * 128, (t + 1) * 128)
            apart = apart_ref[rows, lanes]
            minus = -apart
            for b in range(boards):
                gap = (own[b] - rank_ref[b : b + 1, lanes]).astype(BF16)
                matrix_ref[b, rows, lanes] = jnp.minimum(jnp.maximum(gap, minus), apart)


def build(holding, ranks, boards):
    return pl.pallas_call(
        functools.partial(build_kernel, boards=boards),
        out_shape=jax.ShapeDtypeStruct((boards, WIDE, WIDE), BF16),
        in_specs=[VMEM(), VMEM()],
        out_specs=VMEM(),
        scratch_shapes=[pltpu.VMEM((WIDE, WIDE), BF16), pltpu.VMEM((WIDE, 128), F32)],
        compiler_params=pltpu.CompilerParams(vmem_limit_bytes=40 << 20),
        cost_estimate=pl.CostEstimate(
            flops=boards * WIDE * WIDE * 8, bytes_accessed=boards * WIDE * WIDE, transcendentals=0
        ),
        name="build",
    )(holding, ranks)


def node_totals(same, values):
    high = values.astype(BF16)
    rest = values - high.astype(F32)
    middle = rest.astype(BF16)
    low = (rest - middle.astype(F32)).astype(BF16)
    parts = jnp.concatenate([high, middle, low], axis=0)
    return jnp.dot(same, parts, preferred_element_type=F32)


def policy_of(same, regrets):
    positive = jnp.maximum(regrets, 0.0) + DELTA
    return positive / node_totals(same, positive)


def split_terms(reach):
    high = reach.astype(BF16).astype(F32)
    return [high, reach - high]


def joined(out, first):
    middle = first + BOARD_LEAVES
    return out[first:middle] + out[middle : middle + BOARD_LEAVES]


def board_rows(free, boards):
    return jnp.concatenate(
        [jnp.broadcast_to(free[b : b + 1], (BOARD_LEAVES, WIDE)) for b in boards], axis=0
    )


def first_kernel(
    odd_ref,
    regrets_ref,
    chance_ref,
    even_ref,
    cross_ref,
    part_ref,
    edge_ref,
    same_ref,
    free_ref,
    pot_ref,
    own_matrix_ref,
    side_matrix_ref,
    window_ref,
    reached_ref,
    instant_ref,
    sums_ref,
    policy_ref,
    terms_ref,
    values_ref,
):
    odd = odd_ref[0] == 1
    even, cross = even_ref[...], cross_ref[...]
    left = jnp.where(odd, even, cross)
    right = jnp.where(odd, cross, even)
    window_ref[...] = jnp.zeros_like(window_ref)
    reached_ref[...] = jnp.zeros_like(reached_ref)
    policy_ref[...] = jnp.zeros_like(policy_ref)
    low, high = SIDE, SIDE + OWN
    window_ref[0, low - 15 : low, :HANDS] = left[0:15]
    window_ref[0, low:high, :HANDS] = regrets_ref[...]
    window_ref[0, high : high + 15, :HANDS] = right[0:15]
    policy_ref[0, low - 10 : low, :HANDS] = left[15:25]
    policy_ref[0, low:high, :HANDS] = chance_ref[...]
    policy_ref[0, high : high + 10, :HANDS] = right[15:25]
    window_ref[1, low - 10 : low, :HANDS] = edge_ref[0:10]
    window_ref[1, low:high, :HANDS] = part_ref[0:OWN]
    window_ref[1, high : high + 10, :HANDS] = edge_ref[10:20]
    reached_ref[low - 5 : low, :HANDS] = edge_ref[20:25]
    reached_ref[low:high, :HANDS] = part_ref[OWN : 2 * OWN]
    reached_ref[high : high + 5, :HANDS] = edge_ref[25:30]
    free = board_rows(free_ref, range(8))
    reached_ref[...] = reached_ref[...] * free
    terms = []
    for p in range(2):
        chance = policy_ref[0] * free if p == 0 else reached_ref[...]
        policy = policy_of(same_ref[p], window_ref[p])
        policy_ref[p] = policy
        terms.append(split_terms(chance * policy))
    for b in range(8):
        rows = slice(b * BOARD_LEAVES, (b + 1) * BOARD_LEAVES)
        block = jnp.concatenate([term[rows] for player in terms for term in player], axis=0)
        terms_ref[b] = block.astype(BF16)

    def board(b, matrix):
        out = jnp.dot(terms_ref[b], matrix, preferred_element_type=F32)
        rows = slice(b * BOARD_LEAVES, (b + 1) * BOARD_LEAVES)
        factor = pot_ref[rows, 0:1] * (-1.0 / HANDS)
        free = free_ref[b : b + 1, :]
        values_ref[1, rows, :] = joined(out, 0) * factor * free
        values_ref[0, rows, :] = joined(out, PIECES * BOARD_LEAVES) * factor * free

    for b in range(8):
        if 2 <= b < 6:
            board(b, own_matrix_ref[b - 2])
        else:
            board(b, side_matrix_ref[b if b < 2 else b - 4])

    sums = []
    for p in range(2):
        values = values_ref[p]
        instant = values - node_totals(same_ref[p], policy_ref[p] * values)
        instant_ref[p] = instant
        mine = instant[SIDE : SIDE + OWN]
        sums.append(jnp.sum(mine * mine))
    lane = lax.broadcasted_iota(jnp.int32, sums_ref.shape, 1)
    sums_ref[...] = jnp.where(lane == 0, sums[0], jnp.where(lane == 1, sums[1], 0.0))


def first(odd, regrets, chance, even, cross, part, edge, same, free, pot, own_matrix, side_matrix):
    shapes = (
        jax.ShapeDtypeStruct((2, WINDOW, WIDE), F32),
        jax.ShapeDtypeStruct((WINDOW, WIDE), F32),
        jax.ShapeDtypeStruct((2, WINDOW, WIDE), F32),
        jax.ShapeDtypeStruct((128, 128), F32),
    )
    arrays = (regrets, chance, even, cross, part, edge, same, free, pot)
    return pl.pallas_call(
        first_kernel,
        out_shape=shapes,
        in_specs=[pl.BlockSpec(memory_space=pltpu.SMEM)]
        + [VMEM()] * (len(arrays) + 2),
        out_specs=[VMEM()] * len(shapes),
        scratch_shapes=[
            pltpu.VMEM((2, WINDOW, WIDE), F32),
            pltpu.VMEM((8, 2 * PIECES * BOARD_LEAVES, WIDE), BF16),
            pltpu.VMEM((2, WINDOW, WIDE), F32),
        ],
        compiler_params=pltpu.CompilerParams(vmem_limit_bytes=40 << 20),
        name="first",
    )(odd, *arrays, own_matrix, side_matrix)


def second_kernel(
    gathered_ref,
    window_ref,
    reached_ref,
    instant_ref,
    same_ref,
    free_ref,
    pot_ref,
    own_matrix_ref,
    side_matrix_ref,
    out_values_ref,
    moved_ref,
    mine_ref,
    sums_ref,
    policy_ref,
    terms_ref,
    values_ref,
    *,
    count,
):
    values_ref[...] = jnp.zeros_like(values_ref)
    sums = jnp.sum(gathered_ref[...], axis=0, keepdims=True)
    scale = jnp.sqrt(sums / count + EPSILON)
    moved = window_ref[0] + instant_ref[0] / scale[:, 0:1]
    moved_ref[...] = moved[SIDE : SIDE + OWN]
    policy_ref[...] = policy_of(same_ref[0], moved)
    other = window_ref[1] + instant_ref[1] / scale[:, 1:2]
    terms = split_terms(reached_ref[...] * policy_of(same_ref[1], other))
    for b in range(8):
        rows = slice(b * BOARD_LEAVES, (b + 1) * BOARD_LEAVES)
        block = jnp.concatenate([term[rows] for term in terms], axis=0)
        terms_ref[b] = block.astype(BF16)

    def board(b, matrix):
        out = jnp.dot(terms_ref[b], matrix, preferred_element_type=F32)
        rows = slice(b * BOARD_LEAVES, (b + 1) * BOARD_LEAVES)
        factor = pot_ref[rows, 0:1] * (-1.0 / HANDS)
        values_ref[rows, :] = joined(out, 0) * factor * free_ref[b : b + 1, :]

    for b in range(1, 7):
        if 2 <= b < 6:
            board(b, own_matrix_ref[b - 2])
        else:
            board(b, side_matrix_ref[1 if b == 1 else 2])

    values = values_ref[...]
    instant = values - node_totals(same_ref[0], policy_ref[...] * values)
    mine = instant[SIDE : SIDE + OWN]
    mine_ref[...] = mine
    out_values_ref[...] = values[SIDE : SIDE + OWN, :HANDS]
    lane = lax.broadcasted_iota(jnp.int32, sums_ref.shape, 1)
    sums_ref[...] = jnp.where(lane == 0, jnp.sum(mine * mine), 0.0)


def second(gathered, window, reached, instant, same, free, pot, own_matrix, side_matrix, count):
    shapes = (
        jax.ShapeDtypeStruct((OWN, HANDS), F32),
        jax.ShapeDtypeStruct((OWN, WIDE), F32),
        jax.ShapeDtypeStruct((OWN, WIDE), F32),
        jax.ShapeDtypeStruct((128, 128), F32),
    )
    arrays = (gathered, window, reached, instant, same, free, pot)
    return pl.pallas_call(
        functools.partial(second_kernel, count=count),
        out_shape=shapes,
        in_specs=[VMEM()] * (len(arrays) + 2),
        out_specs=[VMEM()] * len(shapes),
        scratch_shapes=[
            pltpu.VMEM((WINDOW, WIDE), F32),
            pltpu.VMEM((8, PIECES * BOARD_LEAVES, WIDE), BF16),
            pltpu.VMEM((WINDOW, WIDE), F32),
        ],
        compiler_params=pltpu.CompilerParams(vmem_limit_bytes=40 << 20),
        name="second",
    )(*arrays, own_matrix, side_matrix)


def local(chance_reach, regrets_start, pot, parent, hand_cards, board_cards, hand_rank):
    chance = chance_reach[0]
    regrets = regrets_start[0]
    index = lax.axis_index(LEAF)
    devices = lax.axis_size(LEAF)
    leaf_count = parent.shape[1]
    odd = index % 2 == 1

    padded = jnp.concatenate(
        [jnp.full((SIDE,), -1, jnp.int32), parent[0], jnp.full((SIDE,), -2, jnp.int32)]
    )
    nodes = lax.dynamic_slice_in_dim(padded, index * OWN, WINDOW).astype(F32)
    ranks = hand_rank.astype(F32)
    held = board_cards[:, :, None, None] == hand_cards.T[None, None]
    free = 1.0 - jnp.any(held, axis=(1, 2)).astype(F32)

    def row(vector):
        return jnp.pad(vector[None], ((0, 0), (0, HANDS - vector.shape[0])))

    swap = [(0, 1), (1, 0)]
    part = lax.ppermute(
        jnp.concatenate([regrets, chance, row(nodes)], axis=0), "player", swap
    )
    last = jnp.concatenate(
        [regrets[OWN - 15 :], chance[OWN - 10 :], ranks[2:4], free[2:4], row(pot[SIDE:])], axis=0
    )
    start = jnp.concatenate(
        [regrets[:15], chance[:10], ranks[0:2], free[0:2], row(pot[:SIDE])], axis=0
    )
    even = lax.ppermute(
        jnp.where(odd, start, last), LEAF, [(i, i ^ 1) for i in range(devices)]
    )
    cross = lax.ppermute(
        jnp.where(odd, last, start),
        LEAF,
        [(i, i + 1) for i in range(1, devices - 1, 2)]
        + [(i + 1, i) for i in range(1, devices - 1, 2)],
    )
    left = jnp.where(odd, even, cross)
    right = jnp.where(odd, cross, even)
    edge = lax.ppermute(
        jnp.concatenate([left[5:15], right[0:10], left[20:25], right[15:20]], axis=0),
        "player",
        swap,
    )

    def widened(array):
        return jnp.pad(array, ((0, 8 - array.shape[0]), (0, WIDE - HANDS)))

    holding = holding_table(hand_cards)
    own_matrix = build(holding, widened(ranks), 4)
    side_matrix = build(holding, widened(jnp.concatenate([left[25:27], right[25:27]], axis=0)), 4)
    all_free = widened(jnp.concatenate([left[27:29], free, right[27:29]], axis=0))
    all_pot = jnp.concatenate([left[29, :SIDE], pot, right[29, :SIDE]])
    all_pot = jnp.broadcast_to(all_pot[:, None], (WINDOW, 128))
    both = jnp.stack([nodes, part[2 * OWN, :WINDOW]])
    same = (both[:, :, None] == both[:, None, :]).astype(BF16)
    same = jnp.concatenate([same, same, same], axis=2)

    def gathered(sums):
        return lax.all_to_all(sums.reshape(devices, 1, 128), LEAF, 0, 0).reshape(128, 128)

    count = float(leaf_count * HANDS)
    window, reached, instant, sums = first(
        odd.astype(jnp.int32)[None], regrets, chance, even, cross, part, edge,
        same, all_free, all_pot, own_matrix, side_matrix,
    )
    values, moved, mine, sums = second(
        gathered(sums), window, reached, instant, same, all_free, all_pot,
        own_matrix, side_matrix, count,
    )
    squares = jnp.sum(gathered(sums)[:, 0])
    scale = jnp.sqrt(squares / count + EPSILON)
    final = (moved + mine / scale)[:, :HANDS]
    return (final[None], values[None])


def solution(mesh):
    split = Mesh(
        mesh.devices.reshape(4, 4, 4, 2, mesh.shape["player"]),
        ("leaf_0", "leaf_1", "leaf_2", "leaf_3", "player"),
    )
    placed = (
        P("player", LEAF, None),
        P("player", LEAF, None),
        P(LEAF),
        P("player", None),
        P(),
        P(LEAF, None),
        P(LEAF, None),
    )
    return jax.shard_map(
        local,
        mesh=split,
        in_specs=placed,
        out_specs=(P("player", LEAF, None), P("player", LEAF, None)),
        check_vma=False,
    )
```

time: 264 us -> 124 us (0.47)
  matrix products: 76.9 us -> 0 us
  Pallas kernels: 0 us -> 62.6 us
  blocking collectives: 75.5 us -> 36.9 us
  other arithmetic: 41.5 us -> 5.29 us
  waiting for transfers between devices: 25.8 us -> 0.01 us
  starting transfers between devices: 27.5 us -> 11.2 us
  between operations: 7 us -> 1.62 us
  local copies, waits for them, and re-layouts: 8.85 us -> 5.71 us
    dot_general x10 -> x0, matrix products: 76.9 us -> none  [the longest x8 71.9 us: one_board(): summed = jnp.dot(opp_block, matrix.T, precision=lax.Precision.HIGHEST)]
    psum x8 -> x0, blocking collectives: 75.5 us -> none  [over_axes(): return functools.reduce(lax.psum, axes, array)]
    pallas_call x0 -> x4, Pallas kernels: none -> 62.6 us  [the longest x2 32.2 us: build(): pl.pallas_call(functools.partial(build_kernel, boards=boards), out_shape=...]
    all_to_all x0 -> x2, blocking collectives: none -> 36.9 us  [gathered(): lax.all_to_all(sums.reshape(devices, 1, 128), LEAF, 0, 0).reshape(128, 128)]
    dynamic_update_slice x4 -> x0, other arithmetic: 27.5 us -> none  [local(): lax.map(lambda items: payoff_matrix(items[0], items[1], apart_mask), (han...]
    ppermute x10 -> x4, waiting for transfers between devices: 25.8 us -> 0.01 us  [the longest x1 0.01 us: local(): lax.ppermute(jnp.concatenate([left[5:15], right[0:10], left[20:25], right...]
    ppermute x10 -> x4, starting transfers between devices: 27.5 us -> 11.2 us  [the longest x1 6.1 us: local(): lax.ppermute(jnp.concatenate([regrets, chance, row(nodes)], axis=0), 'pla...]
    scatter-add x4 -> x0, other arithmetic: 4.16 us -> none  [node_totals(): jax.ops.segment_sum(values, local_ids, num_segments=leaf_rows)]
  transfers between devices with their start and end apart: 10 -> 4, of which waited for: 8 -> 0; matrix products, arithmetic and copies ran while one was open for 15% -> 3% of each run, Pallas kernels for 0% -> 26%
where the time goes in v1:
time: 124 us; the launch traced here: 123 us
  Pallas kernels  62.6 us (50%)
  blocking collectives  36.9 us (30%)
  starting transfers between devices  11.2 us (9%)
  local copies, waits for them, and re-layouts  5.71 us (5%)
  other arithmetic  5.29 us (4%)
  between operations  1.62 us (1%)
    all_to_all x2, blocking collectives, gathered(): lax.all_to_all(sums.reshape(devices, 1, 128), LEAF, 0, 0).reshape(128, 128)  36.9 us
    pallas_call x2, Pallas kernels, build(): pl.pallas_call(functools.partial(build_kernel, boards=boards), out_shape=...  32.2 us
    pallas_call x1, Pallas kernels, first(): pl.pallas_call(first_kernel, out_shape=shapes, in_specs=[pl.BlockSpec(mem...  15.9 us
    pallas_call x1, Pallas kernels, second(): pl.pallas_call(functools.partial(second_kernel, count=count), out_shape=s...  14.5 us
    ppermute x1, starting transfers between devices, local(): lax.ppermute(jnp.concatenate([regrets, chance, row(nodes)], axis=0), 'pla...  6.1 us
    ppermute x1, starting transfers between devices, local(): lax.ppermute(jnp.where(odd, last, start), LEAF, [(i, i + 1) for i in rang...  4.94 us
  transfers between devices with their start and end apart: 4, of which 0 were waited for; matrix products, arithmetic and copies ran while one was open for 3% of the time, Pallas kernels for 26%

profile of v1, /device:TPU:1, one launch (start us, length us, event | category | flops | bytes accessed | tf_op | source)
XLA Modules:
  0.0 123.3 jit_solution(5219537774351293353)
XLA Ops:
  0.6 0.8 slice_bitcast_fusion.6
  1.5 0.8 copy.11
  2.2 0.8 compare_reduce_fusion
  3.1 0.7 convert_element_type.26
  3.8 0.9 slice_bitcast_fusion
  4.8 1.0 slice_bitcast_fusion.1
  5.8 0.2 concatenate.30
  6.0 0.2 concatenate.29
  6.2 4.9 %collective-permute-start.1 = (f32[30,1326]{1,0:T(8,128)S(1)}, f32[30,1326]{1,0:T(8,128)S(1)}, u32[]{:S(2)}, u32[]{:S(2)}) collective-permute-start(f32[30,1326]{1,0:T(8,128)S(1)} %get-tuple-element.22), channel_id=1, source_target_pairs={{2,4},{6,8},{10,12},{14,16},{18,20},{22,24},{26,28},{30,32},{34,36... | collective-permute-start | bytes 477368 | tf_op jit(solution)/shard_map/ppermute | solution.py:328
  11.2 0.1 collective-permute-start
  11.3 0.8 concatenate.31
  12.1 0.1 convert_bitcast_fusion
  12.2 1.0 select_maximum_fusion
  13.2 6.1 %collective-permute-start.2 = (f32[65,1326]{1,0:T(8,128)S(1)}, f32[65,1326]{1,0:T(8,128)S(1)}, u32[]{:S(2)}, u32[]{:S(2)}) collective-permute-start(f32[65,1326]{1,0:T(8,128)S(1)} %select_maximum_fusion), channel_id=1, source_target_pairs={{0,1},{1,0},{2,3},{3,2},{4,5},{5,4},{6,7},{7,6},{8,9},{9,8},{10,11... | collective-permute-start | bytes 1034288 | tf_op jit(solution)/shard_map/ppermute | solution.py:316
  19.3 0.8 slice_reduce_fusion.2
  20.2 0.8 fusion
  21.0 0.1 pad_convert_fusion.holding_ref
  21.0 0.0 copy-start.2
  21.1 0.0 copy-start.1
  21.1 16.1 %build.2.own_matrix_ref = bf16[4,1408,1408]{2,1,0:T(8,128)(2,1)} custom-call(bf16[1408,128]{1,0:T(8,128)(2,1)S(1)} %pad_convert_fusion.holding_ref, f32[8,1408]{1,0:T(8,128)S(1)} %pad.31.rank_ref), custom_call_target="tpu_custom_call" | custom-call | flops 63438848 | bytes 7929856 | tf_op jit(solution)/shard_map/build/pallas_call | solution.py:72
  37.4 0.1 collective-permute-start.3
  37.5 16.1 %build.3.side_matrix_ref = bf16[4,1408,1408]{2,1,0:T(8,128)(2,1)} custom-call(bf16[1408,128]{1,0:T(8,128)(2,1)S(1)} %pad_convert_fusion.holding_ref, f32[8,1408]{1,0:T(8,128)S(1)} %select_maximum_fusion.1.rank_ref), custom_call_target="tpu_custom_call" | custom-call | flops 63438848 | bytes 7929856 | tf_op jit(solution)/shard_map/build/pallas_call | solution.py:72
  53.6 0.1 pad_maximum_fusion.2
  53.7 0.1 broadcast_compare_fusion
  53.8 0.1 add_convert_fusion.same_ref
  53.9 0.1 broadcast_in_dim.37.pot_ref
  54.0 15.9 %first.1 = (f32[2,64,1408]{2,1,0:T(8,128)S(1)}, f32[64,1408]{1,0:T(8,128)S(1)}, f32[2,64,1408]{2,1,0:T(8,128)S(1)}, f32[128,128]{1,0:T(8,128)S(1)}) custom-call(s32[1]{0:T(128)} %bitcast.odd_ref, f32[32,1326]{1,0:T(8,128)S(1)} %bitcast.35, f32[32,1326]{1,0:T(8,128)S(1)} %bitcast.37, f32[30,1326]{1,0:T(8,128)S(1)} %collective-permute-done.even_ref, ...), custom_call_target="tpu_custom_call" | custom-call | tf_op jit(solution)/shard_map/first/pallas_call | solution.py:203
  69.9 21.4 %all_to_all.10 = f32[128,1,128]{2,1,0:T(1,128)S(1)} all-to-all(f32[128,1,128]{2,1,0:T(1,128)S(1)} %bitcast.40), channel_id=1, replica_groups=mesh['leaf_0'=4,'leaf_1'=4,'leaf_2'=4,'leaf_3'=2,'player'=2] {'leaf_0','..., dimensions={0} | all-to-all | bytes 131072 | tf_op jit(solution)/shard_map/all_to_all | solution.py:356
  91.4 14.5 %second.1 = (f32[32,1326]{1,0:T(8,128)}, f32[32,1408]{1,0:T(8,128)S(1)}, f32[32,1408]{1,0:T(8,128)S(1)}, f32[128,128]{1,0:T(8,128)S(1)}) custom-call(f32[128,128]{1,0:T(8,128)S(1)} %bitcast.38, f32[2,64,1408]{2,1,0:T(8,128)S(1)} %get-tuple-element.11.window_ref, f32[64,1408]{1,0:T(8,128)S(1)} %get-tuple-element.12.reached_ref, ...), custom_call_target="tpu_custom_call" | custom-call | tf_op jit(solution)/shard_map/second/pallas_call | solution.py:281
  105.9 15.4 %all_to_all.11 = f32[128,1,128]{2,1,0:T(1,128)S(1)} all-to-all(f32[128,1,128]{2,1,0:T(1,128)S(1)} %bitcast.39), channel_id=1, replica_groups=mesh['leaf_0'=4,'leaf_1'=4,'leaf_2'=4,'leaf_3'=2,'player'=2] {'leaf_0','..., dimensions={0} | all-to-all | bytes 131072 | tf_op jit(solution)/shard_map/all_to_all | solution.py:356
  121.3 0.6 slice_reduce_fusion
  122.6 0.7 fusion.1
  (30 shorter events, 0.3 us)
Async XLA Ops:
  6.2 30.9 %collective-permute-start.1 = (f32[30,1326]{1,0:T(8,128)S(1)}, f32[30,1326]{1,0:T(8,128)S(1)}, u32[]{:S(2)}, u32[]{:S(2)}) collective-permute-start(f32[30,1326]{1,0:T(8,128)S(1)} %get-tuple-element.22), channel_id=1, source_target_pairs={{2,4},{6,8},{10,12},{14,16},{18,20},{22,24},{26,28},{30,32},{34,36... | collective-permute-start | bytes 477368 | tf_op jit(solution)/shard_map/ppermute | solution.py:328
  11.2 26.0 %collective-permute-start = (f32[30,1326]{1,0:T(8,128)S(1)}, f32[30,1326]{1,0:T(8,128)S(1)}, u32[]{:S(2)}, u32[]{:S(2)}) collective-permute-start(f32[30,1326]{1,0:T(8,128)S(1)} %get-tuple-element.23), channel_id=1, source_target_pairs={{0,2},{2,0},{4,6},{6,4},{8,10},{10,8},{12,14},{14,12},{16,18},{18,... | collective-permute-start | bytes 477368 | tf_op jit(solution)/shard_map/ppermute | solution.py:325
  13.2 40.5 %collective-permute-start.2 = (f32[65,1326]{1,0:T(8,128)S(1)}, f32[65,1326]{1,0:T(8,128)S(1)}, u32[]{:S(2)}, u32[]{:S(2)}) collective-permute-start(f32[65,1326]{1,0:T(8,128)S(1)} %select_maximum_fusion), channel_id=1, source_target_pairs={{0,1},{1,0},{2,3},{3,2},{4,5},{5,4},{6,7},{7,6},{8,9},{9,8},{10,11... | collective-permute-start | bytes 1034288 | tf_op jit(solution)/shard_map/ppermute | solution.py:316
  21.0 32.5 %copy-start.2 = (f32[32]{0:T(128)S(1)}, f32[32]{0:T(128)}, u32[]{:S(2)}) copy-start(f32[32]{0:T(128)} %param.9) | copy-start | bytes 388
  21.0 33.0 %copy-start = (f32[1,32,1326]{2,1,0:T(8,128)S(1)}, f32[1,32,1326]{2,1,0:T(8,128)}, u32[]{:S(2)}) copy-start(f32[1,32,1326]{2,1,0:T(8,128)} %param.8) | copy-start | bytes 509188
  21.1 32.9 %copy-start.1 = (f32[1,32,1326]{2,1,0:T(8,128)S(1)}, f32[1,32,1326]{2,1,0:T(8,128)}, u32[]{:S(2)}) copy-start(f32[1,32,1326]{2,1,0:T(8,128)} %param.7) | copy-start | bytes 509188
  37.4 16.6 %collective-permute-start.3 = (f32[30,1326]{1,0:T(8,128)S(1)}, f32[30,1326]{1,0:T(8,128)S(1)}, u32[]{:S(2)}, u32[]{:S(2)}) collective-permute-start(f32[30,1326]{1,0:T(8,128)S(1)} %pad_maximum_fusion), channel_id=1, source_target_pairs={{0,1},{1,0},{2,3},{3,2},{4,5},{5,4},{6,7},{7,6},{8,9},{9,8},{10,11... | collective-permute-start | bytes 477368 | tf_op jit(solution)/shard_map/ppermute | solution.py:336

commit v2 on v1

v2 whole, which is shorter than its diff:
```python
import functools

import jax
import jax.numpy as jnp
from jax import lax
from jax.experimental import pallas as pl
from jax.experimental.pallas import tpu as pltpu
from jax.sharding import Mesh
from jax.sharding import PartitionSpec as P

LEAF = ("leaf_0", "leaf_1", "leaf_2", "leaf_3")
DELTA = 0.05
EPSILON = 1e-06

HANDS = 1326
WIDE = 1408
OWN = 32
SIDE = 16
WINDOW = OWN + 2 * SIDE
BOARD_LEAVES = 8
EDGE = 30
LIMIT = 16 << 20
SMALL = 6 << 20
PIECES = 2
BF16 = jnp.bfloat16
F32 = jnp.float32
VMEM = functools.partial(pl.BlockSpec, memory_space=pltpu.VMEM)


def pack_kernel(
    odd_ref, boards_hbm, pot_ref, regrets_hbm, chance_hbm, rank_hbm, cards_hbm,
    part_ref, even_ref, cross_ref, wide_rank_ref, free_ref, holding_ref,
    board_cards_ref, rank_ref, cards_ref, sems,
):
    regrets_ref, chance_ref = part_ref.at[:OWN], part_ref.at[OWN:]
    copies = [
        pltpu.make_async_copy(source, target, sems.at[at])
        for at, (source, target) in enumerate(
            [
                (regrets_hbm, regrets_ref),
                (chance_hbm, chance_ref),
                (rank_hbm, rank_ref),
                (cards_hbm, cards_ref),
                (boards_hbm, board_cards_ref),
            ]
        )
    ]
    for copy in copies:
        copy.start()
    for copy in copies:
        copy.wait()
    ranks = rank_ref[...].astype(F32)
    lower, upper = cards_ref[0:1, :], cards_ref[1:2, :]
    rows = []
    for b in range(4):
        taken = jnp.zeros((1, HANDS), jnp.bool_)
        for j in range(5):
            card = board_cards_ref[b, j]
            taken = taken | (lower == card) | (upper == card)
        rows.append(jnp.where(taken, 0.0, 1.0))
    wide_rank_ref[...] = jnp.zeros_like(wide_rank_ref)
    free_ref[...] = jnp.zeros_like(free_ref)
    wide_rank_ref[0:4, :HANDS] = ranks
    for b in range(4):
        free_ref[b : b + 1, :HANDS] = rows[b]
    deck = lax.broadcasted_iota(jnp.int32, (128, HANDS), 0)
    holding_ref[...] = jnp.zeros_like(holding_ref)
    holding_ref[:, :HANDS] = jnp.where((deck == lower) | (deck == upper), 1.0, 0.0).astype(BF16)

    def ends(ref, last):
        at = OWN - 15 if last else 0
        ref[0:15] = regrets_ref[at : at + 15]
        at = OWN - 10 if last else 0
        ref[15:25] = chance_ref[at : at + 10]
        at = 2 if last else 0
        ref[25:27] = ranks[at : at + 2]
        ref[27:28] = rows[at]
        ref[28:29] = rows[at + 1]
        ref[29:30] = jnp.zeros((1, HANDS), F32)
        at = SIDE if last else 0
        ref[29:30, 0:128] = pot_ref[at // SIDE : at // SIDE + 1, :]

    @pl.when(odd_ref[0] == 1)
    def _():
        ends(even_ref, False)
        ends(cross_ref, True)

    @pl.when(odd_ref[0] != 1)
    def _():
        ends(even_ref, True)
        ends(cross_ref, False)


SMEM = functools.partial(pl.BlockSpec, memory_space=pltpu.SMEM)
HBM = functools.partial(pl.BlockSpec, memory_space=pltpu.HBM)


def pack(odd, board_cards, pot_rows, regrets, chance, hand_rank, cards):
    shapes = (
        jax.ShapeDtypeStruct((2 * OWN, HANDS), F32),
        jax.ShapeDtypeStruct((EDGE, HANDS), F32),
        jax.ShapeDtypeStruct((EDGE, HANDS), F32),
        jax.ShapeDtypeStruct((8, WIDE), F32),
        jax.ShapeDtypeStruct((8, WIDE), F32),
        jax.ShapeDtypeStruct((128, WIDE), BF16),
    )
    return pl.pallas_call(
        pack_kernel,
        out_shape=shapes,
        in_specs=[SMEM(), HBM(), VMEM(), HBM(), HBM(), HBM(), HBM()],
        out_specs=[VMEM()] * len(shapes),
        scratch_shapes=[
            pltpu.SMEM((4, 5), jnp.int32),
            pltpu.VMEM((4, HANDS), jnp.int32),
            pltpu.VMEM((2, HANDS), jnp.int32),
            pltpu.SemaphoreType.DMA((5,)),
        ],
        compiler_params=pltpu.CompilerParams(vmem_limit_bytes=SMALL),
        name="pack",
    )(odd, board_cards, pot_rows, regrets, chance, hand_rank, cards)


def sides(odd_ref, even_ref, cross_ref, rows):
    odd = odd_ref[0] == 1
    even, cross = even_ref[rows], cross_ref[rows]
    return jnp.where(odd, even, cross), jnp.where(odd, cross, even)


def edges_kernel(odd_ref, even_ref, cross_ref, nodes_ref, token_ref, edge_ref):
    left, right = sides(odd_ref, even_ref, cross_ref, slice(0, 25))
    edge_ref[0:10] = left[5:15]
    edge_ref[10:20] = right[0:10]
    edge_ref[20:25] = left[20:25]
    edge_ref[25:30] = right[15:20]
    edge_ref[30:31] = jnp.zeros((1, HANDS), F32)
    edge_ref[30:31, 0:128] = nodes_ref[...] + token_ref[0:1, :]


def edges(odd, even, cross, nodes, token):
    return pl.pallas_call(
        edges_kernel,
        out_shape=jax.ShapeDtypeStruct((31, HANDS), F32),
        in_specs=[SMEM()] + [VMEM()] * 4,
        out_specs=VMEM(),
        compiler_params=pltpu.CompilerParams(vmem_limit_bytes=SMALL),
        name="edges",
    )(odd, even, cross, nodes, token)


ROWS = 128


def fill(rank_ref, apart_ref, column_ref, targets):
    ranks = rank_ref[...]
    for t in range(WIDE // 128):
        lanes = slice(t * 128, (t + 1) * 128)
        tile = jnp.concatenate([ranks[:, lanes], jnp.zeros((120, 128), F32)], axis=0)
        column_ref[lanes, :] = tile.T

    @pl.loop(0, WIDE // ROWS)
    def _(i):
        rows = pl.ds(pl.multiple_of(i * ROWS, ROWS), ROWS)
        column = column_ref[rows, :]
        own = [jnp.broadcast_to(column[:, b : b + 1], (ROWS, 128)) for b, _, _ in targets]
        for t in range(WIDE // 128):
            lanes = slice(t * 128, (t + 1) * 128)
            apart = apart_ref[rows, lanes]
            minus = -apart
            for at, (b, matrix_ref, slot) in enumerate(targets):
                gap = (own[at] - rank_ref[b : b + 1, lanes]).astype(BF16)
                matrix_ref[slot, rows, lanes] = jnp.minimum(jnp.maximum(gap, minus), apart)


def build_a_kernel(holding_ref, rank_ref, matrix_ref, apart_ref, token_ref, column_ref):
    token_ref[...] = jnp.zeros_like(token_ref)
    holding = holding_ref[...]
    shared = jnp.dot(holding.T, holding, preferred_element_type=F32)
    apart_ref[...] = (1.0 - jnp.minimum(shared, 1.0)).astype(BF16)
    fill(rank_ref, apart_ref, column_ref, [(0, matrix_ref, 0), (1, matrix_ref, 1)])


def build_b_kernel(
    odd_ref, even_ref, cross_ref, own_rank_ref, apart_ref,
    matrix_ref, near_ref, far_ref, rank_ref, column_ref,
):
    left, right = sides(odd_ref, even_ref, cross_ref, slice(25, 27))
    rank_ref[...] = own_rank_ref[...]
    rank_ref[4:6, :HANDS] = left
    rank_ref[6:8, :HANDS] = right
    targets = [(2, matrix_ref, 0), (3, matrix_ref, 1), (5, near_ref, 0), (6, near_ref, 1)]
    fill(rank_ref, apart_ref, column_ref, targets + [(4, far_ref, 0), (7, far_ref, 1)])


def cost(boards):
    return pl.CostEstimate(
        flops=boards * WIDE * WIDE * 8, bytes_accessed=boards * WIDE * WIDE * 2, transcendentals=0
    )


MATRIX = jax.ShapeDtypeStruct((2, WIDE, WIDE), BF16)


def build_a(holding, ranks):
    return pl.pallas_call(
        build_a_kernel,
        out_shape=(
            MATRIX,
            jax.ShapeDtypeStruct((WIDE, WIDE), BF16),
            jax.ShapeDtypeStruct((8, 128), F32),
        ),
        in_specs=[VMEM()] * 2,
        out_specs=[VMEM()] * 3,
        scratch_shapes=[pltpu.VMEM((WIDE, 128), F32)],
        compiler_params=pltpu.CompilerParams(vmem_limit_bytes=LIMIT),
        cost_estimate=cost(2),
        name="build_a",
    )(holding, ranks)


def build_b(odd, even, cross, ranks, apart):
    return pl.pallas_call(
        build_b_kernel,
        out_shape=(MATRIX, MATRIX, MATRIX),
        in_specs=[SMEM()] + [VMEM()] * 4,
        out_specs=[VMEM()] * 3,
        scratch_shapes=[pltpu.VMEM((8, WIDE), F32), pltpu.VMEM((WIDE, 128), F32)],
        compiler_params=pltpu.CompilerParams(vmem_limit_bytes=LIMIT),
        cost_estimate=cost(6),
        name="build_b",
    )(odd, even, cross, ranks, apart)


def node_totals(same, values):
    high = values.astype(BF16)
    rest = values - high.astype(F32)
    middle = rest.astype(BF16)
    low = (rest - middle.astype(F32)).astype(BF16)
    parts = jnp.concatenate([high, middle, low], axis=0)
    return jnp.dot(same, parts, preferred_element_type=F32)


def policy_of(same, regrets):
    positive = jnp.maximum(regrets, 0.0) + DELTA
    return positive / node_totals(same, positive)


def split_terms(reach):
    high = reach.astype(BF16).astype(F32)
    return [high, reach - high]


def joined(out, first):
    middle = first + BOARD_LEAVES
    return out[first:middle] + out[middle : middle + BOARD_LEAVES]


def column_of(row):
    return jnp.broadcast_to(row, (128, 128)).T


def same_node(row):
    equal = jnp.where(jnp.broadcast_to(row, (128, 128)) == column_of(row), 1.0, 0.0)
    equal = equal[:WINDOW, :WINDOW]
    return jnp.concatenate([equal, equal, equal], axis=1).astype(BF16)


def board_rows(free, boards):
    return jnp.concatenate(
        [jnp.broadcast_to(free[b : b + 1], (BOARD_LEAVES, WIDE)) for b in boards], axis=0
    )


def first_kernel(
    odd_ref,
    packed_ref,
    even_ref,
    cross_ref,
    part_ref,
    edge_ref,
    nodes_ref,
    own_free_ref,
    own_pot_ref,
    first_matrix_ref,
    last_matrix_ref,
    near_ref,
    far_ref,
    window_ref,
    reached_ref,
    instant_ref,
    sums_ref,
    same_ref,
    free_ref,
    pot_ref,
    policy_ref,
    terms_ref,
    values_ref,
):
    left, right = sides(odd_ref, even_ref, cross_ref, slice(0, EDGE))
    same_ref[0] = same_node(nodes_ref[...])
    same_ref[1] = same_node(edge_ref[30:31, 0:128])
    free_ref[...] = jnp.zeros_like(free_ref)
    free_ref[0:2, :HANDS] = left[27:29]
    free_ref[2:6] = own_free_ref[0:4]
    free_ref[6:8, :HANDS] = right[27:29]
    pot_ref[0:SIDE] = column_of(left[29:30, 0:128])[:SIDE]
    pot_ref[SIDE : 2 * SIDE] = column_of(own_pot_ref[0:1, :])[:SIDE]
    pot_ref[2 * SIDE : 3 * SIDE] = column_of(own_pot_ref[1:2, :])[:SIDE]
    pot_ref[3 * SIDE : 4 * SIDE] = column_of(right[29:30, 0:128])[:SIDE]
    window_ref[...] = jnp.zeros_like(window_ref)
    reached_ref[...] = jnp.zeros_like(reached_ref)
    policy_ref[...] = jnp.zeros_like(policy_ref)
    low, high = SIDE, SIDE + OWN
    window_ref[0, low - 15 : low, :HANDS] = left[0:15]
    window_ref[0, low:high, :HANDS] = packed_ref[:OWN]
    window_ref[0, high : high + 15, :HANDS] = right[0:15]
    policy_ref[0, low - 10 : low, :HANDS] = left[15:25]
    policy_ref[0, low:high, :HANDS] = packed_ref[OWN:]
    policy_ref[0, high : high + 10, :HANDS] = right[15:25]
    window_ref[1, low - 10 : low, :HANDS] = edge_ref[0:10]
    window_ref[1, low:high, :HANDS] = part_ref[0:OWN]
    window_ref[1, high : high + 10, :HANDS] = edge_ref[10:20]
    reached_ref[low - 5 : low, :HANDS] = edge_ref[20:25]
    reached_ref[low:high, :HANDS] = part_ref[OWN : 2 * OWN]
    reached_ref[high : high + 5, :HANDS] = edge_ref[25:30]
    free = board_rows(free_ref, range(8))
    reached_ref[...] = reached_ref[...] * free
    terms = []
    for p in range(2):
        chance = policy_ref[0] * free if p == 0 else reached_ref[...]
        policy = policy_of(same_ref[p], window_ref[p])
        policy_ref[p] = policy
        terms.append(split_terms(chance * policy))
    for b in range(8):
        rows = slice(b * BOARD_LEAVES, (b + 1) * BOARD_LEAVES)
        block = jnp.concatenate([term[rows] for player in terms for term in player], axis=0)
        terms_ref[b] = block.astype(BF16)

    def board(b, matrix):
        out = jnp.dot(terms_ref[b], matrix, preferred_element_type=F32)
        rows = slice(b * BOARD_LEAVES, (b + 1) * BOARD_LEAVES)
        factor = pot_ref[rows, 0:1] * (-1.0 / HANDS)
        free = free_ref[b : b + 1, :]
        values_ref[1, rows, :] = joined(out, 0) * factor * free
        values_ref[0, rows, :] = joined(out, PIECES * BOARD_LEAVES) * factor * free

    board(2, first_matrix_ref[0])
    board(3, first_matrix_ref[1])
    board(4, last_matrix_ref[0])
    board(5, last_matrix_ref[1])
    board(1, near_ref[0])
    board(6, near_ref[1])
    board(0, far_ref[0])
    board(7, far_ref[1])

    sums = []
    for p in range(2):
        values = values_ref[p]
        instant = values - node_totals(same_ref[p], policy_ref[p] * values)
        instant_ref[p] = instant
        mine = instant[SIDE : SIDE + OWN]
        sums.append(jnp.sum(mine * mine))
    lane = lax.broadcasted_iota(jnp.int32, sums_ref.shape, 1)
    sums_ref[...] = jnp.where(lane == 0, sums[0], jnp.where(lane == 1, sums[1], 0.0))


def first(odd, packed, even, cross, part, edge, nodes, free, pot_rows, matrices):
    shapes = (
        jax.ShapeDtypeStruct((2, WINDOW, WIDE), F32),
        jax.ShapeDtypeStruct((WINDOW, WIDE), F32),
        jax.ShapeDtypeStruct((2, WINDOW, WIDE), F32),
        jax.ShapeDtypeStruct((128, 128), F32),
        jax.ShapeDtypeStruct((2, WINDOW, 3 * WINDOW), BF16),
        jax.ShapeDtypeStruct((8, WIDE), F32),
        jax.ShapeDtypeStruct((WINDOW, 128), F32),
    )
    arrays = (packed, even, cross, part, edge, nodes, free, pot_rows) + matrices
    return pl.pallas_call(
        first_kernel,
        out_shape=shapes,
        in_specs=[SMEM()] + [VMEM()] * len(arrays),
        out_specs=[VMEM()] * len(shapes),
        scratch_shapes=[
            pltpu.VMEM((2, WINDOW, WIDE), F32),
            pltpu.VMEM((8, 2 * PIECES * BOARD_LEAVES, WIDE), BF16),
            pltpu.VMEM((2, WINDOW, WIDE), F32),
        ],
        compiler_params=pltpu.CompilerParams(vmem_limit_bytes=LIMIT),
        name="first",
    )(odd, *arrays)


def second_kernel(
    gathered_ref,
    window_ref,
    reached_ref,
    instant_ref,
    same_ref,
    free_ref,
    pot_ref,
    first_matrix_ref,
    last_matrix_ref,
    near_ref,
    out_values_ref,
    moved_ref,
    mine_ref,
    sums_ref,
    policy_ref,
    terms_ref,
    values_ref,
    *,
    count,
):
    values_ref[...] = jnp.zeros_like(values_ref)
    sums = jnp.sum(gathered_ref[...], axis=0, keepdims=True)
    scale = jnp.sqrt(sums / count + EPSILON)
    moved = window_ref[0] + instant_ref[0] / scale[:, 0:1]
    moved_ref[...] = moved[SIDE : SIDE + OWN]
    policy_ref[...] = policy_of(same_ref[0], moved)
    other = window_ref[1] + instant_ref[1] / scale[:, 1:2]
    terms = split_terms(reached_ref[...] * policy_of(same_ref[1], other))
    for b in range(8):
        rows = slice(b * BOARD_LEAVES, (b + 1) * BOARD_LEAVES)
        block = jnp.concatenate([term[rows] for term in terms], axis=0)
        terms_ref[b] = block.astype(BF16)

    def board(b, matrix):
        out = jnp.dot(terms_ref[b], matrix, preferred_element_type=F32)
        rows = slice(b * BOARD_LEAVES, (b + 1) * BOARD_LEAVES)
        factor = pot_ref[rows, 0:1] * (-1.0 / HANDS)
        values_ref[rows, :] = joined(out, 0) * factor * free_ref[b : b + 1, :]

    board(2, first_matrix_ref[0])
    board(3, first_matrix_ref[1])
    board(4, last_matrix_ref[0])
    board(5, last_matrix_ref[1])
    board(1, near_ref[0])
    board(6, near_ref[1])

    values = values_ref[...]
    instant = values - node_totals(same_ref[0], policy_ref[...] * values)
    mine = instant[SIDE : SIDE + OWN]
    mine_ref[...] = mine
    out_values_ref[...] = values[SIDE : SIDE + OWN, :HANDS]
    lane = lax.broadcasted_iota(jnp.int32, sums_ref.shape, 1)
    sums_ref[...] = jnp.where(lane == 0, jnp.sum(mine * mine), 0.0)


def second(gathered, window, reached, instant, same, free, pot, matrices, count):
    shapes = (
        jax.ShapeDtypeStruct((OWN, HANDS), F32),
        jax.ShapeDtypeStruct((OWN, WIDE), F32),
        jax.ShapeDtypeStruct((OWN, WIDE), F32),
        jax.ShapeDtypeStruct((128, 128), F32),
    )
    arrays = (gathered, window, reached, instant, same, free, pot) + matrices
    return pl.pallas_call(
        functools.partial(second_kernel, count=count),
        out_shape=shapes,
        in_specs=[VMEM()] * len(arrays),
        out_specs=[VMEM()] * len(shapes),
        scratch_shapes=[
            pltpu.VMEM((WINDOW, WIDE), F32),
            pltpu.VMEM((8, PIECES * BOARD_LEAVES, WIDE), BF16),
            pltpu.VMEM((WINDOW, WIDE), F32),
        ],
        compiler_params=pltpu.CompilerParams(vmem_limit_bytes=LIMIT),
        name="second",
    )(*arrays)


def tail_kernel(gathered_ref, moved_ref, mine_ref, out_ref, *, count):
    sums = jnp.sum(gathered_ref[...], axis=0, keepdims=True)
    scale = jnp.sqrt(sums / count + EPSILON)[:, 0:1]
    out_ref[...] = (moved_ref[...] + mine_ref[...] / scale)[:, :HANDS]


def tail(gathered, moved, mine, count):
    return pl.pallas_call(
        functools.partial(tail_kernel, count=count),
        out_shape=jax.ShapeDtypeStruct((OWN, HANDS), F32),
        in_specs=[VMEM()] * 3,
        out_specs=VMEM(),
        compiler_params=pltpu.CompilerParams(vmem_limit_bytes=SMALL),
        name="tail",
    )(gathered, moved, mine)


def local(chance_reach, regrets_start, pot, parent, hand_cards, board_cards, hand_rank):
    chance = chance_reach[0]
    regrets = regrets_start[0]
    index = lax.axis_index(LEAF)
    devices = lax.axis_size(LEAF)
    leaf_count = parent.shape[1]
    odd = lax.rem(index, 2).astype(jnp.int32)[None]

    pot_rows = jnp.pad(pot.reshape(2, SIDE), ((0, 0), (0, 128 - SIDE)))
    packed, even, cross, ranks, free, holding = pack(
        odd, board_cards, pot_rows, regrets, chance, hand_rank, hand_cards.T
    )
    swap = [(0, 1), (1, 0)]
    part = lax.ppermute(packed, "player", swap)
    even = lax.ppermute(even, LEAF, [(i, i ^ 1) for i in range(devices)])
    cross = lax.ppermute(
        cross,
        LEAF,
        [(i, i + 1) for i in range(1, devices - 1, 2)]
        + [(i + 1, i) for i in range(1, devices - 1, 2)],
    )
    padded = jnp.pad(parent[0], (SIDE, 128), constant_values=-1)
    nodes = lax.dynamic_slice_in_dim(padded, index * OWN, 128).astype(F32)[None]
    first_matrix, apart, token = build_a(holding, ranks)
    edge = lax.ppermute(edges(odd, even, cross, nodes, token), "player", swap)
    last_matrix, near, far = build_b(odd, even, cross, ranks, apart)

    def gathered(sums):
        return lax.all_to_all(sums.reshape(devices, 1, 128), LEAF, 0, 0).reshape(128, 128)

    count = float(leaf_count * HANDS)
    window, reached, instant, sums, same, all_free, all_pot = first(
        odd, packed, even, cross, part, edge, nodes, free, pot_rows,
        (first_matrix, last_matrix, near, far),
    )
    values, moved, mine, sums = second(
        gathered(sums), window, reached, instant, same, all_free, all_pot,
        (first_matrix, last_matrix, near), count,
    )
    final = tail(gathered(sums), moved, mine, count)
    return (final[None], values[None])


def solution(mesh):
    split = Mesh(
        mesh.devices.reshape(4, 4, 4, 2, mesh.shape["player"]),
        ("leaf_0", "leaf_1", "leaf_2", "leaf_3", "player"),
    )
    placed = (
        P("player", LEAF, None),
        P("player", LEAF, None),
        P(LEAF),
        P("player", None),
        P(),
        P(LEAF, None),
        P(LEAF, None),
    )
    return jax.shard_map(
        local,
        mesh=split,
        in_specs=placed,
        out_specs=(P("player", LEAF, None), P("player", LEAF, None)),
        check_vma=False,
    )
```

time: 124 us -> 98.4 us (0.79)
  Pallas kernels: 62.6 us -> 24.4 us
  waiting for transfers between devices: 0.01 us -> 12.6 us
  local copies, waits for them, and re-layouts: 5.71 us -> 11 us
  other arithmetic: 5.29 us -> 0.79 us
    pallas_call x3 -> x6, Pallas kernels: 48.1 us -> 19.9 us  [the longest x1 7.52 us: build_b(): pl.pallas_call(build_b_kernel, out_shape=(MATRIX, MATRIX, MATRIX), in_spe...]
    ppermute x4, waiting for transfers between devices: 0.01 us -> 12.6 us  [the longest x1 12.6 us: local(): lax.ppermute(cross, LEAF, [(i, i + 1) for i in range(1, devices - 1, 2)]...]
    pallas_call x1, Pallas kernels: 14.5 us -> 4.52 us  [second(): pl.pallas_call(functools.partial(second_kernel, count=count), out_shape=s...]
    unnamed x7 -> x14, local copies, waits for them, and re-layouts: 0.79 us -> 10.3 us
    slice x11 -> x0, local copies, waits for them, and re-layouts: 2.79 us -> none  [the longest x1 0.95 us: local(): regrets[OWN - 15:]]
    concatenate x6 -> x0, other arithmetic: 1.29 us -> none  [the longest x1 1.04 us: local(): jnp.concatenate([regrets, chance, row(nodes)], axis=0)]
  transfers between devices with their start and end apart: 4 -> 4, of which waited for: 0 -> 1; matrix products, arithmetic and copies ran while one was open for 3% -> 1% of each run, Pallas kernels for 26% -> 12%
where the time goes in v2:
time: 98.4 us; the launch traced here: 97.9 us
  blocking collectives  36.8 us (37%)
  Pallas kernels  24.4 us (25%)
  waiting for transfers between devices  12.6 us (13%)
  starting transfers between devices  11.7 us (12%)
  local copies, waits for them, and re-layouts  11 us (11%)
    all_to_all x2, blocking collectives, gathered(): lax.all_to_all(sums.reshape(devices, 1, 128), LEAF, 0, 0).reshape(128, 128)  36.8 us
    ppermute x1, waiting for transfers between devices, local(): lax.ppermute(cross, LEAF, [(i, i + 1) for i in range(1, devices - 1, 2)]...  12.6 us
    unnamed x14, local copies, waits for them, and re-layouts  10.3 us
    ppermute x1, starting transfers between devices, local(): part = lax.ppermute(packed, 'player', swap)  7.83 us
    pallas_call x1, Pallas kernels, build_b(): pl.pallas_call(build_b_kernel, out_shape=(MATRIX, MATRIX, MATRIX), in_spe...  7.52 us
    pallas_call x1, Pallas kernels, first(): pl.pallas_call(first_kernel, out_shape=shapes, in_specs=[SMEM()] + [VMEM(...  6.1 us
    pallas_call x1, Pallas kernels, second(): pl.pallas_call(functools.partial(second_kernel, count=count), out_shape=s...  4.52 us
    pallas_call x1, Pallas kernels, build_a(): pl.pallas_call(build_a_kernel, out_shape=(MATRIX, jax.ShapeDtypeStruct((W...  4.14 us
  transfers between devices with their start and end apart: 4, of which 1 were waited for; matrix products, arithmetic and copies ran while one was open for 1% of the time, Pallas kernels for 12%

profile of v2, /device:TPU:1, one launch (start us, length us, event | category | flops | bytes accessed | tf_op | source)
XLA Modules:
  0.0 97.9 jit_solution(12256783527367919934)
XLA Ops:
  0.6 0.7 reshape.19
  1.4 0.0 copy-start.2
  1.4 0.9 copy-done.2
  2.3 0.0 copy-start.3
  2.3 0.9 copy-done.3
  3.2 0.0 copy-start.4
  3.2 0.7 copy-done.4
  4.0 0.0 copy-start.5
  4.0 0.7 copy-done.5
  4.7 0.0 copy-start.6
  4.7 0.7 copy-done.6
  5.4 1.3 %pack.1 = (f32[64,1326]{1,0:T(8,128)S(1)}, f32[30,1326]{1,0:T(8,128)S(1)}, f32[30,1326]{1,0:T(8,128)S(1)}, f32[8,1408]{1,0:T(8,128)S(1)}, f32[8,1408]{1,0:T(8,128)S(1)}, /*index=5*/bf16[128,1408]{1,0:T(8,128)(2,1)S(1)}) custom-call(s32[1]{0:T(128)} %bitcast.odd_ref, s32[4,5]{1,0:T(4,128)S(1)} %copy-done.6, f32[2,128]{1,0:T(2,128)S(1)} %pad.8.pot_ref.own_pot_ref, ...), custom_call_target="tpu_custom_call" | custom-call | tf_op jit(solution)/shard_map/pack/pallas_call | solution.py:107
  6.6 7.8 %collective-permute-start.2 = (f32[64,1326]{1,0:T(8,128)S(1)}, f32[64,1326]{1,0:T(8,128)S(1)}, u32[]{:S(2)}, u32[]{:S(2)}) collective-permute-start(f32[64,1326]{1,0:T(8,128)S(1)} %get-tuple-element.25.packed_ref), channel_id=1, source_target_pairs={{0,1},{1,0},{2,3},{3,2},{4,5},{5,4},{6,7},{7,6},{8,9},{9,8},{10,11... | collective-permute-start | bytes 1018376 | tf_op jit(solution)/shard_map/ppermute | solution.py:501
  14.5 1.0 collective-permute-start
  15.4 2.5 %collective-permute-start.1 = (f32[30,1326]{1,0:T(8,128)S(1)}, f32[30,1326]{1,0:T(8,128)S(1)}, u32[]{:S(2)}, u32[]{:S(2)}) collective-permute-start(f32[30,1326]{1,0:T(8,128)S(1)} %get-tuple-element.27), channel_id=1, source_target_pairs={{2,4},{6,8},{10,12},{14,16},{18,20},{22,24},{26,28},{30,32},{34,36... | collective-permute-start | bytes 477368 | tf_op jit(solution)/shard_map/ppermute | solution.py:503
  17.9 4.1 %build_a.1 = (bf16[2,1408,1408]{2,1,0:T(8,128)(2,1)S(1)}, bf16[1408,1408]{1,0:T(8,128)(2,1)S(1)}, f32[8,128]{1,0:T(8,128)S(1)}) custom-call(bf16[128,1408]{1,0:T(8,128)(2,1)S(1)} %get-tuple-element.28.holding_ref, f32[8,1408]{1,0:T(8,128)S(1)} %get-tuple-element.29.rank_ref.own_rank_ref), custom_call_target="tpu_custom_call" | custom-call | flops 31719424 | bytes 7929856 | tf_op jit(solution)/shard_map/build_a/pallas_call | solution.py:204
  22.1 0.8 convert_bitcast_fusion.nodes_ref
  22.9 0.0 collective-permute-done.even_ref
  22.9 12.6 %collective-permute-done.1.cross_ref = f32[30,1326]{1,0:T(8,128)S(1)} collective-permute-done((f32[30,1326]{1,0:T(8,128)S(1)}, f32[30,1326]{1,0:T(8,128)S(1)}, u32[]{:S(2)}, u32[]{:S(2)}) %collective-permute-start.1) | collective-permute-done | bytes 159152 | tf_op jit(solution)/shard_map/ppermute | solution.py:503
  35.5 0.4 collective-permute-start.3
  35.9 7.5 %build_b.1 = (bf16[2,1408,1408]{2,1,0:T(8,128)(2,1)S(1)}, bf16[2,1408,1408]{2,1,0:T(8,128)(2,1)S(1)}, bf16[2,1408,1408]{2,1,0:T(8,128)(2,1)S(1)}) custom-call(s32[1]{0:T(128)} %bitcast.odd_ref, f32[30,1326]{1,0:T(8,128)S(1)} %collective-permute-done.even_ref, f32[30,1326]{1,0:T(8,128)S(1)} %collective-permute-done.1.cross_ref, ...), custom_call_target="tpu_custom_call" | custom-call | flops 95158272 | bytes 23789568 | tf_op jit(solution)/shard_map/build_b/pallas_call | solution.py:221
  43.4 0.0 copy-start
  43.4 3.1 %copy-done = bf16[2,1408,1408]{2,1,0:T(8,128)(2,1)} copy-done((bf16[2,1408,1408]{2,1,0:T(8,128)(2,1)}, bf16[2,1408,1408]{2,1,0:T(8,128)(2,1)S(1)}, u32[]{:S(2)}) %copy-start) | copy-done | bytes 7929880
  46.5 0.0 collective-permute-done.3.edge_ref
  46.5 0.0 collective-permute-done.2.part_ref
  46.5 0.0 copy-start.1
  46.5 3.2 %copy-done.1 = bf16[2,1408,1408]{2,1,0:T(8,128)(2,1)S(1)} copy-done((bf16[2,1408,1408]{2,1,0:T(8,128)(2,1)S(1)}, bf16[2,1408,1408]{2,1,0:T(8,128)(2,1)}, u32[]{:S(2)}) %copy-start.1) | copy-done | bytes 7929880
  49.7 6.1 %first.1 = (f32[2,64,1408]{2,1,0:T(8,128)S(1)}, f32[64,1408]{1,0:T(8,128)S(1)}, f32[2,64,1408]{2,1,0:T(8,128)S(1)}, f32[128,128]{1,0:T(8,128)S(1)}, bf16[2,64,19...) custom-call(s32[1]{0:T(128)} %bitcast.odd_ref, f32[64,1326]{1,0:T(8,128)S(1)} %get-tuple-element.25.packed_ref, ...), custom_call_target="tpu_custom_call" | custom-call | tf_op jit(solution)/shard_map/first/pallas_call | solution.py:377
  55.8 21.3 %all_to_all.10 = f32[128,1,128]{2,1,0:T(1,128)S(1)} all-to-all(f32[128,1,128]{2,1,0:T(1,128)S(1)} %bitcast.21), channel_id=1, replica_groups=mesh['leaf_0'=4,'leaf_1'=4,'leaf_2'=4,'leaf_3'=2,'player'=2] {'leaf_0','..., dimensions={0} | all-to-all | bytes 131072 | tf_op jit(solution)/shard_map/all_to_all | solution.py:516
  77.2 4.5 %second.1 = (f32[32,1326]{1,0:T(8,128)}, f32[32,1408]{1,0:T(8,128)S(1)}, f32[32,1408]{1,0:T(8,128)S(1)}, f32[128,128]{1,0:T(8,128)S(1)}) custom-call(f32[128,128]{1,0:T(8,128)S(1)} %bitcast.17, f32[2,64,1408]{2,1,0:T(8,128)S(1)} %get-tuple-element.38.window_ref, f32[64,1408]{1,0:T(8,128)S(1)} %get-tuple-element.39.reached_ref, ...), custom_call_target="tpu_custom_call" | custom-call | tf_op jit(solution)/shard_map/second/pallas_call | solution.py:456
  81.7 15.4 %all_to_all.11 = f32[128,1,128]{2,1,0:T(1,128)S(1)} all-to-all(f32[128,1,128]{2,1,0:T(1,128)S(1)} %bitcast.22), channel_id=1, replica_groups=mesh['leaf_0'=4,'leaf_1'=4,'leaf_2'=4,'leaf_3'=2,'player'=2] {'leaf_0','..., dimensions={0} | all-to-all | bytes 131072 | tf_op jit(solution)/shard_map/all_to_all | solution.py:516
  97.1 0.8 tail.1
  (2 shorter events, 0.0 us)
Async XLA Ops:
  1.4 0.9 copy-start.2
  2.3 0.9 copy-start.3
  3.2 0.7 copy-start.4
  4.0 0.7 copy-start.5
  4.7 0.7 copy-start.6
  6.6 39.9 %collective-permute-start.2 = (f32[64,1326]{1,0:T(8,128)S(1)}, f32[64,1326]{1,0:T(8,128)S(1)}, u32[]{:S(2)}, u32[]{:S(2)}) collective-permute-start(f32[64,1326]{1,0:T(8,128)S(1)} %get-tuple-element.25.packed_ref), channel_id=1, source_target_pairs={{0,1},{1,0},{2,3},{3,2},{4,5},{5,4},{6,7},{7,6},{8,9},{9,8},{10,11... | collective-permute-start | bytes 1018376 | tf_op jit(solution)/shard_map/ppermute | solution.py:501
  14.5 8.4 %collective-permute-start = (f32[30,1326]{1,0:T(8,128)S(1)}, f32[30,1326]{1,0:T(8,128)S(1)}, u32[]{:S(2)}, u32[]{:S(2)}) collective-permute-start(f32[30,1326]{1,0:T(8,128)S(1)} %get-tuple-element.26), channel_id=1, source_target_pairs={{0,2},{2,0},{4,6},{6,4},{8,10},{10,8},{12,14},{14,12},{16,18},{18,... | collective-permute-start | bytes 477368 | tf_op jit(solution)/shard_map/ppermute | solution.py:502
  15.4 20.0 %collective-permute-start.1 = (f32[30,1326]{1,0:T(8,128)S(1)}, f32[30,1326]{1,0:T(8,128)S(1)}, u32[]{:S(2)}, u32[]{:S(2)}) collective-permute-start(f32[30,1326]{1,0:T(8,128)S(1)} %get-tuple-element.27), channel_id=1, source_target_pairs={{2,4},{6,8},{10,12},{14,16},{18,20},{22,24},{26,28},{30,32},{34,36... | collective-permute-start | bytes 477368 | tf_op jit(solution)/shard_map/ppermute | solution.py:503
  35.5 11.0 %collective-permute-start.3 = (f32[31,1326]{1,0:T(8,128)S(1)}, f32[31,1326]{1,0:T(8,128)S(1)}, u32[]{:S(2)}, u32[]{:S(2)}) collective-permute-start(f32[31,1326]{1,0:T(8,128)S(1)} %edges.1), channel_id=1, source_target_pairs={{0,1},{1,0},{2,3},{3,2},{4,5},{5,4},{6,7},{7,6},{8,9},{9,8},{10,11... | collective-permute-start | bytes 493280 | tf_op jit(solution)/shard_map/ppermute | solution.py:512
  43.4 3.1 %copy-start = (bf16[2,1408,1408]{2,1,0:T(8,128)(2,1)}, bf16[2,1408,1408]{2,1,0:T(8,128)(2,1)S(1)}, u32[]{:S(2)}) copy-start(bf16[2,1408,1408]{2,1,0:T(8,128)(2,1)S(1)} %get-tuple-element.34.last_matrix_ref) | copy-start | bytes 23789572
  46.5 3.3 %copy-start.1 = (bf16[2,1408,1408]{2,1,0:T(8,128)(2,1)S(1)}, bf16[2,1408,1408]{2,1,0:T(8,128)(2,1)}, u32[]{:S(2)}) copy-start(bf16[2,1408,1408]{2,1,0:T(8,128)(2,1)} %copy-done) | copy-start | bytes 23789572

commit v3 on v2

--- a/solution.py
+++ b/solution.py
@@ -19,7 +19,7 @@
 WINDOW = OWN + 2 * SIDE
 BOARD_LEAVES = 8
 EDGE = 30
-LIMIT = 16 << 20
+LIMIT = 10 << 20
 SMALL = 6 << 20
 PIECES = 2
 BF16 = jnp.bfloat16
@@ -28,26 +28,32 @@
 
 
 def pack_kernel(
-    odd_ref, boards_hbm, pot_ref, regrets_hbm, chance_hbm, rank_hbm, cards_hbm,
-    part_ref, even_ref, cross_ref, wide_rank_ref, free_ref, holding_ref,
-    board_cards_ref, rank_ref, cards_ref, sems,
+    place_ref, boards_hbm, pot_ref, regrets_hbm, chance_hbm, rank_hbm, cards_hbm, parent_hbm,
+    part_ref, even_ref, cross_ref, even_other_ref, cross_other_ref,
+    wide_rank_ref, free_ref, holding_ref, pots_ref, nodes_ref,
+    board_cards_ref, rank_ref, cards_ref, parent_ref, sems,
 ):
-    regrets_ref, chance_ref = part_ref.at[:OWN], part_ref.at[OWN:]
+    regrets_ref, chance_ref = part_ref.at[:OWN], part_ref.at[OWN : 2 * OWN]
+    moves = [
+        (boards_hbm, board_cards_ref),
+        (rank_hbm, rank_ref),
+        (cards_hbm, cards_ref),
+        (parent_hbm, parent_ref),
+        (regrets_hbm, regrets_ref),
+        (chance_hbm, chance_ref),
+    ]
     copies = [
         pltpu.make_async_copy(source, target, sems.at[at])
-        for at, (source, target) in enumerate(
-            [
-                (regrets_hbm, regrets_ref),
-                (chance_hbm, chance_ref),
-                (rank_hbm, rank_ref),
-                (cards_hbm, cards_ref),
-                (boards_hbm, board_cards_ref),
-            ]
-        )
+        for at, (source, target) in enumerate(moves)
     ]
     for copy in copies:
         copy.start()
-    for copy in copies:
+    pots_ref[...] = jnp.zeros_like(pots_ref)
+    pots_ref[0:1, 0:OWN] = pot_ref[...]
+    wide_rank_ref[...] = jnp.zeros_like(wide_rank_ref)
+    free_ref[...] = jnp.zeros_like(free_ref)
+    holding_ref[...] = jnp.zeros_like(holding_ref)
+    for copy in copies[:4]:
         copy.wait()
     ranks = rank_ref[...].astype(F32)
     lower, upper = cards_ref[0:1, :], cards_ref[1:2, :]
@@ -58,93 +64,100 @@
             card = board_cards_ref[b, j]
             taken = taken | (lower == card) | (upper == card)
         rows.append(jnp.where(taken, 0.0, 1.0))
-    wide_rank_ref[...] = jnp.zeros_like(wide_rank_ref)
-    free_ref[...] = jnp.zeros_like(free_ref)
     wide_rank_ref[0:4, :HANDS] = ranks
     for b in range(4):
         free_ref[b : b + 1, :HANDS] = rows[b]
     deck = lax.broadcasted_iota(jnp.int32, (128, HANDS), 0)
-    holding_ref[...] = jnp.zeros_like(holding_ref)
     holding_ref[:, :HANDS] = jnp.where((deck == lower) | (deck == upper), 1.0, 0.0).astype(BF16)
 
-    def ends(ref, last):
+    leaves = parent_ref.shape[0] * 128
+    begin = place_ref[0] * OWN - SIDE
+    line = (begin + 128) // 128 - 1
+    held = [
+        parent_ref[pl.ds(jnp.clip(line + j, 0, leaves // 128 - 1), 1), :].astype(F32)
+        for j in range(2)
+    ]
+    held = jnp.broadcast_to(jnp.concatenate(held, axis=1), (8, 256))
+    held = pltpu.roll(held, lax.rem((line + 2) * 128 - begin, 256), 1)[0:1, 0:128]
+    leaf = begin + lax.broadcasted_iota(jnp.int32, (1, 128), 1)
+    held = jnp.where((leaf >= 0) & (leaf < leaves), held, -1.0)
+    nodes_ref[...] = jnp.broadcast_to(held, nodes_ref.shape)
+    for copy in copies[4:]:
+        copy.wait()
+
+    def ends(ref, other_ref, last):
         at = OWN - 15 if last else 0
         ref[0:15] = regrets_ref[at : at + 15]
         at = OWN - 10 if last else 0
         ref[15:25] = chance_ref[at : at + 10]
+        other_ref[0:10] = regrets_ref[at : at + 10]
+        at = OWN - 5 if last else 0
+        other_ref[10:15] = chance_ref[at : at + 5]
+        other_ref[15:16] = jnp.zeros((1, HANDS), F32)
         at = 2 if last else 0
         ref[25:27] = ranks[at : at + 2]
         ref[27:28] = rows[at]
         ref[28:29] = rows[at + 1]
         ref[29:30] = jnp.zeros((1, HANDS), F32)
-        at = SIDE if last else 0
-        ref[29:30, 0:128] = pot_ref[at // SIDE : at // SIDE + 1, :]
-
-    @pl.when(odd_ref[0] == 1)
+        ref[29:30, 0:128] = pots_ref[0:1, :]
+
+    @pl.when(place_ref[1] == 1)
     def _():
-        ends(even_ref, False)
-        ends(cross_ref, True)
-
-    @pl.when(odd_ref[0] != 1)
+        ends(even_ref, even_other_ref, False)
+        ends(cross_ref, cross_other_ref, True)
+
+    @pl.when(place_ref[1] != 1)
     def _():
-        ends(even_ref, True)
-        ends(cross_ref, False)
+        ends(even_ref, even_other_ref, True)
+        ends(cross_ref, cross_other_ref, False)
+
+    part_ref[2 * OWN :] = jnp.zeros((1, HANDS), F32)
+    part_ref[2 * OWN :, 0:128] = held
 
 
 SMEM = functools.partial(pl.BlockSpec, memory_space=pltpu.SMEM)
 HBM = functools.partial(pl.BlockSpec, memory_space=pltpu.HBM)
 
 
-def pack(odd, board_cards, pot_rows, regrets, chance, hand_rank, cards):
+def in_hbm(array):
+    return pltpu.with_memory_space_constraint(array, pltpu.HBM)
+
+
+def pack(place, board_cards, pot_row, regrets, chance, hand_rank, cards, parent):
     shapes = (
-        jax.ShapeDtypeStruct((2 * OWN, HANDS), F32),
+        jax.ShapeDtypeStruct((2 * OWN + 1, HANDS), F32),
         jax.ShapeDtypeStruct((EDGE, HANDS), F32),
         jax.ShapeDtypeStruct((EDGE, HANDS), F32),
+        jax.ShapeDtypeStruct((16, HANDS), F32),
+        jax.ShapeDtypeStruct((16, HANDS), F32),
         jax.ShapeDtypeStruct((8, WIDE), F32),
         jax.ShapeDtypeStruct((8, WIDE), F32),
         jax.ShapeDtypeStruct((128, WIDE), BF16),
-    )
+        jax.ShapeDtypeStruct((8, 128), F32),
+        jax.ShapeDtypeStruct((8, 128), F32),
+    )
+    large = (regrets, chance, hand_rank, cards, parent)
     return pl.pallas_call(
         pack_kernel,
         out_shape=shapes,
-        in_specs=[SMEM(), HBM(), VMEM(), HBM(), HBM(), HBM(), HBM()],
+        in_specs=[SMEM(), HBM(), VMEM()] + [HBM()] * len(large),
         out_specs=[VMEM()] * len(shapes),
         scratch_shapes=[
             pltpu.SMEM((4, 5), jnp.int32),
             pltpu.VMEM((4, HANDS), jnp.int32),
             pltpu.VMEM((2, HANDS), jnp.int32),
-            pltpu.SemaphoreType.DMA((5,)),
+            pltpu.VMEM(parent.shape, jnp.int32),
+            pltpu.SemaphoreType.DMA((6,)),
         ],
         compiler_params=pltpu.CompilerParams(vmem_limit_bytes=SMALL),
         name="pack",
-    )(odd, board_cards, pot_rows, regrets, chance, hand_rank, cards)
-
-
-def sides(odd_ref, even_ref, cross_ref, rows):
-    odd = odd_ref[0] == 1
+    )(place, in_hbm(board_cards), pot_row, *map(in_hbm, large))
+
+
+def sides(place_ref, even_ref, cross_ref, rows):
+    odd = place_ref[1] == 1
     even, cross = even_ref[rows], cross_ref[rows]
     return jnp.where(odd, even, cross), jnp.where(odd, cross, even)
-
-
-def edges_kernel(odd_ref, even_ref, cross_ref, nodes_ref, token_ref, edge_ref):
-    left, right = sides(odd_ref, even_ref, cross_ref, slice(0, 25))
-    edge_ref[0:10] = left[5:15]
-    edge_ref[10:20] = right[0:10]
-    edge_ref[20:25] = left[20:25]
-    edge_ref[25:30] = right[15:20]
-    edge_ref[30:31] = jnp.zeros((1, HANDS), F32)
-    edge_ref[30:31, 0:128] = nodes_ref[...] + token_ref[0:1, :]
-
-
-def edges(odd, even, cross, nodes, token):
-    return pl.pallas_call(
-        edges_kernel,
-        out_shape=jax.ShapeDtypeStruct((31, HANDS), F32),
-        in_specs=[SMEM()] + [VMEM()] * 4,
-        out_specs=VMEM(),
-        compiler_params=pltpu.CompilerParams(vmem_limit_bytes=SMALL),
-        name="edges",
-    )(odd, even, cross, nodes, token)
 
 
 ROWS = 128
@@ -171,63 +184,59 @@
                 matrix_ref[slot, rows, lanes] = jnp.minimum(jnp.maximum(gap, minus), apart)
 
 
-def build_a_kernel(holding_ref, rank_ref, matrix_ref, apart_ref, token_ref, column_ref):
-    token_ref[...] = jnp.zeros_like(token_ref)
+def build_own_kernel(holding_ref, rank_ref, matrix_ref, apart_ref, column_ref):
     holding = holding_ref[...]
-    shared = jnp.dot(holding.T, holding, preferred_element_type=F32)
-    apart_ref[...] = (1.0 - jnp.minimum(shared, 1.0)).astype(BF16)
-    fill(rank_ref, apart_ref, column_ref, [(0, matrix_ref, 0), (1, matrix_ref, 1)])
-
-
-def build_b_kernel(
-    odd_ref, even_ref, cross_ref, own_rank_ref, apart_ref,
-    matrix_ref, near_ref, far_ref, rank_ref, column_ref,
+    half = WIDE // 2
+    for rows in (slice(0, half), slice(half, WIDE)):
+        shared = jnp.dot(holding.T[rows], holding, preferred_element_type=F32)
+        apart_ref[rows, :] = (1.0 - jnp.minimum(shared, 1.0)).astype(BF16)
+    fill(rank_ref, apart_ref, column_ref, [(b, matrix_ref, b) for b in range(4)])
+
+
+def build_side_kernel(
+    place_ref, even_ref, cross_ref, apart_ref, near_ref, far_ref, rank_ref, column_ref
 ):
-    left, right = sides(odd_ref, even_ref, cross_ref, slice(25, 27))
-    rank_ref[...] = own_rank_ref[...]
-    rank_ref[4:6, :HANDS] = left
-    rank_ref[6:8, :HANDS] = right
-    targets = [(2, matrix_ref, 0), (3, matrix_ref, 1), (5, near_ref, 0), (6, near_ref, 1)]
-    fill(rank_ref, apart_ref, column_ref, targets + [(4, far_ref, 0), (7, far_ref, 1)])
-
-
-def cost(boards):
-    return pl.CostEstimate(
-        flops=boards * WIDE * WIDE * 8, bytes_accessed=boards * WIDE * WIDE * 2, transcendentals=0
-    )
-
-
-MATRIX = jax.ShapeDtypeStruct((2, WIDE, WIDE), BF16)
-
-
-def build_a(holding, ranks):
+    left, right = sides(place_ref, even_ref, cross_ref, slice(25, 27))
+    rank_ref[...] = jnp.zeros_like(rank_ref)
+    rank_ref[0:2, :HANDS] = left
+    rank_ref[2:4, :HANDS] = right
+    targets = [(1, near_ref, 0), (2, near_ref, 1), (0, far_ref, 0), (3, far_ref, 1)]
+    fill(rank_ref, apart_ref, column_ref, targets)
+
+
+BUILD_COST = pl.CostEstimate(
+    flops=32 * WIDE * WIDE, bytes_accessed=8 * WIDE * WIDE, transcendentals=0
+)
+
+
+def matrices_shape(boards):
+    return jax.ShapeDtypeStruct((boards, WIDE, WIDE), BF16)
+
+
+def build_own(holding, ranks):
     return pl.pallas_call(
-        build_a_kernel,
-        out_shape=(
-            MATRIX,
-            jax.ShapeDtypeStruct((WIDE, WIDE), BF16),
-            jax.ShapeDtypeStruct((8, 128), F32),
-        ),
+        build_own_kernel,
+        out_shape=(matrices_shape(4), jax.ShapeDtypeStruct((WIDE, WIDE), BF16)),
         in_specs=[VMEM()] * 2,
-        out_specs=[VMEM()] * 3,
+        out_specs=[VMEM()] * 2,
         scratch_shapes=[pltpu.VMEM((WIDE, 128), F32)],
         compiler_params=pltpu.CompilerParams(vmem_limit_bytes=LIMIT),
-        cost_estimate=cost(2),
-        name="build_a",
+        cost_estimate=BUILD_COST,
+        name="build_own",
     )(holding, ranks)
 
 
-def build_b(odd, even, cross, ranks, apart):
+def build_side(place, even, cross, apart):
     return pl.pallas_call(
-        build_b_kernel,
-        out_shape=(MATRIX, MATRIX, MATRIX),
-        in_specs=[SMEM()] + [VMEM()] * 4,
-        out_specs=[VMEM()] * 3,
+        build_side_kernel,
+        out_shape=(matrices_shape(2), matrices_shape(2)),
+        in_specs=[SMEM()] + [VMEM()] * 3,
+        out_specs=[VMEM()] * 2,
         scratch_shapes=[pltpu.VMEM((8, WIDE), F32), pltpu.VMEM((WIDE, 128), F32)],
         compiler_params=pltpu.CompilerParams(vmem_limit_bytes=LIMIT),
-        cost_estimate=cost(6),
-        name="build_b",
-    )(odd, even, cross, ranks, apart)
+        cost_estimate=BUILD_COST,
+        name="build_side",
+    )(place, even, cross, apart)
 
 
 def node_totals(same, values):
@@ -271,17 +280,17 @@
 
 
 def first_kernel(
-    odd_ref,
+    place_ref,
     packed_ref,
     even_ref,
     cross_ref,
     part_ref,
-    edge_ref,
+    even_other_ref,
+    cross_other_ref,
     nodes_ref,
     own_free_ref,
-    own_pot_ref,
-    first_matrix_ref,
-    last_matrix_ref,
+    pots_ref,
+    own_matrix_ref,
     near_ref,
     far_ref,
     window_ref,
@@ -295,17 +304,17 @@
     terms_ref,
     values_ref,
 ):
-    left, right = sides(odd_ref, even_ref, cross_ref, slice(0, EDGE))
-    same_ref[0] = same_node(nodes_ref[...])
-    same_ref[1] = same_node(edge_ref[30:31, 0:128])
+    left, right = sides(place_ref, even_ref, cross_ref, slice(0, EDGE))
+    left_other, right_other = sides(place_ref, even_other_ref, cross_other_ref, slice(0, 15))
+    same_ref[0] = same_node(nodes_ref[0:1, :])
+    same_ref[1] = same_node(part_ref[2 * OWN :, 0:128])
     free_ref[...] = jnp.zeros_like(free_ref)
     free_ref[0:2, :HANDS] = left[27:29]
     free_ref[2:6] = own_free_ref[0:4]
     free_ref[6:8, :HANDS] = right[27:29]
-    pot_ref[0:SIDE] = column_of(left[29:30, 0:128])[:SIDE]
-    pot_ref[SIDE : 2 * SIDE] = column_of(own_pot_ref[0:1, :])[:SIDE]
-    pot_ref[2 * SIDE : 3 * SIDE] = column_of(own_pot_ref[1:2, :])[:SIDE]
-    pot_ref[3 * SIDE : 4 * SIDE] = column_of(right[29:30, 0:128])[:SIDE]
+    pot_ref[0:SIDE] = column_of(left[29:30, 0:128])[SIDE:OWN]
+    pot_ref[SIDE : SIDE + OWN] = column_of(pots_ref[0:1, :])[:OWN]
+    pot_ref[SIDE + OWN :] = column_of(right[29:30, 0:128])[:SIDE]
     window_ref[...] = jnp.zeros_like(window_ref)
     reached_ref[...] = jnp.zeros_like(reached_ref)
     policy_ref[...] = jnp.zeros_like(policy_ref)
@@ -314,14 +323,14 @@
     window_ref[0, low:high, :HANDS] = packed_ref[:OWN]
     window_ref[0, high : high + 15, :HANDS] = right[0:15]
     policy_ref[0, low - 10 : low, :HANDS] = left[15:25]
-    policy_ref[0, low:high, :HANDS] = packed_ref[OWN:]
+    policy_ref[0, low:high, :HANDS] = packed_ref[OWN : 2 * OWN]
     policy_ref[0, high : high + 10, :HANDS] = right[15:25]
-    window_ref[1, low - 10 : low, :HANDS] = edge_ref[0:10]
+    window_ref[1, low - 10 : low, :HANDS] = left_other[0:10]
     window_ref[1, low:high, :HANDS] = part_ref[0:OWN]
-    window_ref[1, high : high + 10, :HANDS] = edge_ref[10:20]
-    reached_ref[low - 5 : low, :HANDS] = edge_ref[20:25]
+    window_ref[1, high : high + 10, :HANDS] = right_other[0:10]
+    reached_ref[low - 5 : low, :HANDS] = left_other[10:15]
     reached_ref[low:high, :HANDS] = part_ref[OWN : 2 * OWN]
-    reached_ref[high : high + 5, :HANDS] = edge_ref[25:30]
+    reached_ref[high : high + 5, :HANDS] = right_other[10:15]
     free = board_rows(free_ref, range(8))
     reached_ref[...] = reached_ref[...] * free
     terms = []
@@ -343,10 +352,8 @@
         values_ref[1, rows, :] = joined(out, 0) * factor * free
         values_ref[0, rows, :] = joined(out, PIECES * BOARD_LEAVES) * factor * free
 
-    board(2, first_matrix_ref[0])
-    board(3, first_matrix_ref[1])
-    board(4, last_matrix_ref[0])
-    board(5, last_matrix_ref[1])
+    for b in range(4):
+        board(b + 2, own_matrix_ref[b])
     board(1, near_ref[0])
     board(6, near_ref[1])
     board(0, far_ref[0])
@@ -363,7 +370,7 @@
     sums_ref[...] = jnp.where(lane == 0, sums[0], jnp.where(lane == 1, sums[1], 0.0))
 
 
-def first(odd, packed, even, cross, part, edge, nodes, free, pot_rows, matrices):
+def first(place, arrays):
     shapes = (
         jax.ShapeDtypeStruct((2, WINDOW, WIDE), F32),
         jax.ShapeDtypeStruct((WINDOW, WIDE), F32),
@@ -373,7 +380,6 @@
         jax.ShapeDtypeStruct((8, WIDE), F32),
         jax.ShapeDtypeStruct((WINDOW, 128), F32),
     )
-    arrays = (packed, even, cross, part, edge, nodes, free, pot_rows) + matrices
     return pl.pallas_call(
         first_kernel,
         out_shape=shapes,
@@ -386,7 +392,7 @@
         ],
         compiler_params=pltpu.CompilerParams(vmem_limit_bytes=LIMIT),
         name="first",
-    )(odd, *arrays)
+    )(place, *arrays)
 
 
 def second_kernel(
@@ -397,8 +403,7 @@
     same_ref,
     free_ref,
     pot_ref,
-    first_matrix_ref,
-    last_matrix_ref,
+    own_matrix_ref,
     near_ref,
     out_values_ref,
     moved_ref,
@@ -429,10 +434,8 @@
         factor = pot_ref[rows, 0:1] * (-1.0 / HANDS)
         values_ref[rows, :] = joined(out, 0) * factor * free_ref[b : b + 1, :]
 
-    board(2, first_matrix_ref[0])
-    board(3, first_matrix_ref[1])
-    board(4, last_matrix_ref[0])
-    board(5, last_matrix_ref[1])
+    for b in range(4):
+        board(b + 2, own_matrix_ref[b])
     board(1, near_ref[0])
     board(6, near_ref[1])
 
@@ -486,43 +489,44 @@
 
 
 def local(chance_reach, regrets_start, pot, parent, hand_cards, board_cards, hand_rank):
-    chance = chance_reach[0]
-    regrets = regrets_start[0]
-    index = lax.axis_index(LEAF)
+    index = lax.axis_index(LEAF).astype(jnp.int32)
     devices = lax.axis_size(LEAF)
     leaf_count = parent.shape[1]
-    odd = lax.rem(index, 2).astype(jnp.int32)[None]
-
-    pot_rows = jnp.pad(pot.reshape(2, SIDE), ((0, 0), (0, 128 - SIDE)))
-    packed, even, cross, ranks, free, holding = pack(
-        odd, board_cards, pot_rows, regrets, chance, hand_rank, hand_cards.T
-    )
-    swap = [(0, 1), (1, 0)]
-    part = lax.ppermute(packed, "player", swap)
-    even = lax.ppermute(even, LEAF, [(i, i ^ 1) for i in range(devices)])
-    cross = lax.ppermute(
-        cross,
-        LEAF,
-        [(i, i + 1) for i in range(1, devices - 1, 2)]
-        + [(i + 1, i) for i in range(1, devices - 1, 2)],
-    )
-    padded = jnp.pad(parent[0], (SIDE, 128), constant_values=-1)
-    nodes = lax.dynamic_slice_in_dim(padded, index * OWN, 128).astype(F32)[None]
-    first_matrix, apart, token = build_a(holding, ranks)
-    edge = lax.ppermute(edges(odd, even, cross, nodes, token), "player", swap)
-    last_matrix, near, far = build_b(odd, even, cross, ranks, apart)
+    place = jnp.stack([index, lax.rem(index, 2)])
+
+    even_pairs = [(i, i ^ 1) for i in range(devices)]
+    cross_pairs = [(i, i + 1) for i in range(1, devices - 1, 2)]
+    cross_pairs = cross_pairs + [(j, i) for i, j in cross_pairs]
+
+    def diagonal(pairs):
+        return [(2 * i + p, 2 * j + 1 - p) for i, j in pairs for p in range(2)]
+
+    packed, even, cross, even_other, cross_other, ranks, free, holding, pots, nodes = pack(
+        place, board_cards, pot[None], regrets_start[0], chance_reach[0], hand_rank,
+        hand_cards.T, parent.reshape(-1, 128),
+    )
+    both = LEAF + ("player",)
+    part = lax.ppermute(packed, "player", [(0, 1), (1, 0)])
+    even = lax.ppermute(even, LEAF, even_pairs)
+    cross = lax.ppermute(cross, LEAF, cross_pairs)
+    even_other = lax.ppermute(even_other, both, diagonal(even_pairs))
+    cross_other = lax.ppermute(cross_other, both, diagonal(cross_pairs))
+
+    own_matrix, apart = build_own(holding, ranks)
+    near, far = build_side(place, even, cross, apart)
 
     def gathered(sums):
         return lax.all_to_all(sums.reshape(devices, 1, 128), LEAF, 0, 0).reshape(128, 128)
 
     count = float(leaf_count * HANDS)
     window, reached, instant, sums, same, all_free, all_pot = first(
-        odd, packed, even, cross, part, edge, nodes, free, pot_rows,
-        (first_matrix, last_matrix, near, far),
+        place,
+        (packed, even, cross, part, even_other, cross_other, nodes, free, pots)
+        + (own_matrix, near, far),
     )
     values, moved, mine, sums = second(
         gathered(sums), window, reached, instant, same, all_free, all_pot,
-        (first_matrix, last_matrix, near), count,
+        (own_matrix, near), count,
     )
     final = tail(gathered(sums), moved, mine, count)
     return (final[None], values[None])

time: 98.4 us -> 92.2 us (0.937)
  local copies, waits for them, and re-layouts: 11 us -> 0.66 us
  starting transfers between devices: 11.7 us -> 18.5 us
  waiting for transfers between devices: 12.6 us -> 8.71 us
  Pallas kernels: 24.4 us -> 26 us
    unnamed x14 -> x2, local copies, waits for them, and re-layouts: 10.3 us -> 0.66 us
    ppermute x4 -> x5, starting transfers between devices: 11.7 us -> 18.5 us  [the longest x1 7.83 us: local(): part = lax.ppermute(packed, 'player', [(0, 1), (1, 0)])]
    ppermute x4 -> x5, waiting for transfers between devices: 12.6 us -> 8.71 us  [the longest x1 8.7 us: local(): cross = lax.ppermute(cross, LEAF, cross_pairs)]
    pallas_call x3 -> x2, Pallas kernels: 11.7 us -> 12.2 us  [the longest x1 6.32 us: build_own(): pl.pallas_call(build_own_kernel, out_shape=(matrices_shape(4), jax.ShapeD...]
  transfers between devices with their start and end apart: 4 -> 5, of which waited for: 1 -> 1; matrix products, arithmetic and copies ran while one was open for 1% -> 0% of each run, Pallas kernels for 12% -> 13%
where the time goes in v3:
time: 92.2 us; the launch traced here: 91.9 us
  blocking collectives  37.3 us (40%)
  Pallas kernels  26 us (28%)
  starting transfers between devices  18.5 us (20%)
  waiting for transfers between devices  8.71 us (9%)
    all_to_all x2, blocking collectives, gathered(): lax.all_to_all(sums.reshape(devices, 1, 128), LEAF, 0, 0).reshape(128, 128)  37.3 us
    ppermute x1, waiting for transfers between devices, local(): cross = lax.ppermute(cross, LEAF, cross_pairs)  8.7 us
    ppermute x1, starting transfers between devices, local(): part = lax.ppermute(packed, 'player', [(0, 1), (1, 0)])  7.83 us
    ppermute x1, starting transfers between devices, local(): cross_other = lax.ppermute(cross_other, both, diagonal(cross_pairs))  7.09 us
    pallas_call x1, Pallas kernels, first(): pl.pallas_call(first_kernel, out_shape=shapes, in_specs=[SMEM()] + [VMEM(...  6.67 us
    pallas_call x1, Pallas kernels, build_own(): pl.pallas_call(build_own_kernel, out_shape=(matrices_shape(4), jax.ShapeD...  6.32 us
    pallas_call x1, Pallas kernels, build_side(): pl.pallas_call(build_side_kernel, out_shape=(matrices_shape(2), matrices_...  5.9 us
    pallas_call x1, Pallas kernels, second(): pl.pallas_call(functools.partial(second_kernel, count=count), out_shape=s...  4.54 us
  transfers between devices with their start and end apart: 5, of which 1 were waited for; matrix products, arithmetic and copies ran while one was open for 0% of the time, Pallas kernels for 13%

profile of v3, /device:TPU:1, one launch (start us, length us, event | category | flops | bytes accessed | tf_op | source)
XLA Modules:
  0.0 91.9 jit_solution(5792496750514395517)
XLA Ops:
  0.6 0.1 pad_add_fusion.place_ref
  0.7 0.0 copy-start
  0.7 0.7 copy-done
  1.4 1.7 %pack.1 = (f32[65,1326]{1,0:T(8,128)S(1)}, f32[30,1326]{1,0:T(8,128)S(1)}, f32[30,1326]{1,0:T(8,128)S(1)}, f32[16,1326]{1,0:T(8,128)S(1)}, f32[16,1326]{1,0:T(8,...) custom-call(s32[2]{0:T(128)S(1)} %pad_add_fusion.place_ref, ...), custom_call_target="tpu_custom_call" | custom-call | tf_op jit(solution)/shard_map/pack/pallas_call | solution.py:140
  3.1 7.8 %collective-permute-start.2 = (f32[65,1326]{1,0:T(8,128)S(1)}, f32[65,1326]{1,0:T(8,128)S(1)}, u32[]{:S(2)}, u32[]{:S(2)}) collective-permute-start(f32[65,1326]{1,0:T(8,128)S(1)} %get-tuple-element.27.packed_ref), channel_id=1, source_target_pairs={{0,1},{1,0},{2,3},{3,2},{4,5},{5,4},{6,7},{7,6},{8,9},{9,8},{10,11... | collective-permute-start | bytes 1034288 | tf_op jit(solution)/shard_map/ppermute | solution.py:509
  10.9 1.0 %collective-permute-start = (f32[30,1326]{1,0:T(8,128)S(1)}, f32[30,1326]{1,0:T(8,128)S(1)}, u32[]{:S(2)}, u32[]{:S(2)}) collective-permute-start(f32[30,1326]{1,0:T(8,128)S(1)} %get-tuple-element.28), channel_id=1, source_target_pairs={{0,2},{2,0},{4,6},{6,4},{8,10},{10,8},{12,14},{14,12},{16,18},{18,... | collective-permute-start | bytes 477368 | tf_op jit(solution)/shard_map/ppermute | solution.py:510
  11.9 2.5 %collective-permute-start.1 = (f32[30,1326]{1,0:T(8,128)S(1)}, f32[30,1326]{1,0:T(8,128)S(1)}, u32[]{:S(2)}, u32[]{:S(2)}) collective-permute-start(f32[30,1326]{1,0:T(8,128)S(1)} %get-tuple-element.29), channel_id=1, source_target_pairs={{2,4},{6,8},{10,12},{14,16},{18,20},{22,24},{26,28},{30,32},{34,36... | collective-permute-start | bytes 477368 | tf_op jit(solution)/shard_map/ppermute | solution.py:511
  14.4 0.1 collective-permute-start.3
  14.5 7.1 %collective-permute-start.4 = (f32[16,1326]{1,0:T(8,128)S(1)}, f32[16,1326]{1,0:T(8,128)S(1)}, u32[]{:S(2)}, u32[]{:S(2)}) collective-permute-start(f32[16,1326]{1,0:T(8,128)S(1)} %get-tuple-element.31), channel_id=1, source_target_pairs={{2,5},{3,4},{6,9},{7,8},{10,13},{11,12},{14,17},{15,16},{18,21},{1... | collective-permute-start | bytes 254600 | tf_op jit(solution)/shard_map/ppermute | solution.py:513
  21.6 6.3 %build_own.1 = (bf16[4,1408,1408]{2,1,0:T(8,128)(2,1)S(1)}, bf16[1408,1408]{1,0:T(8,128)(2,1)S(1)}) custom-call(bf16[128,1408]{1,0:T(8,128)(2,1)S(1)} %get-tuple-element.35.holding_ref, f32[8,1408]{1,0:T(8,128)S(1)} %get-tuple-element.36.rank_ref), custom_call_target="tpu_custom_call" | custom-call | flops 63438848 | bytes 15859712 | tf_op jit(solution)/shard_map/build_own/pallas_call | solution.py:217
  27.9 0.0 collective-permute-done.even_ref
  28.0 8.7 %collective-permute-done.1.cross_ref = f32[30,1326]{1,0:T(8,128)S(1)} collective-permute-done((f32[30,1326]{1,0:T(8,128)S(1)}, f32[30,1326]{1,0:T(8,128)S(1)}, u32[]{:S(2)}, u32[]{:S(2)}) %collective-permute-start.1) | collective-permute-done | bytes 159152 | tf_op jit(solution)/shard_map/ppermute | solution.py:511
  36.7 5.9 %build_side.1 = (bf16[2,1408,1408]{2,1,0:T(8,128)(2,1)S(1)}, bf16[2,1408,1408]{2,1,0:T(8,128)(2,1)S(1)}) custom-call(s32[2]{0:T(128)S(1)} %pad_add_fusion.place_ref, f32[30,1326]{1,0:T(8,128)S(1)} %collective-permute-done.even_ref, f32[30,1326]{1,0:T(8,128)S(1)} %collective-permute-done.1.cross_ref, bf16[1408,1408]{1,0:T(8,128)(2,1)S(1)} %get-tuple-element.38.apart_ref), custom_call_target="tpu_custom_call" | custom-call | flops 63438848 | bytes 15859712 | tf_op jit(solution)/shard_map/build_side/pallas_call | solution.py:230
  42.6 0.0 collective-permute-done.3.even_other_ref
  42.6 0.0 collective-permute-done.4.cross_other_ref
  42.6 0.0 collective-permute-done.2.part_ref
  42.6 6.7 %first.1 = (f32[2,64,1408]{2,1,0:T(8,128)S(1)}, f32[64,1408]{1,0:T(8,128)S(1)}, f32[2,64,1408]{2,1,0:T(8,128)S(1)}, f32[128,128]{1,0:T(8,128)S(1)}, bf16[2,64,19...) custom-call(s32[2]{0:T(128)S(1)} %pad_add_fusion.place_ref, ...), custom_call_target="tpu_custom_call" | custom-call | tf_op jit(solution)/shard_map/first/pallas_call | solution.py:383
  49.3 21.9 %all_to_all.10 = f32[128,1,128]{2,1,0:T(1,128)S(1)} all-to-all(f32[128,1,128]{2,1,0:T(1,128)S(1)} %bitcast.19), channel_id=1, replica_groups=mesh['leaf_0'=4,'leaf_1'=4,'leaf_2'=4,'leaf_3'=2,'player'=2] {'leaf_0','..., dimensions={0} | all-to-all | bytes 131072 | tf_op jit(solution)/shard_map/all_to_all | solution.py:519
  71.2 4.5 %second.1 = (f32[32,1326]{1,0:T(8,128)}, f32[32,1408]{1,0:T(8,128)S(1)}, f32[32,1408]{1,0:T(8,128)S(1)}, f32[128,128]{1,0:T(8,128)S(1)}) custom-call(f32[128,128]{1,0:T(8,128)S(1)} %bitcast.17, f32[2,64,1408]{2,1,0:T(8,128)S(1)} %get-tuple-element.42.window_ref, f32[64,1408]{1,0:T(8,128)S(1)} %get-tuple-element.43.reached_ref, ...), custom_call_target="tpu_custom_call" | custom-call | tf_op jit(solution)/shard_map/second/pallas_call | solution.py:459
  75.7 15.4 %all_to_all.11 = f32[128,1,128]{2,1,0:T(1,128)S(1)} all-to-all(f32[128,1,128]{2,1,0:T(1,128)S(1)} %bitcast.20), channel_id=1, replica_groups=mesh['leaf_0'=4,'leaf_1'=4,'leaf_2'=4,'leaf_3'=2,'player'=2] {'leaf_0','..., dimensions={0} | all-to-all | bytes 131072 | tf_op jit(solution)/shard_map/all_to_all | solution.py:519
  91.1 0.8 tail.1
Async XLA Ops:
  0.7 0.7 copy-start
  3.1 39.5 %collective-permute-start.2 = (f32[65,1326]{1,0:T(8,128)S(1)}, f32[65,1326]{1,0:T(8,128)S(1)}, u32[]{:S(2)}, u32[]{:S(2)}) collective-permute-start(f32[65,1326]{1,0:T(8,128)S(1)} %get-tuple-element.27.packed_ref), channel_id=1, source_target_pairs={{0,1},{1,0},{2,3},{3,2},{4,5},{5,4},{6,7},{7,6},{8,9},{9,8},{10,11... | collective-permute-start | bytes 1034288 | tf_op jit(solution)/shard_map/ppermute | solution.py:509
  10.9 17.0 %collective-permute-start = (f32[30,1326]{1,0:T(8,128)S(1)}, f32[30,1326]{1,0:T(8,128)S(1)}, u32[]{:S(2)}, u32[]{:S(2)}) collective-permute-start(f32[30,1326]{1,0:T(8,128)S(1)} %get-tuple-element.28), channel_id=1, source_target_pairs={{0,2},{2,0},{4,6},{6,4},{8,10},{10,8},{12,14},{14,12},{16,18},{18,... | collective-permute-start | bytes 477368 | tf_op jit(solution)/shard_map/ppermute | solution.py:510
  11.9 24.8 %collective-permute-start.1 = (f32[30,1326]{1,0:T(8,128)S(1)}, f32[30,1326]{1,0:T(8,128)S(1)}, u32[]{:S(2)}, u32[]{:S(2)}) collective-permute-start(f32[30,1326]{1,0:T(8,128)S(1)} %get-tuple-element.29), channel_id=1, source_target_pairs={{2,4},{6,8},{10,12},{14,16},{18,20},{22,24},{26,28},{30,32},{34,36... | collective-permute-start | bytes 477368 | tf_op jit(solution)/shard_map/ppermute | solution.py:511
  14.4 28.2 %collective-permute-start.3 = (f32[16,1326]{1,0:T(8,128)S(1)}, f32[16,1326]{1,0:T(8,128)S(1)}, u32[]{:S(2)}, u32[]{:S(2)}) collective-permute-start(f32[16,1326]{1,0:T(8,128)S(1)} %get-tuple-element.30), channel_id=1, source_target_pairs={{0,3},{1,2},{2,1},{3,0},{4,7},{5,6},{6,5},{7,4},{8,11},{9,10},{10,... | collective-permute-start | bytes 254600 | tf_op jit(solution)/shard_map/ppermute | solution.py:512
  14.5 28.1 %collective-permute-start.4 = (f32[16,1326]{1,0:T(8,128)S(1)}, f32[16,1326]{1,0:T(8,128)S(1)}, u32[]{:S(2)}, u32[]{:S(2)}) collective-permute-start(f32[16,1326]{1,0:T(8,128)S(1)} %get-tuple-element.31), channel_id=1, source_target_pairs={{2,5},{3,4},{6,9},{7,8},{10,13},{11,12},{14,17},{15,16},{18,21},{1... | collective-permute-start | bytes 254600 | tf_op jit(solution)/shard_map/ppermute | solution.py:513

commit v4 on v3

--- a/solution.py
+++ b/solution.py
@@ -18,7 +18,7 @@
 SIDE = 16
 WINDOW = OWN + 2 * SIDE
 BOARD_LEAVES = 8
-EDGE = 30
+EDGE = 66
 LIMIT = 10 << 20
 SMALL = 6 << 20
 PIECES = 2
@@ -27,9 +27,38 @@
 VMEM = functools.partial(pl.BlockSpec, memory_space=pltpu.VMEM)
 
 
+def edge_rows(rows_ref, edge_ref, last):
+    at = OWN - 10 if last else 0
+    edge_ref[0:10] = rows_ref[at : at + 10]
+    at = 2 * OWN - 5 if last else OWN
+    edge_ref[10:15] = rows_ref[at : at + 5]
+    edge_ref[15:16] = jnp.zeros((1, HANDS), F32)
+
+
+def forward_kernel(place_ref, part_ref, after_ref, edge_ref):
+    @pl.when(place_ref[1] == 1)
+    def _():
+        edge_rows(part_ref, edge_ref, False)
+
+    @pl.when(place_ref[1] != 1)
+    def _():
+        edge_rows(part_ref, edge_ref, True)
+
+
+def forward(place, part, after):
+    return pl.pallas_call(
+        forward_kernel,
+        out_shape=jax.ShapeDtypeStruct((16, HANDS), F32),
+        in_specs=[SMEM(), VMEM(), VMEM()],
+        out_specs=VMEM(),
+        compiler_params=pltpu.CompilerParams(vmem_limit_bytes=SMALL),
+        name="forward",
+    )(place, part, after)
+
+
 def pack_kernel(
     place_ref, boards_hbm, pot_ref, regrets_hbm, chance_hbm, rank_hbm, cards_hbm, parent_hbm,
-    part_ref, even_ref, cross_ref, even_other_ref, cross_other_ref,
+    part_ref, even_ref, cross_ref, cross_other_ref,
     wide_rank_ref, free_ref, holding_ref, pots_ref, nodes_ref,
     board_cards_ref, rank_ref, cards_ref, parent_ref, sems,
 ):
@@ -85,31 +114,30 @@
     for copy in copies[4:]:
         copy.wait()
 
-    def ends(ref, other_ref, last):
+    def ends(ref, last):
         at = OWN - 15 if last else 0
         ref[0:15] = regrets_ref[at : at + 15]
         at = OWN - 10 if last else 0
         ref[15:25] = chance_ref[at : at + 10]
-        other_ref[0:10] = regrets_ref[at : at + 10]
-        at = OWN - 5 if last else 0
-        other_ref[10:15] = chance_ref[at : at + 5]
-        other_ref[15:16] = jnp.zeros((1, HANDS), F32)
         at = 2 if last else 0
         ref[25:27] = ranks[at : at + 2]
         ref[27:28] = rows[at]
         ref[28:29] = rows[at + 1]
         ref[29:30] = jnp.zeros((1, HANDS), F32)
         ref[29:30, 0:128] = pots_ref[0:1, :]
+        ref[30:] = jnp.zeros((EDGE - 30, HANDS), F32)
 
     @pl.when(place_ref[1] == 1)
     def _():
-        ends(even_ref, even_other_ref, False)
-        ends(cross_ref, cross_other_ref, True)
+        ends(even_ref, False)
+        ends(cross_ref, True)
+        edge_rows(part_ref, cross_other_ref, True)
 
     @pl.when(place_ref[1] != 1)
     def _():
-        ends(even_ref, even_other_ref, True)
-        ends(cross_ref, cross_other_ref, False)
+        ends(even_ref, True)
+        ends(cross_ref, False)
+        edge_rows(part_ref, cross_other_ref, False)
 
     part_ref[2 * OWN :] = jnp.zeros((1, HANDS), F32)
     part_ref[2 * OWN :, 0:128] = held
@@ -128,7 +156,6 @@
         jax.ShapeDtypeStruct((2 * OWN + 1, HANDS), F32),
         jax.ShapeDtypeStruct((EDGE, HANDS), F32),
         jax.ShapeDtypeStruct((EDGE, HANDS), F32),
-        jax.ShapeDtypeStruct((16, HANDS), F32),
         jax.ShapeDtypeStruct((16, HANDS), F32),
         jax.ShapeDtypeStruct((8, WIDE), F32),
         jax.ShapeDtypeStruct((8, WIDE), F32),
@@ -194,8 +221,9 @@
 
 
 def build_side_kernel(
-    place_ref, even_ref, cross_ref, apart_ref, near_ref, far_ref, rank_ref, column_ref
+    place_ref, even_ref, cross_ref, apart_ref, near_ref, far_ref, token_ref, rank_ref, column_ref
 ):
+    token_ref[...] = jnp.zeros_like(token_ref)
     left, right = sides(place_ref, even_ref, cross_ref, slice(25, 27))
     rank_ref[...] = jnp.zeros_like(rank_ref)
     rank_ref[0:2, :HANDS] = left
@@ -229,9 +257,13 @@
 def build_side(place, even, cross, apart):
     return pl.pallas_call(
         build_side_kernel,
-        out_shape=(matrices_shape(2), matrices_shape(2)),
+        out_shape=(
+            matrices_shape(2),
+            matrices_shape(2),
+            jax.ShapeDtypeStruct((8, 128), F32),
+        ),
         in_specs=[SMEM()] + [VMEM()] * 3,
-        out_specs=[VMEM()] * 2,
+        out_specs=[VMEM()] * 3,
         scratch_shapes=[pltpu.VMEM((8, WIDE), F32), pltpu.VMEM((WIDE, 128), F32)],
         compiler_params=pltpu.CompilerParams(vmem_limit_bytes=LIMIT),
         cost_estimate=BUILD_COST,
@@ -304,7 +336,7 @@
     terms_ref,
     values_ref,
 ):
-    left, right = sides(place_ref, even_ref, cross_ref, slice(0, EDGE))
+    left, right = sides(place_ref, even_ref, cross_ref, slice(0, 30))
     left_other, right_other = sides(place_ref, even_other_ref, cross_other_ref, slice(0, 15))
     same_ref[0] = same_node(nodes_ref[0:1, :])
     same_ref[1] = same_node(part_ref[2 * OWN :, 0:128])
@@ -498,22 +530,21 @@
     cross_pairs = [(i, i + 1) for i in range(1, devices - 1, 2)]
     cross_pairs = cross_pairs + [(j, i) for i, j in cross_pairs]
 
-    def diagonal(pairs):
-        return [(2 * i + p, 2 * j + 1 - p) for i, j in pairs for p in range(2)]
-
-    packed, even, cross, even_other, cross_other, ranks, free, holding, pots, nodes = pack(
+    diagonal = [(2 * i + p, 2 * j + 1 - p) for i, j in cross_pairs for p in range(2)]
+
+    packed, even, cross, cross_other, ranks, free, holding, pots, nodes = pack(
         place, board_cards, pot[None], regrets_start[0], chance_reach[0], hand_rank,
         hand_cards.T, parent.reshape(-1, 128),
     )
-    both = LEAF + ("player",)
+    cross = lax.ppermute(cross, LEAF, cross_pairs)
+    even = lax.ppermute(even, LEAF, even_pairs)
     part = lax.ppermute(packed, "player", [(0, 1), (1, 0)])
-    even = lax.ppermute(even, LEAF, even_pairs)
-    cross = lax.ppermute(cross, LEAF, cross_pairs)
-    even_other = lax.ppermute(even_other, both, diagonal(even_pairs))
-    cross_other = lax.ppermute(cross_other, both, diagonal(cross_pairs))
+    cross_other = lax.ppermute(cross_other, LEAF + ("player",), diagonal)
 
     own_matrix, apart = build_own(holding, ranks)
-    near, far = build_side(place, even, cross, apart)
+    near, far, built = build_side(place, even, cross, apart)
+
+    even_other = lax.ppermute(forward(place, part, built), LEAF, even_pairs)
 
     def gathered(sums):
         return lax.all_to_all(sums.reshape(devices, 1, 128), LEAF, 0, 0).reshape(128, 128)

time: 92.2 us -> 92.7 us (level)
  blocking collectives: 37.3 us -> 48.8 us
  waiting for transfers between devices: 8.71 us -> 2.24 us
  starting transfers between devices: 18.5 us -> 13.5 us
    all_to_all x2, blocking collectives: 37.3 us -> 48.8 us  [gathered(): lax.all_to_all(sums.reshape(devices, 1, 128), LEAF, 0, 0).reshape(128, 128)]
    ppermute x1, waiting for transfers between devices: 8.7 us -> 0.01 us  [local(): cross = lax.ppermute(cross, LEAF, cross_pairs)]
    ppermute x2, starting transfers between devices: 7.18 us -> 2.38 us  [the longest x1 2.29 us: local(): cross_other = lax.ppermute(cross_other, LEAF + ('player',), diagonal)]
    ppermute x1, starting transfers between devices: 0.95 us -> 3.32 us  [local(): even = lax.ppermute(even, LEAF, even_pairs)]
    ppermute x1, starting transfers between devices: 7.83 us -> 5.9 us  [local(): part = lax.ppermute(packed, 'player', [(0, 1), (1, 0)])]
    ppermute x2, waiting for transfers between devices: 0.01 us -> 1.28 us  [the longest x1 0.74 us: local(): even_other = lax.ppermute(forward(place, part, built), LEAF, even_pairs)]
    ppermute x1, waiting for transfers between devices: 0.01 us -> 0.96 us  [local(): part = lax.ppermute(packed, 'player', [(0, 1), (1, 0)])]
  transfers between devices with their start and end apart: 5 -> 5, of which waited for: 1 -> 3; matrix products, arithmetic and copies ran while one was open for 0% -> 0% of each run, Pallas kernels for 13% -> 14%
where the time goes in v4:
time: 92.7 us; the launch traced here: 92.5 us
  blocking collectives  48.8 us (53%)
  Pallas kernels  26.5 us (29%)
  starting transfers between devices  13.5 us (15%)
  waiting for transfers between devices  2.24 us (2%)
    all_to_all x2, blocking collectives, gathered(): lax.all_to_all(sums.reshape(devices, 1, 128), LEAF, 0, 0).reshape(128, 128)  48.8 us
    pallas_call x1, Pallas kernels, first(): pl.pallas_call(first_kernel, out_shape=shapes, in_specs=[SMEM()] + [VMEM(...  6.66 us
    pallas_call x1, Pallas kernels, build_own(): pl.pallas_call(build_own_kernel, out_shape=(matrices_shape(4), jax.ShapeD...  6.3 us
    ppermute x1, starting transfers between devices, local(): part = lax.ppermute(packed, 'player', [(0, 1), (1, 0)])  5.9 us
    pallas_call x1, Pallas kernels, build_side(): pl.pallas_call(build_side_kernel, out_shape=(matrices_shape(2), matrices_...  5.9 us
    pallas_call x1, Pallas kernels, second(): pl.pallas_call(functools.partial(second_kernel, count=count), out_shape=s...  4.55 us
    ppermute x1, starting transfers between devices, local(): even = lax.ppermute(even, LEAF, even_pairs)  3.32 us
    ppermute x1, starting transfers between devices, local(): cross_other = lax.ppermute(cross_other, LEAF + ('player',), diagonal)  2.29 us
  transfers between devices with their start and end apart: 5, of which 3 were waited for; matrix products, arithmetic and copies ran while one was open for 0% of the time, Pallas kernels for 14%

profile of v4, /device:TPU:1, one launch (start us, length us, event | category | flops | bytes accessed | tf_op | source)
XLA Modules:
  0.0 92.5 jit_solution(2821693027046872252)
XLA Ops:
  0.6 0.1 pad_add_fusion.place_ref
  0.7 0.0 copy-start
  0.7 0.7 copy-done
  1.4 1.7 %pack.1 = (f32[65,1326]{1,0:T(8,128)S(1)}, f32[66,1326]{1,0:T(8,128)S(1)}, f32[66,1326]{1,0:T(8,128)S(1)}, f32[16,1326]{1,0:T(8,128)S(1)}, f32[8,1408]{1,0:T(8,1...) custom-call(s32[2]{0:T(128)S(1)} %pad_add_fusion.place_ref, ...), custom_call_target="tpu_custom_call" | custom-call | tf_op jit(solution)/shard_map/pack/pallas_call | solution.py:167
  3.1 3.3 %collective-permute-start = (f32[66,1326]{1,0:T(8,128)S(1)}, f32[66,1326]{1,0:T(8,128)S(1)}, u32[]{:S(2)}, u32[]{:S(2)}) collective-permute-start(f32[66,1326]{1,0:T(8,128)S(1)} %get-tuple-element.28), channel_id=1, source_target_pairs={{0,2},{2,0},{4,6},{6,4},{8,10},{10,8},{12,14},{14,12},{16,18},{18,... | collective-permute-start | bytes 1050200 | tf_op jit(solution)/shard_map/ppermute | solution.py:540
  6.4 1.9 %collective-permute-start.1 = (f32[66,1326]{1,0:T(8,128)S(1)}, f32[66,1326]{1,0:T(8,128)S(1)}, u32[]{:S(2)}, u32[]{:S(2)}) collective-permute-start(f32[66,1326]{1,0:T(8,128)S(1)} %get-tuple-element.29), channel_id=1, source_target_pairs={{2,4},{6,8},{10,12},{14,16},{18,20},{22,24},{26,28},{30,32},{34,36... | collective-permute-start | bytes 1050200 | tf_op jit(solution)/shard_map/ppermute | solution.py:539
  8.4 5.9 %collective-permute-start.2 = (f32[65,1326]{1,0:T(8,128)S(1)}, f32[65,1326]{1,0:T(8,128)S(1)}, u32[]{:S(2)}, u32[]{:S(2)}) collective-permute-start(f32[65,1326]{1,0:T(8,128)S(1)} %get-tuple-element.27.packed_ref), channel_id=1, source_target_pairs={{0,1},{1,0},{2,3},{3,2},{4,5},{5,4},{6,7},{7,6},{8,9},{9,8},{10,11... | collective-permute-start | bytes 1034288 | tf_op jit(solution)/shard_map/ppermute | solution.py:541
  14.3 2.3 %collective-permute-start.4 = (f32[16,1326]{1,0:T(8,128)S(1)}, f32[16,1326]{1,0:T(8,128)S(1)}, u32[]{:S(2)}, u32[]{:S(2)}) collective-permute-start(f32[16,1326]{1,0:T(8,128)S(1)} %get-tuple-element.34), channel_id=1, source_target_pairs={{2,5},{3,4},{6,9},{7,8},{10,13},{11,12},{14,17},{15,16},{18,21},{1... | collective-permute-start | bytes 254600 | tf_op jit(solution)/shard_map/ppermute | solution.py:542
  16.6 6.3 %build_own.1 = (bf16[4,1408,1408]{2,1,0:T(8,128)(2,1)S(1)}, bf16[1408,1408]{1,0:T(8,128)(2,1)S(1)}) custom-call(bf16[128,1408]{1,0:T(8,128)(2,1)S(1)} %get-tuple-element.30.holding_ref, f32[8,1408]{1,0:T(8,128)S(1)} %get-tuple-element.31.rank_ref), custom_call_target="tpu_custom_call" | custom-call | flops 63438848 | bytes 15859712 | tf_op jit(solution)/shard_map/build_own/pallas_call | solution.py:245
  22.9 0.0 collective-permute-done.even_ref
  22.9 0.0 collective-permute-done.1.cross_ref
  22.9 5.9 %build_side.1 = (bf16[2,1408,1408]{2,1,0:T(8,128)(2,1)S(1)}, bf16[2,1408,1408]{2,1,0:T(8,128)(2,1)S(1)}, f32[8,128]{1,0:T(8,128)S(1)}) custom-call(s32[2]{0:T(128)S(1)} %pad_add_fusion.place_ref, f32[66,1326]{1,0:T(8,128)S(1)} %collective-permute-done.even_ref, f32[66,1326]{1,0:T(8,128)S(1)} %collective-permute-done.1.cross_ref, ...), custom_call_target="tpu_custom_call" | custom-call | flops 63438848 | bytes 15859712 | tf_op jit(solution)/shard_map/build_side/pallas_call | solution.py:258
  28.8 1.0 %collective-permute-done.2.part_ref = f32[65,1326]{1,0:T(8,128)S(1)} collective-permute-done((f32[65,1326]{1,0:T(8,128)S(1)}, f32[65,1326]{1,0:T(8,128)S(1)}, u32[]{:S(2)}, u32[]{:S(2)}) %collective-permute-start.2) | collective-permute-done | bytes 344792 | tf_op jit(solution)/shard_map/ppermute | solution.py:541
  29.7 0.6 forward.1
  30.3 0.1 collective-permute-start.3
  30.4 0.5 collective-permute-done.4.cross_other_ref
  31.0 0.7 collective-permute-done.3.even_other_ref
  31.7 6.7 %first.1 = (f32[2,64,1408]{2,1,0:T(8,128)S(1)}, f32[64,1408]{1,0:T(8,128)S(1)}, f32[2,64,1408]{2,1,0:T(8,128)S(1)}, f32[128,128]{1,0:T(8,128)S(1)}, bf16[2,64,19...) custom-call(s32[2]{0:T(128)S(1)} %pad_add_fusion.place_ref, ...), custom_call_target="tpu_custom_call" | custom-call | tf_op jit(solution)/shard_map/first/pallas_call | solution.py:415
  38.4 33.3 %all_to_all.10 = f32[128,1,128]{2,1,0:T(1,128)S(1)} all-to-all(f32[128,1,128]{2,1,0:T(1,128)S(1)} %bitcast.19), channel_id=1, replica_groups=mesh['leaf_0'=4,'leaf_1'=4,'leaf_2'=4,'leaf_3'=2,'player'=2] {'leaf_0','..., dimensions={0} | all-to-all | bytes 131072 | tf_op jit(solution)/shard_map/all_to_all | solution.py:550
  71.7 4.5 %second.1 = (f32[32,1326]{1,0:T(8,128)}, f32[32,1408]{1,0:T(8,128)S(1)}, f32[32,1408]{1,0:T(8,128)S(1)}, f32[128,128]{1,0:T(8,128)S(1)}) custom-call(f32[128,128]{1,0:T(8,128)S(1)} %bitcast.17, f32[2,64,1408]{2,1,0:T(8,128)S(1)} %get-tuple-element.42.window_ref, f32[64,1408]{1,0:T(8,128)S(1)} %get-tuple-element.43.reached_ref, ...), custom_call_target="tpu_custom_call" | custom-call | tf_op jit(solution)/shard_map/second/pallas_call | solution.py:491
  76.3 15.4 %all_to_all.11 = f32[128,1,128]{2,1,0:T(1,128)S(1)} all-to-all(f32[128,1,128]{2,1,0:T(1,128)S(1)} %bitcast.20), channel_id=1, replica_groups=mesh['leaf_0'=4,'leaf_1'=4,'leaf_2'=4,'leaf_3'=2,'player'=2] {'leaf_0','..., dimensions={0} | all-to-all | bytes 131072 | tf_op jit(solution)/shard_map/all_to_all | solution.py:550
  91.7 0.8 tail.1
Async XLA Ops:
  0.7 0.7 copy-start
  3.1 19.7 %collective-permute-start = (f32[66,1326]{1,0:T(8,128)S(1)}, f32[66,1326]{1,0:T(8,128)S(1)}, u32[]{:S(2)}, u32[]{:S(2)}) collective-permute-start(f32[66,1326]{1,0:T(8,128)S(1)} %get-tuple-element.28), channel_id=1, source_target_pairs={{0,2},{2,0},{4,6},{6,4},{8,10},{10,8},{12,14},{14,12},{16,18},{18,... | collective-permute-start | bytes 1050200 | tf_op jit(solution)/shard_map/ppermute | solution.py:540
  6.4 16.4 %collective-permute-start.1 = (f32[66,1326]{1,0:T(8,128)S(1)}, f32[66,1326]{1,0:T(8,128)S(1)}, u32[]{:S(2)}, u32[]{:S(2)}) collective-permute-start(f32[66,1326]{1,0:T(8,128)S(1)} %get-tuple-element.29), channel_id=1, source_target_pairs={{2,4},{6,8},{10,12},{14,16},{18,20},{22,24},{26,28},{30,32},{34,36... | collective-permute-start | bytes 1050200 | tf_op jit(solution)/shard_map/ppermute | solution.py:539
  8.4 21.4 %collective-permute-start.2 = (f32[65,1326]{1,0:T(8,128)S(1)}, f32[65,1326]{1,0:T(8,128)S(1)}, u32[]{:S(2)}, u32[]{:S(2)}) collective-permute-start(f32[65,1326]{1,0:T(8,128)S(1)} %get-tuple-element.27.packed_ref), channel_id=1, source_target_pairs={{0,1},{1,0},{2,3},{3,2},{4,5},{5,4},{6,7},{7,6},{8,9},{9,8},{10,11... | collective-permute-start | bytes 1034288 | tf_op jit(solution)/shard_map/ppermute | solution.py:541
  14.3 16.7 %collective-permute-start.4 = (f32[16,1326]{1,0:T(8,128)S(1)}, f32[16,1326]{1,0:T(8,128)S(1)}, u32[]{:S(2)}, u32[]{:S(2)}) collective-permute-start(f32[16,1326]{1,0:T(8,128)S(1)} %get-tuple-element.34), channel_id=1, source_target_pairs={{2,5},{3,4},{6,9},{7,8},{10,13},{11,12},{14,17},{15,16},{18,21},{1... | collective-permute-start | bytes 254600 | tf_op jit(solution)/shard_map/ppermute | solution.py:542
  30.3 1.4 %collective-permute-start.3 = (f32[16,1326]{1,0:T(8,128)S(1)}, f32[16,1326]{1,0:T(8,128)S(1)}, u32[]{:S(2)}, u32[]{:S(2)}) collective-permute-start(f32[16,1326]{1,0:T(8,128)S(1)} %forward.1), channel_id=1, source_target_pairs={{0,2},{2,0},{4,6},{6,4},{8,10},{10,8},{12,14},{14,12},{16,18},{18,... | collective-permute-start | bytes 254600 | tf_op jit(solution)/shard_map/ppermute | solution.py:547

commit v5 on v4

--- a/solution.py
+++ b/solution.py
@@ -18,7 +18,7 @@
 SIDE = 16
 WINDOW = OWN + 2 * SIDE
 BOARD_LEAVES = 8
-EDGE = 66
+EDGE = 34
 LIMIT = 10 << 20
 SMALL = 6 << 20
 PIECES = 2
@@ -27,48 +27,47 @@
 VMEM = functools.partial(pl.BlockSpec, memory_space=pltpu.VMEM)
 
 
-def edge_rows(rows_ref, edge_ref, last):
+def edge_rows(regrets_ref, chance_ref, edge_ref, last):
     at = OWN - 10 if last else 0
-    edge_ref[0:10] = rows_ref[at : at + 10]
-    at = 2 * OWN - 5 if last else OWN
-    edge_ref[10:15] = rows_ref[at : at + 5]
+    edge_ref[0:10] = regrets_ref[at : at + 10]
+    at = OWN - 5 if last else 0
+    edge_ref[10:15] = chance_ref[at : at + 5]
     edge_ref[15:16] = jnp.zeros((1, HANDS), F32)
 
 
-def forward_kernel(place_ref, part_ref, after_ref, edge_ref):
+def forward_kernel(place_ref, regrets_ref, chance_ref, after_ref, edge_ref):
     @pl.when(place_ref[1] == 1)
     def _():
-        edge_rows(part_ref, edge_ref, False)
+        edge_rows(regrets_ref, chance_ref, edge_ref, False)
 
     @pl.when(place_ref[1] != 1)
     def _():
-        edge_rows(part_ref, edge_ref, True)
-
-
-def forward(place, part, after):
+        edge_rows(regrets_ref, chance_ref, edge_ref, True)
+
+
+def forward(place, regrets, chance, after):
     return pl.pallas_call(
         forward_kernel,
         out_shape=jax.ShapeDtypeStruct((16, HANDS), F32),
-        in_specs=[SMEM(), VMEM(), VMEM()],
+        in_specs=[SMEM()] + [VMEM()] * 3,
         out_specs=VMEM(),
         compiler_params=pltpu.CompilerParams(vmem_limit_bytes=SMALL),
         name="forward",
-    )(place, part, after)
+    )(place, regrets, chance, after)
 
 
 def pack_kernel(
     place_ref, boards_hbm, pot_ref, regrets_hbm, chance_hbm, rank_hbm, cards_hbm, parent_hbm,
-    part_ref, even_ref, cross_ref, cross_other_ref,
+    regrets_ref, chance_ref, even_ref, cross_ref, cross_other_ref,
     wide_rank_ref, free_ref, holding_ref, pots_ref, nodes_ref,
     board_cards_ref, rank_ref, cards_ref, parent_ref, sems,
 ):
-    regrets_ref, chance_ref = part_ref.at[:OWN], part_ref.at[OWN : 2 * OWN]
     moves = [
         (boards_hbm, board_cards_ref),
         (rank_hbm, rank_ref),
         (cards_hbm, cards_ref),
         (parent_hbm, parent_ref),
-        (regrets_hbm, regrets_ref),
+        (regrets_hbm, regrets_ref.at[:OWN]),
         (chance_hbm, chance_ref),
     ]
     copies = [
@@ -131,16 +130,16 @@
     def _():
         ends(even_ref, False)
         ends(cross_ref, True)
-        edge_rows(part_ref, cross_other_ref, True)
+        edge_rows(regrets_ref, chance_ref, cross_other_ref, True)
 
     @pl.when(place_ref[1] != 1)
     def _():
         ends(even_ref, True)
         ends(cross_ref, False)
-        edge_rows(part_ref, cross_other_ref, False)
-
-    part_ref[2 * OWN :] = jnp.zeros((1, HANDS), F32)
-    part_ref[2 * OWN :, 0:128] = held
+        edge_rows(regrets_ref, chance_ref, cross_other_ref, False)
+
+    regrets_ref[OWN:] = jnp.zeros((1, HANDS), F32)
+    regrets_ref[OWN:, 0:128] = held
 
 
 SMEM = functools.partial(pl.BlockSpec, memory_space=pltpu.SMEM)
@@ -153,7 +152,8 @@
 
 def pack(place, board_cards, pot_row, regrets, chance, hand_rank, cards, parent):
     shapes = (
-        jax.ShapeDtypeStruct((2 * OWN + 1, HANDS), F32),
+        jax.ShapeDtypeStruct((OWN + 1, HANDS), F32),
+        jax.ShapeDtypeStruct((OWN, HANDS), F32),
         jax.ShapeDtypeStruct((EDGE, HANDS), F32),
         jax.ShapeDtypeStruct((EDGE, HANDS), F32),
         jax.ShapeDtypeStruct((16, HANDS), F32),
@@ -313,10 +313,12 @@
 
 def first_kernel(
     place_ref,
-    packed_ref,
+    regrets_ref,
+    chance_ref,
     even_ref,
     cross_ref,
-    part_ref,
+    regrets_other_ref,
+    chance_other_ref,
     even_other_ref,
     cross_other_ref,
     nodes_ref,
@@ -339,7 +341,7 @@
     left, right = sides(place_ref, even_ref, cross_ref, slice(0, 30))
     left_other, right_other = sides(place_ref, even_other_ref, cross_other_ref, slice(0, 15))
     same_ref[0] = same_node(nodes_ref[0:1, :])
-    same_ref[1] = same_node(part_ref[2 * OWN :, 0:128])
+    same_ref[1] = same_node(regrets_other_ref[OWN:, 0:128])
     free_ref[...] = jnp.zeros_like(free_ref)
     free_ref[0:2, :HANDS] = left[27:29]
     free_ref[2:6] = own_free_ref[0:4]
@@ -352,16 +354,16 @@
     policy_ref[...] = jnp.zeros_like(policy_ref)
     low, high = SIDE, SIDE + OWN
     window_ref[0, low - 15 : low, :HANDS] = left[0:15]
-    window_ref[0, low:high, :HANDS] = packed_ref[:OWN]
+    window_ref[0, low:high, :HANDS] = regrets_ref[:OWN]
     window_ref[0, high : high + 15, :HANDS] = right[0:15]
     policy_ref[0, low - 10 : low, :HANDS] = left[15:25]
-    policy_ref[0, low:high, :HANDS] = packed_ref[OWN : 2 * OWN]
+    policy_ref[0, low:high, :HANDS] = chance_ref[...]
     policy_ref[0, high : high + 10, :HANDS] = right[15:25]
     window_ref[1, low - 10 : low, :HANDS] = left_other[0:10]
-    window_ref[1, low:high, :HANDS] = part_ref[0:OWN]
+    window_ref[1, low:high, :HANDS] = regrets_other_ref[:OWN]
     window_ref[1, high : high + 10, :HANDS] = right_other[0:10]
     reached_ref[low - 5 : low, :HANDS] = left_other[10:15]
-    reached_ref[low:high, :HANDS] = part_ref[OWN : 2 * OWN]
+    reached_ref[low:high, :HANDS] = chance_other_ref[...]
     reached_ref[high : high + 5, :HANDS] = right_other[10:15]
     free = board_rows(free_ref, range(8))
     reached_ref[...] = reached_ref[...] * free
@@ -532,19 +534,20 @@
 
     diagonal = [(2 * i + p, 2 * j + 1 - p) for i, j in cross_pairs for p in range(2)]
 
-    packed, even, cross, cross_other, ranks, free, holding, pots, nodes = pack(
+    regrets, chance, even, cross, cross_other, ranks, free, holding, pots, nodes = pack(
         place, board_cards, pot[None], regrets_start[0], chance_reach[0], hand_rank,
         hand_cards.T, parent.reshape(-1, 128),
     )
     cross = lax.ppermute(cross, LEAF, cross_pairs)
     even = lax.ppermute(even, LEAF, even_pairs)
-    part = lax.ppermute(packed, "player", [(0, 1), (1, 0)])
+    regrets_other = lax.ppermute(regrets, "player", [(0, 1), (1, 0)])
+    chance_other = lax.ppermute(chance, "player", [(0, 1), (1, 0)])
     cross_other = lax.ppermute(cross_other, LEAF + ("player",), diagonal)
 
     own_matrix, apart = build_own(holding, ranks)
     near, far, built = build_side(place, even, cross, apart)
 
-    even_other = lax.ppermute(forward(place, part, built), LEAF, even_pairs)
+    even_other = lax.ppermute(forward(place, regrets_other, chance_other, built), LEAF, even_pairs)
 
     def gathered(sums):
         return lax.all_to_all(sums.reshape(devices, 1, 128), LEAF, 0, 0).reshape(128, 128)
@@ -552,8 +555,8 @@
     count = float(leaf_count * HANDS)
     window, reached, instant, sums, same, all_free, all_pot = first(
         place,
-        (packed, even, cross, part, even_other, cross_other, nodes, free, pots)
-        + (own_matrix, near, far),
+        (regrets, chance, even, cross, regrets_other, chance_other, even_other, cross_other)
+        + (nodes, free, pots, own_matrix, near, far),
     )
     values, moved, mine, sums = second(
         gathered(sums), window, reached, instant, same, all_free, all_pot,

time: 92.7 us -> 87.7 us (0.946)
  blocking collectives: 48.8 us -> 39.3 us
  starting transfers between devices: 13.5 us -> 19 us
  waiting for transfers between devices: 2.24 us -> 1.29 us
    all_to_all x2, blocking collectives: 48.8 us -> 39.3 us  [gathered(): lax.all_to_all(sums.reshape(devices, 1, 128), LEAF, 0, 0).reshape(128, 128)]
    ppermute x1, starting transfers between devices: 2.29 us -> 7.64 us  [local(): cross_other = lax.ppermute(cross_other, LEAF + ('player',), diagonal)]
    ppermute x2 -> x3, waiting for transfers between devices: 1.7 us -> 0.47 us  [the longest x1 0.47 us: local(): lax.ppermute(forward(place, regrets_other, chance_other, built), LEAF, ev...]
    ppermute x2 -> x3, starting transfers between devices: 5.99 us -> 6.09 us  [the longest x1 5.9 us: local(): regrets_other = lax.ppermute(regrets, 'player', [(0, 1), (1, 0)])]
  transfers between devices with their start and end apart: 5 -> 6, of which waited for: 3 -> 2; matrix products, arithmetic and copies ran while one was open for 0% -> 0% of each run, Pallas kernels for 14% -> 15%
where the time goes in v5:
time: 87.7 us; the launch traced here: 87.5 us
  blocking collectives  39.3 us (45%)
  Pallas kernels  26.5 us (30%)
  starting transfers between devices  19 us (22%)
  waiting for transfers between devices  1.29 us (1%)
    all_to_all x2, blocking collectives, gathered(): lax.all_to_all(sums.reshape(devices, 1, 128), LEAF, 0, 0).reshape(128, 128)  39.3 us
    ppermute x1, starting transfers between devices, local(): cross_other = lax.ppermute(cross_other, LEAF + ('player',), diagonal)  7.64 us
    pallas_call x1, Pallas kernels, first(): pl.pallas_call(first_kernel, out_shape=shapes, in_specs=[SMEM()] + [VMEM(...  6.65 us
    pallas_call x1, Pallas kernels, build_own(): pl.pallas_call(build_own_kernel, out_shape=(matrices_shape(4), jax.ShapeD...  6.29 us
    ppermute x1, starting transfers between devices, local(): regrets_other = lax.ppermute(regrets, 'player', [(0, 1), (1, 0)])  5.9 us
    pallas_call x1, Pallas kernels, build_side(): pl.pallas_call(build_side_kernel, out_shape=(matrices_shape(2), matrices_...  5.9 us
    pallas_call x1, Pallas kernels, second(): pl.pallas_call(functools.partial(second_kernel, count=count), out_shape=s...  4.55 us
    ppermute x1, starting transfers between devices, local(): even = lax.ppermute(even, LEAF, even_pairs)  3.32 us
  transfers between devices with their start and end apart: 6, of which 2 were waited for; matrix products, arithmetic and copies ran while one was open for 0% of the time, Pallas kernels for 15%

profile of v5, /device:TPU:1, one launch (start us, length us, event | category | flops | bytes accessed | tf_op | source)
XLA Modules:
  0.0 87.5 jit_solution(14557647638165194287)
XLA Ops:
  0.6 0.1 pad_add_fusion.place_ref
  0.7 0.0 copy-start
  0.7 0.7 copy-done
  1.4 1.7 %pack.1 = (f32[33,1326]{1,0:T(8,128)S(1)}, f32[32,1326]{1,0:T(8,128)S(1)}, f32[34,1326]{1,0:T(8,128)S(1)}, f32[34,1326]{1,0:T(8,128)S(1)}, f32[16,1326]{1,0:T(8,...) custom-call(s32[2]{0:T(128)S(1)} %pad_add_fusion.place_ref, ...), custom_call_target="tpu_custom_call" | custom-call | tf_op jit(solution)/shard_map/pack/pallas_call | solution.py:167
  3.1 3.3 %collective-permute-start = (f32[34,1326]{1,0:T(8,128)S(1)}, f32[34,1326]{1,0:T(8,128)S(1)}, u32[]{:S(2)}, u32[]{:S(2)}) collective-permute-start(f32[34,1326]{1,0:T(8,128)S(1)} %get-tuple-element.30), channel_id=1, source_target_pairs={{0,2},{2,0},{4,6},{6,4},{8,10},{10,8},{12,14},{14,12},{16,18},{18,... | collective-permute-start | bytes 541016 | tf_op jit(solution)/shard_map/ppermute | solution.py:542
  6.4 1.9 %collective-permute-start.1 = (f32[34,1326]{1,0:T(8,128)S(1)}, f32[34,1326]{1,0:T(8,128)S(1)}, u32[]{:S(2)}, u32[]{:S(2)}) collective-permute-start(f32[34,1326]{1,0:T(8,128)S(1)} %get-tuple-element.31), channel_id=1, source_target_pairs={{2,4},{6,8},{10,12},{14,16},{18,20},{22,24},{26,28},{30,32},{34,36... | collective-permute-start | bytes 541016 | tf_op jit(solution)/shard_map/ppermute | solution.py:541
  8.3 5.9 %collective-permute-start.2 = (f32[33,1326]{1,0:T(8,128)S(1)}, f32[33,1326]{1,0:T(8,128)S(1)}, u32[]{:S(2)}, u32[]{:S(2)}) collective-permute-start(f32[33,1326]{1,0:T(8,128)S(1)} %get-tuple-element.28.regrets_ref), channel_id=1, source_target_pairs={{0,1},{1,0},{2,3},{3,2},{4,5},{5,4},{6,7},{7,6},{8,9},{9,8},{10,11... | collective-permute-start | bytes 525104 | tf_op jit(solution)/shard_map/ppermute | solution.py:543
  14.2 0.1 collective-permute-start.3
  14.3 7.6 %collective-permute-start.5 = (f32[16,1326]{1,0:T(8,128)S(1)}, f32[16,1326]{1,0:T(8,128)S(1)}, u32[]{:S(2)}, u32[]{:S(2)}) collective-permute-start(f32[16,1326]{1,0:T(8,128)S(1)} %get-tuple-element.36), channel_id=1, source_target_pairs={{2,5},{3,4},{6,9},{7,8},{10,13},{11,12},{14,17},{15,16},{18,21},{1... | collective-permute-start | bytes 254600 | tf_op jit(solution)/shard_map/ppermute | solution.py:545
  22.0 6.3 %build_own.1 = (bf16[4,1408,1408]{2,1,0:T(8,128)(2,1)S(1)}, bf16[1408,1408]{1,0:T(8,128)(2,1)S(1)}) custom-call(bf16[128,1408]{1,0:T(8,128)(2,1)S(1)} %get-tuple-element.32.holding_ref, f32[8,1408]{1,0:T(8,128)S(1)} %get-tuple-element.33.rank_ref), custom_call_target="tpu_custom_call" | custom-call | flops 63438848 | bytes 15859712 | tf_op jit(solution)/shard_map/build_own/pallas_call | solution.py:245
  28.3 0.0 collective-permute-done.even_ref
  28.3 0.0 collective-permute-done.1.cross_ref
  28.3 5.9 %build_side.1 = (bf16[2,1408,1408]{2,1,0:T(8,128)(2,1)S(1)}, bf16[2,1408,1408]{2,1,0:T(8,128)(2,1)S(1)}, f32[8,128]{1,0:T(8,128)S(1)}) custom-call(s32[2]{0:T(128)S(1)} %pad_add_fusion.place_ref, f32[34,1326]{1,0:T(8,128)S(1)} %collective-permute-done.even_ref, f32[34,1326]{1,0:T(8,128)S(1)} %collective-permute-done.1.cross_ref, ...), custom_call_target="tpu_custom_call" | custom-call | flops 63438848 | bytes 15859712 | tf_op jit(solution)/shard_map/build_side/pallas_call | solution.py:258
  34.2 0.0 collective-permute-done.3.chance_ref.chance_other_ref
  34.2 0.0 collective-permute-done.2.regrets_ref.regrets_other_ref
  34.2 0.6 forward.1
  34.8 0.1 collective-permute-start.4
  34.9 0.8 collective-permute-done.5.cross_other_ref
  35.7 0.5 collective-permute-done.4.even_other_ref
  36.2 6.7 %first.1 = (f32[2,64,1408]{2,1,0:T(8,128)S(1)}, f32[64,1408]{1,0:T(8,128)S(1)}, f32[2,64,1408]{2,1,0:T(8,128)S(1)}, f32[128,128]{1,0:T(8,128)S(1)}, bf16[2,64,19...) custom-call(s32[2]{0:T(128)S(1)} %pad_add_fusion.place_ref, ...), custom_call_target="tpu_custom_call" | custom-call | tf_op jit(solution)/shard_map/first/pallas_call | solution.py:417
  42.9 23.8 %all_to_all.10 = f32[128,1,128]{2,1,0:T(1,128)S(1)} all-to-all(f32[128,1,128]{2,1,0:T(1,128)S(1)} %bitcast.19), channel_id=1, replica_groups=mesh['leaf_0'=4,'leaf_1'=4,'leaf_2'=4,'leaf_3'=2,'player'=2] {'leaf_0','..., dimensions={0} | all-to-all | bytes 131072 | tf_op jit(solution)/shard_map/all_to_all | solution.py:553
  66.7 4.5 %second.1 = (f32[32,1326]{1,0:T(8,128)}, f32[32,1408]{1,0:T(8,128)S(1)}, f32[32,1408]{1,0:T(8,128)S(1)}, f32[128,128]{1,0:T(8,128)S(1)}) custom-call(f32[128,128]{1,0:T(8,128)S(1)} %bitcast.17, f32[2,64,1408]{2,1,0:T(8,128)S(1)} %get-tuple-element.44.window_ref, f32[64,1408]{1,0:T(8,128)S(1)} %get-tuple-element.45.reached_ref, ...), custom_call_target="tpu_custom_call" | custom-call | tf_op jit(solution)/shard_map/second/pallas_call | solution.py:493
  71.2 15.4 %all_to_all.11 = f32[128,1,128]{2,1,0:T(1,128)S(1)} all-to-all(f32[128,1,128]{2,1,0:T(1,128)S(1)} %bitcast.20), channel_id=1, replica_groups=mesh['leaf_0'=4,'leaf_1'=4,'leaf_2'=4,'leaf_3'=2,'player'=2] {'leaf_0','..., dimensions={0} | all-to-all | bytes 131072 | tf_op jit(solution)/shard_map/all_to_all | solution.py:553
  86.7 0.8 tail.1
Async XLA Ops:
  0.7 0.7 copy-start
  3.1 25.2 %collective-permute-start = (f32[34,1326]{1,0:T(8,128)S(1)}, f32[34,1326]{1,0:T(8,128)S(1)}, u32[]{:S(2)}, u32[]{:S(2)}) collective-permute-start(f32[34,1326]{1,0:T(8,128)S(1)} %get-tuple-element.30), channel_id=1, source_target_pairs={{0,2},{2,0},{4,6},{6,4},{8,10},{10,8},{12,14},{14,12},{16,18},{18,... | collective-permute-start | bytes 541016 | tf_op jit(solution)/shard_map/ppermute | solution.py:542
  6.4 21.9 %collective-permute-start.1 = (f32[34,1326]{1,0:T(8,128)S(1)}, f32[34,1326]{1,0:T(8,128)S(1)}, u32[]{:S(2)}, u32[]{:S(2)}) collective-permute-start(f32[34,1326]{1,0:T(8,128)S(1)} %get-tuple-element.31), channel_id=1, source_target_pairs={{2,4},{6,8},{10,12},{14,16},{18,20},{22,24},{26,28},{30,32},{34,36... | collective-permute-start | bytes 541016 | tf_op jit(solution)/shard_map/ppermute | solution.py:541
  8.3 25.9 %collective-permute-start.2 = (f32[33,1326]{1,0:T(8,128)S(1)}, f32[33,1326]{1,0:T(8,128)S(1)}, u32[]{:S(2)}, u32[]{:S(2)}) collective-permute-start(f32[33,1326]{1,0:T(8,128)S(1)} %get-tuple-element.28.regrets_ref), channel_id=1, source_target_pairs={{0,1},{1,0},{2,3},{3,2},{4,5},{5,4},{6,7},{7,6},{8,9},{9,8},{10,11... | collective-permute-start | bytes 525104 | tf_op jit(solution)/shard_map/ppermute | solution.py:543
  14.2 20.0 %collective-permute-start.3 = (f32[32,1326]{1,0:T(8,128)S(1)}, f32[32,1326]{1,0:T(8,128)S(1)}, u32[]{:S(2)}, u32[]{:S(2)}) collective-permute-start(f32[32,1326]{1,0:T(8,128)S(1)} %get-tuple-element.29.chance_ref), channel_id=1, source_target_pairs={{0,1},{1,0},{2,3},{3,2},{4,5},{5,4},{6,7},{7,6},{8,9},{9,8},{10,11... | collective-permute-start | bytes 509192 | tf_op jit(solution)/shard_map/ppermute | solution.py:544
  14.3 21.4 %collective-permute-start.5 = (f32[16,1326]{1,0:T(8,128)S(1)}, f32[16,1326]{1,0:T(8,128)S(1)}, u32[]{:S(2)}, u32[]{:S(2)}) collective-permute-start(f32[16,1326]{1,0:T(8,128)S(1)} %get-tuple-element.36), channel_id=1, source_target_pairs={{2,5},{3,4},{6,9},{7,8},{10,13},{11,12},{14,17},{15,16},{18,21},{1... | collective-permute-start | bytes 254600 | tf_op jit(solution)/shard_map/ppermute | solution.py:545
  34.8 1.4 %collective-permute-start.4 = (f32[16,1326]{1,0:T(8,128)S(1)}, f32[16,1326]{1,0:T(8,128)S(1)}, u32[]{:S(2)}, u32[]{:S(2)}) collective-permute-start(f32[16,1326]{1,0:T(8,128)S(1)} %forward.1), channel_id=1, source_target_pairs={{0,2},{2,0},{4,6},{6,4},{8,10},{10,8},{12,14},{14,12},{16,18},{18,... | collective-permute-start | bytes 254600 | tf_op jit(solution)/shard_map/ppermute | solution.py:550

commit v6 on v5

--- a/solution.py
+++ b/solution.py
@@ -18,7 +18,8 @@
 SIDE = 16
 WINDOW = OWN + 2 * SIDE
 BOARD_LEAVES = 8
-EDGE = 34
+EDGE = 32
+EARLY = 2
 LIMIT = 10 << 20
 SMALL = 6 << 20
 PIECES = 2
@@ -30,8 +31,11 @@
 def edge_rows(regrets_ref, chance_ref, edge_ref, last):
     at = OWN - 10 if last else 0
     edge_ref[0:10] = regrets_ref[at : at + 10]
-    at = OWN - 5 if last else 0
-    edge_ref[10:15] = chance_ref[at : at + 5]
+    if last:
+        edge_ref[10 : 15 - EARLY] = chance_ref[OWN - 5 : OWN - EARLY]
+        edge_ref[15 - EARLY : 15] = regrets_ref[OWN + 1 :]
+    else:
+        edge_ref[10:15] = chance_ref[0:5]
     edge_ref[15:16] = jnp.zeros((1, HANDS), F32)
 
 
@@ -49,7 +53,7 @@
     return pl.pallas_call(
         forward_kernel,
         out_shape=jax.ShapeDtypeStruct((16, HANDS), F32),
-        in_specs=[SMEM()] + [VMEM()] * 3,
+        in_specs=[SMEM(), VMEM(), VMEM(), SMEM()],
         out_specs=VMEM(),
         compiler_params=pltpu.CompilerParams(vmem_limit_bytes=SMALL),
         name="forward",
@@ -57,10 +61,10 @@
 
 
 def pack_kernel(
-    place_ref, boards_hbm, pot_ref, regrets_hbm, chance_hbm, rank_hbm, cards_hbm, parent_hbm,
+    place_ref, boards_hbm, pot_hbm, regrets_hbm, chance_hbm, rank_hbm, cards_hbm, parent_hbm,
     regrets_ref, chance_ref, even_ref, cross_ref, cross_other_ref,
     wide_rank_ref, free_ref, holding_ref, pots_ref, nodes_ref,
-    board_cards_ref, rank_ref, cards_ref, parent_ref, sems,
+    board_cards_ref, pot_ref, rank_ref, cards_ref, parent_ref, all_chance_ref, sems,
 ):
     moves = [
         (boards_hbm, board_cards_ref),
@@ -68,7 +72,8 @@
         (cards_hbm, cards_ref),
         (parent_hbm, parent_ref),
         (regrets_hbm, regrets_ref.at[:OWN]),
-        (chance_hbm, chance_ref),
+        (chance_hbm, all_chance_ref),
+        (pot_hbm, pot_ref),
     ]
     copies = [
         pltpu.make_async_copy(source, target, sems.at[at])
@@ -77,7 +82,6 @@
     for copy in copies:
         copy.start()
     pots_ref[...] = jnp.zeros_like(pots_ref)
-    pots_ref[0:1, 0:OWN] = pot_ref[...]
     wide_rank_ref[...] = jnp.zeros_like(wide_rank_ref)
     free_ref[...] = jnp.zeros_like(free_ref)
     holding_ref[...] = jnp.zeros_like(holding_ref)
@@ -112,12 +116,15 @@
     nodes_ref[...] = jnp.broadcast_to(held, nodes_ref.shape)
     for copy in copies[4:]:
         copy.wait()
+    pots_ref[0:1, 0:OWN] = pot_ref[...]
+    chance_ref[...] = all_chance_ref[0 : OWN - EARLY]
+    regrets_ref[OWN + 1 :] = all_chance_ref[OWN - EARLY :]
 
     def ends(ref, last):
         at = OWN - 15 if last else 0
         ref[0:15] = regrets_ref[at : at + 15]
         at = OWN - 10 if last else 0
-        ref[15:25] = chance_ref[at : at + 10]
+        ref[15:25] = all_chance_ref[at : at + 10]
         at = 2 if last else 0
         ref[25:27] = ranks[at : at + 2]
         ref[27:28] = rows[at]
@@ -138,8 +145,8 @@
         ends(cross_ref, False)
         edge_rows(regrets_ref, chance_ref, cross_other_ref, False)
 
-    regrets_ref[OWN:] = jnp.zeros((1, HANDS), F32)
-    regrets_ref[OWN:, 0:128] = held
+    regrets_ref[OWN : OWN + 1] = jnp.zeros((1, HANDS), F32)
+    regrets_ref[OWN : OWN + 1, 0:128] = held
 
 
 SMEM = functools.partial(pl.BlockSpec, memory_space=pltpu.SMEM)
@@ -152,8 +159,8 @@
 
 def pack(place, board_cards, pot_row, regrets, chance, hand_rank, cards, parent):
     shapes = (
-        jax.ShapeDtypeStruct((OWN + 1, HANDS), F32),
-        jax.ShapeDtypeStruct((OWN, HANDS), F32),
+        jax.ShapeDtypeStruct((OWN + 1 + EARLY, HANDS), F32),
+        jax.ShapeDtypeStruct((OWN - EARLY, HANDS), F32),
         jax.ShapeDtypeStruct((EDGE, HANDS), F32),
         jax.ShapeDtypeStruct((EDGE, HANDS), F32),
         jax.ShapeDtypeStruct((16, HANDS), F32),
@@ -163,22 +170,24 @@
         jax.ShapeDtypeStruct((8, 128), F32),
         jax.ShapeDtypeStruct((8, 128), F32),
     )
-    large = (regrets, chance, hand_rank, cards, parent)
+    large = (board_cards, pot_row, regrets, chance, hand_rank, cards, parent)
     return pl.pallas_call(
         pack_kernel,
         out_shape=shapes,
-        in_specs=[SMEM(), HBM(), VMEM()] + [HBM()] * len(large),
+        in_specs=[SMEM()] + [HBM()] * len(large),
         out_specs=[VMEM()] * len(shapes),
         scratch_shapes=[
             pltpu.SMEM((4, 5), jnp.int32),
+            pltpu.VMEM((1, OWN), F32),
             pltpu.VMEM((4, HANDS), jnp.int32),
             pltpu.VMEM((2, HANDS), jnp.int32),
             pltpu.VMEM(parent.shape, jnp.int32),
-            pltpu.SemaphoreType.DMA((6,)),
+            pltpu.VMEM((OWN, HANDS), F32),
+            pltpu.SemaphoreType.DMA((7,)),
         ],
         compiler_params=pltpu.CompilerParams(vmem_limit_bytes=SMALL),
         name="pack",
-    )(place, in_hbm(board_cards), pot_row, *map(in_hbm, large))
+    )(place, *map(in_hbm, large))
 
 
 def sides(place_ref, even_ref, cross_ref, rows):
@@ -220,16 +229,39 @@
     fill(rank_ref, apart_ref, column_ref, [(b, matrix_ref, b) for b in range(4)])
 
 
+def outer_boards(mine, other):
+    leaf = lax.broadcasted_iota(jnp.int32, mine.shape, 1)
+    inside = leaf < WINDOW
+
+    def node_at(row, at):
+        return jnp.max(jnp.where(leaf == at, row, -2.0))
+
+    def ends_of(row, node):
+        held = inside & (row == node)
+        return jnp.min(jnp.where(held, leaf, WINDOW)), jnp.max(jnp.where(held, leaf, -1))
+
+    begin, _ = ends_of(mine, node_at(mine, SIDE))
+    begin, _ = ends_of(other, node_at(other, begin))
+    _, end = ends_of(mine, node_at(mine, SIDE + OWN - 1))
+    _, end = ends_of(other, node_at(other, end))
+    return (begin < BOARD_LEAVES) | (end >= WINDOW - BOARD_LEAVES)
+
+
 def build_side_kernel(
-    place_ref, even_ref, cross_ref, apart_ref, near_ref, far_ref, token_ref, rank_ref, column_ref
+    place_ref, even_ref, cross_ref, nodes_ref, regrets_other_ref, apart_ref,
+    near_ref, far_ref, token_ref, rank_ref, column_ref,
 ):
-    token_ref[...] = jnp.zeros_like(token_ref)
+    outer = outer_boards(nodes_ref[0:1, :], regrets_other_ref[OWN : OWN + 1, 0:128])
+    token_ref[0] = outer.astype(jnp.int32)
     left, right = sides(place_ref, even_ref, cross_ref, slice(25, 27))
     rank_ref[...] = jnp.zeros_like(rank_ref)
     rank_ref[0:2, :HANDS] = left
     rank_ref[2:4, :HANDS] = right
-    targets = [(1, near_ref, 0), (2, near_ref, 1), (0, far_ref, 0), (3, far_ref, 1)]
-    fill(rank_ref, apart_ref, column_ref, targets)
+    fill(rank_ref, apart_ref, column_ref, [(1, near_ref, 0), (2, near_ref, 1)])
+
+    @pl.when(outer)
+    def _():
+        fill(rank_ref, apart_ref, column_ref, [(0, far_ref, 0), (3, far_ref, 1)])
 
 
 BUILD_COST = pl.CostEstimate(
@@ -254,21 +286,21 @@
     )(holding, ranks)
 
 
-def build_side(place, even, cross, apart):
+def build_side(place, even, cross, nodes, regrets_other, apart):
     return pl.pallas_call(
         build_side_kernel,
         out_shape=(
             matrices_shape(2),
             matrices_shape(2),
-            jax.ShapeDtypeStruct((8, 128), F32),
+            jax.ShapeDtypeStruct((1,), jnp.int32),
         ),
-        in_specs=[SMEM()] + [VMEM()] * 3,
-        out_specs=[VMEM()] * 3,
+        in_specs=[SMEM()] + [VMEM()] * 5,
+        out_specs=[VMEM(), VMEM(), SMEM()],
         scratch_shapes=[pltpu.VMEM((8, WIDE), F32), pltpu.VMEM((WIDE, 128), F32)],
         compiler_params=pltpu.CompilerParams(vmem_limit_bytes=LIMIT),
         cost_estimate=BUILD_COST,
         name="build_side",
-    )(place, even, cross, apart)
+    )(place, even, cross, nodes, regrets_other, apart)
 
 
 def node_totals(same, values):
@@ -313,6 +345,7 @@
 
 def first_kernel(
     place_ref,
+    outer_ref,
     regrets_ref,
     chance_ref,
     even_ref,
@@ -341,7 +374,7 @@
     left, right = sides(place_ref, even_ref, cross_ref, slice(0, 30))
     left_other, right_other = sides(place_ref, even_other_ref, cross_other_ref, slice(0, 15))
     same_ref[0] = same_node(nodes_ref[0:1, :])
-    same_ref[1] = same_node(regrets_other_ref[OWN:, 0:128])
+    same_ref[1] = same_node(regrets_other_ref[OWN : OWN + 1, 0:128])
     free_ref[...] = jnp.zeros_like(free_ref)
     free_ref[0:2, :HANDS] = left[27:29]
     free_ref[2:6] = own_free_ref[0:4]
@@ -357,13 +390,15 @@
     window_ref[0, low:high, :HANDS] = regrets_ref[:OWN]
     window_ref[0, high : high + 15, :HANDS] = right[0:15]
     policy_ref[0, low - 10 : low, :HANDS] = left[15:25]
-    policy_ref[0, low:high, :HANDS] = chance_ref[...]
+    policy_ref[0, low : high - EARLY, :HANDS] = chance_ref[...]
+    policy_ref[0, high - EARLY : high, :HANDS] = regrets_ref[OWN + 1 :]
     policy_ref[0, high : high + 10, :HANDS] = right[15:25]
     window_ref[1, low - 10 : low, :HANDS] = left_other[0:10]
     window_ref[1, low:high, :HANDS] = regrets_other_ref[:OWN]
     window_ref[1, high : high + 10, :HANDS] = right_other[0:10]
     reached_ref[low - 5 : low, :HANDS] = left_other[10:15]
-    reached_ref[low:high, :HANDS] = chance_other_ref[...]
+    reached_ref[low : high - EARLY, :HANDS] = chance_other_ref[...]
+    reached_ref[high - EARLY : high, :HANDS] = regrets_other_ref[OWN + 1 :]
     reached_ref[high : high + 5, :HANDS] = right_other[10:15]
     free = board_rows(free_ref, range(8))
     reached_ref[...] = reached_ref[...] * free
@@ -390,8 +425,18 @@
         board(b + 2, own_matrix_ref[b])
     board(1, near_ref[0])
     board(6, near_ref[1])
-    board(0, far_ref[0])
-    board(7, far_ref[1])
+
+    @pl.when(outer_ref[0] == 1)
+    def _():
+        board(0, far_ref[0])
+        board(7, far_ref[1])
+
+    @pl.when(outer_ref[0] != 1)
+    def _():
+        for p in range(2):
+            for b in (0, 7):
+                rows = slice(b * BOARD_LEAVES, (b + 1) * BOARD_LEAVES)
+                values_ref[p, rows, :] = jnp.zeros((BOARD_LEAVES, WIDE), F32)
 
     sums = []
     for p in range(2):
@@ -404,7 +449,7 @@
     sums_ref[...] = jnp.where(lane == 0, sums[0], jnp.where(lane == 1, sums[1], 0.0))
 
 
-def first(place, arrays):
+def first(place, outer, arrays):
     shapes = (
         jax.ShapeDtypeStruct((2, WINDOW, WIDE), F32),
         jax.ShapeDtypeStruct((WINDOW, WIDE), F32),
@@ -417,7 +462,7 @@
     return pl.pallas_call(
         first_kernel,
         out_shape=shapes,
-        in_specs=[SMEM()] + [VMEM()] * len(arrays),
+        in_specs=[SMEM(), SMEM()] + [VMEM()] * len(arrays),
         out_specs=[VMEM()] * len(shapes),
         scratch_shapes=[
             pltpu.VMEM((2, WINDOW, WIDE), F32),
@@ -426,7 +471,7 @@
         ],
         compiler_params=pltpu.CompilerParams(vmem_limit_bytes=LIMIT),
         name="first",
-    )(place, *arrays)
+    )(place, outer, *arrays)
 
 
 def second_kernel(
@@ -545,9 +590,9 @@
     cross_other = lax.ppermute(cross_other, LEAF + ("player",), diagonal)
 
     own_matrix, apart = build_own(holding, ranks)
-    near, far, built = build_side(place, even, cross, apart)
-
-    even_other = lax.ppermute(forward(place, regrets_other, chance_other, built), LEAF, even_pairs)
+    near, far, outer = build_side(place, even, cross, nodes, regrets_other, apart)
+
+    even_other = lax.ppermute(forward(place, regrets_other, chance_other, outer), LEAF, even_pairs)
 
     def gathered(sums):
         return lax.all_to_all(sums.reshape(devices, 1, 128), LEAF, 0, 0).reshape(128, 128)
@@ -555,6 +600,7 @@
     count = float(leaf_count * HANDS)
     window, reached, instant, sums, same, all_free, all_pot = first(
         place,
+        outer,
         (regrets, chance, even, cross, regrets_other, chance_other, even_other, cross_other)
         + (nodes, free, pots, own_matrix, near, far),
     )

time: 87.7 us -> 87.2 us (level)
  waiting for transfers between devices: 1.29 us -> 3.01 us
  blocking collectives: 39.3 us -> 38.3 us
    ppermute x1, starting transfers between devices: 3.32 us -> 0.95 us  [local(): even = lax.ppermute(even, LEAF, even_pairs)]
    ppermute x1, starting transfers between devices: 5.9 us -> 7.83 us  [local(): regrets_other = lax.ppermute(regrets, 'player', [(0, 1), (1, 0)])]
    ppermute x1, waiting for transfers between devices: 0.01 us -> 1.73 us  [local(): cross = lax.ppermute(cross, LEAF, cross_pairs)]
    all_to_all x2, blocking collectives: 39.3 us -> 38.3 us  [gathered(): lax.all_to_all(sums.reshape(devices, 1, 128), LEAF, 0, 0).reshape(128, 128)]
where the time goes in v6:
time: 87.2 us; the launch traced here: 87 us
  blocking collectives  38.3 us (44%)
  Pallas kernels  25.9 us (30%)
  starting transfers between devices  19 us (22%)
  waiting for transfers between devices  3.01 us (3%)
    all_to_all x2, blocking collectives, gathered(): lax.all_to_all(sums.reshape(devices, 1, 128), LEAF, 0, 0).reshape(128, 128)  38.3 us
    ppermute x1, starting transfers between devices, local(): regrets_other = lax.ppermute(regrets, 'player', [(0, 1), (1, 0)])  7.83 us
    ppermute x1, starting transfers between devices, local(): cross_other = lax.ppermute(cross_other, LEAF + ('player',), diagonal)  7.47 us
    pallas_call x1, Pallas kernels, build_own(): pl.pallas_call(build_own_kernel, out_shape=(matrices_shape(4), jax.ShapeD...  6.3 us
    pallas_call x1, Pallas kernels, first(): pl.pallas_call(first_kernel, out_shape=shapes, in_specs=[SMEM(), SMEM()]...  6.13 us
    pallas_call x1, Pallas kernels, build_side(): pl.pallas_call(build_side_kernel, out_shape=(matrices_shape(2), matrices_...  5.16 us
    pallas_call x1, Pallas kernels, second(): pl.pallas_call(functools.partial(second_kernel, count=count), out_shape=s...  4.53 us
    ppermute x1, starting transfers between devices, local(): cross = lax.ppermute(cross, LEAF, cross_pairs)  2.52 us
  transfers between devices with their start and end apart: 6, of which 2 were waited for; matrix products, arithmetic and copies ran while one was open for 0% of the time, Pallas kernels for 15%

profile of v6, /device:TPU:1, one launch (start us, length us, event | category | flops | bytes accessed | tf_op | source)
XLA Modules:
  0.0 87.0 jit_solution(841742660907394481)
XLA Ops:
  0.6 0.1 pad_add_fusion.place_ref
  0.7 1.8 %pack.1 = (f32[35,1326]{1,0:T(8,128)S(1)}, f32[30,1326]{1,0:T(8,128)S(1)}, f32[32,1326]{1,0:T(8,128)S(1)}, f32[32,1326]{1,0:T(8,128)S(1)}, f32[16,1326]{1,0:T(8,...) custom-call(s32[2]{0:T(128)S(1)} %pad_add_fusion.place_ref, ...), custom_call_target="tpu_custom_call" | custom-call | tf_op jit(solution)/shard_map/pack/pallas_call | solution.py:174
  2.5 7.8 %collective-permute-start.2 = (f32[35,1326]{1,0:T(8,128)S(1)}, f32[35,1326]{1,0:T(8,128)S(1)}, u32[]{:S(2)}, u32[]{:S(2)}) collective-permute-start(f32[35,1326]{1,0:T(8,128)S(1)} %get-tuple-element.31.regrets_ref), channel_id=1, source_target_pairs={{0,1},{1,0},{2,3},{3,2},{4,5},{5,4},{6,7},{7,6},{8,9},{9,8},{10,11... | collective-permute-start | bytes 556928 | tf_op jit(solution)/shard_map/ppermute | solution.py:588
  10.3 0.9 %collective-permute-start = (f32[32,1326]{1,0:T(8,128)S(1)}, f32[32,1326]{1,0:T(8,128)S(1)}, u32[]{:S(2)}, u32[]{:S(2)}) collective-permute-start(f32[32,1326]{1,0:T(8,128)S(1)} %get-tuple-element.28), channel_id=1, source_target_pairs={{0,2},{2,0},{4,6},{6,4},{8,10},{10,8},{12,14},{14,12},{16,18},{18,... | collective-permute-start | bytes 509192 | tf_op jit(solution)/shard_map/ppermute | solution.py:587
  11.3 2.5 %collective-permute-start.1 = (f32[32,1326]{1,0:T(8,128)S(1)}, f32[32,1326]{1,0:T(8,128)S(1)}, u32[]{:S(2)}, u32[]{:S(2)}) collective-permute-start(f32[32,1326]{1,0:T(8,128)S(1)} %get-tuple-element.29), channel_id=1, source_target_pairs={{2,4},{6,8},{10,12},{14,16},{18,20},{22,24},{26,28},{30,32},{34,36... | collective-permute-start | bytes 509192 | tf_op jit(solution)/shard_map/ppermute | solution.py:586
  13.8 0.1 collective-permute-start.3
  13.9 7.5 %collective-permute-start.5 = (f32[16,1326]{1,0:T(8,128)S(1)}, f32[16,1326]{1,0:T(8,128)S(1)}, u32[]{:S(2)}, u32[]{:S(2)}) collective-permute-start(f32[16,1326]{1,0:T(8,128)S(1)} %get-tuple-element.37), channel_id=1, source_target_pairs={{2,5},{3,4},{6,9},{7,8},{10,13},{11,12},{14,17},{15,16},{18,21},{1... | collective-permute-start | bytes 254600 | tf_op jit(solution)/shard_map/ppermute | solution.py:590
  21.4 6.3 %build_own.1 = (bf16[4,1408,1408]{2,1,0:T(8,128)(2,1)S(1)}, bf16[1408,1408]{1,0:T(8,128)(2,1)S(1)}) custom-call(bf16[128,1408]{1,0:T(8,128)(2,1)S(1)} %get-tuple-element.32.holding_ref, f32[8,1408]{1,0:T(8,128)S(1)} %get-tuple-element.33.rank_ref), custom_call_target="tpu_custom_call" | custom-call | flops 63438848 | bytes 15859712 | tf_op jit(solution)/shard_map/build_own/pallas_call | solution.py:277
  27.7 0.0 collective-permute-done.even_ref
  27.7 1.7 %collective-permute-done.1.cross_ref = f32[32,1326]{1,0:T(8,128)S(1)} collective-permute-done((f32[32,1326]{1,0:T(8,128)S(1)}, f32[32,1326]{1,0:T(8,128)S(1)}, u32[]{:S(2)}, u32[]{:S(2)}) %collective-permute-start.1) | collective-permute-done | bytes 169760 | tf_op jit(solution)/shard_map/ppermute | solution.py:586
  29.4 0.0 collective-permute-done.2.regrets_other_ref.regrets_ref
  29.4 5.2 %build_side.1 = (bf16[2,1408,1408]{2,1,0:T(8,128)(2,1)S(1)}, bf16[2,1408,1408]{2,1,0:T(8,128)(2,1)S(1)}, s32[1]{0:T(128)}) custom-call(s32[2]{0:T(128)S(1)} %pad_add_fusion.place_ref, f32[32,1326]{1,0:T(8,128)S(1)} %collective-permute-done.even_ref, f32[32,1326]{1,0:T(8,128)S(1)} %collective-permute-done.1.cross_ref, ...), custom_call_target="tpu_custom_call" | custom-call | flops 63438848 | bytes 15859712 | tf_op jit(solution)/shard_map/build_side/pallas_call | solution.py:290
  34.6 0.0 collective-permute-done.3.chance_ref.chance_other_ref
  34.6 1.2 %forward.1 = f32[16,1326]{1,0:T(8,128)S(1)} custom-call(s32[2]{0:T(128)S(1)} %pad_add_fusion.place_ref, f32[35,1326]{1,0:T(8,128)S(1)} %collective-permute-done.2.regrets_other_ref.regrets_ref, f32[30,1326]{1,0:T(8,128)S(1)} %collective-permute-done.3.chance_ref.chance_other_ref, s32[1]{0:T(128)} %get-tuple-element.35.after_ref.outer_ref), custom_call_target="tpu_custom_call" | custom-call | tf_op jit(solution)/shard_map/forward/pallas_call | solution.py:53
  35.8 0.1 collective-permute-start.4
  35.9 0.0 collective-permute-done.5.cross_other_ref
  35.9 1.3 %collective-permute-done.4.even_other_ref = f32[16,1326]{1,0:T(8,128)S(1)} collective-permute-done((f32[16,1326]{1,0:T(8,128)S(1)}, f32[16,1326]{1,0:T(8,128)S(1)}, u32[]{:S(2)}, u32[]{:S(2)}) %collective-permute-start.4) | collective-permute-done | bytes 84896 | tf_op jit(solution)/shard_map/ppermute | solution.py:595
  37.2 6.1 %first.1 = (f32[2,64,1408]{2,1,0:T(8,128)S(1)}, f32[64,1408]{1,0:T(8,128)S(1)}, f32[2,64,1408]{2,1,0:T(8,128)S(1)}, f32[128,128]{1,0:T(8,128)S(1)}, bf16[2,64,19...) custom-call(s32[2]{0:T(128)S(1)} %pad_add_fusion.place_ref, ...), custom_call_target="tpu_custom_call" | custom-call | tf_op jit(solution)/shard_map/first/pallas_call | solution.py:462
  43.3 22.9 %all_to_all.10 = f32[128,1,128]{2,1,0:T(1,128)S(1)} all-to-all(f32[128,1,128]{2,1,0:T(1,128)S(1)} %bitcast.19), channel_id=1, replica_groups=mesh['leaf_0'=4,'leaf_1'=4,'leaf_2'=4,'leaf_3'=2,'player'=2] {'leaf_0','..., dimensions={0} | all-to-all | bytes 131072 | tf_op jit(solution)/shard_map/all_to_all | solution.py:598
  66.2 4.5 %second.1 = (f32[32,1326]{1,0:T(8,128)}, f32[32,1408]{1,0:T(8,128)S(1)}, f32[32,1408]{1,0:T(8,128)S(1)}, f32[128,128]{1,0:T(8,128)S(1)}) custom-call(f32[128,128]{1,0:T(8,128)S(1)} %bitcast.17, f32[2,64,1408]{2,1,0:T(8,128)S(1)} %get-tuple-element.44.window_ref, f32[64,1408]{1,0:T(8,128)S(1)} %get-tuple-element.45.reached_ref, ...), custom_call_target="tpu_custom_call" | custom-call | tf_op jit(solution)/shard_map/second/pallas_call | solution.py:538
  70.7 15.4 %all_to_all.11 = f32[128,1,128]{2,1,0:T(1,128)S(1)} all-to-all(f32[128,1,128]{2,1,0:T(1,128)S(1)} %bitcast.20), channel_id=1, replica_groups=mesh['leaf_0'=4,'leaf_1'=4,'leaf_2'=4,'leaf_3'=2,'player'=2] {'leaf_0','..., dimensions={0} | all-to-all | bytes 131072 | tf_op jit(solution)/shard_map/all_to_all | solution.py:598
  86.2 0.8 tail.1
Async XLA Ops:
  2.5 26.9 %collective-permute-start.2 = (f32[35,1326]{1,0:T(8,128)S(1)}, f32[35,1326]{1,0:T(8,128)S(1)}, u32[]{:S(2)}, u32[]{:S(2)}) collective-permute-start(f32[35,1326]{1,0:T(8,128)S(1)} %get-tuple-element.31.regrets_ref), channel_id=1, source_target_pairs={{0,1},{1,0},{2,3},{3,2},{4,5},{5,4},{6,7},{7,6},{8,9},{9,8},{10,11... | collective-permute-start | bytes 556928 | tf_op jit(solution)/shard_map/ppermute | solution.py:588
  10.3 17.4 %collective-permute-start = (f32[32,1326]{1,0:T(8,128)S(1)}, f32[32,1326]{1,0:T(8,128)S(1)}, u32[]{:S(2)}, u32[]{:S(2)}) collective-permute-start(f32[32,1326]{1,0:T(8,128)S(1)} %get-tuple-element.28), channel_id=1, source_target_pairs={{0,2},{2,0},{4,6},{6,4},{8,10},{10,8},{12,14},{14,12},{16,18},{18,... | collective-permute-start | bytes 509192 | tf_op jit(solution)/shard_map/ppermute | solution.py:587
  11.3 18.2 %collective-permute-start.1 = (f32[32,1326]{1,0:T(8,128)S(1)}, f32[32,1326]{1,0:T(8,128)S(1)}, u32[]{:S(2)}, u32[]{:S(2)}) collective-permute-start(f32[32,1326]{1,0:T(8,128)S(1)} %get-tuple-element.29), channel_id=1, source_target_pairs={{2,4},{6,8},{10,12},{14,16},{18,20},{22,24},{26,28},{30,32},{34,36... | collective-permute-start | bytes 509192 | tf_op jit(solution)/shard_map/ppermute | solution.py:586
  13.8 20.8 %collective-permute-start.3 = (f32[30,1326]{1,0:T(8,128)S(1)}, f32[30,1326]{1,0:T(8,128)S(1)}, u32[]{:S(2)}, u32[]{:S(2)}) collective-permute-start(f32[30,1326]{1,0:T(8,128)S(1)} %get-tuple-element.36.chance_ref), channel_id=1, source_target_pairs={{0,1},{1,0},{2,3},{3,2},{4,5},{5,4},{6,7},{7,6},{8,9},{9,8},{10,11... | collective-permute-start | bytes 477368 | tf_op jit(solution)/shard_map/ppermute | solution.py:589
  13.9 22.0 %collective-permute-start.5 = (f32[16,1326]{1,0:T(8,128)S(1)}, f32[16,1326]{1,0:T(8,128)S(1)}, u32[]{:S(2)}, u32[]{:S(2)}) collective-permute-start(f32[16,1326]{1,0:T(8,128)S(1)} %get-tuple-element.37), channel_id=1, source_target_pairs={{2,5},{3,4},{6,9},{7,8},{10,13},{11,12},{14,17},{15,16},{18,21},{1... | collective-permute-start | bytes 254600 | tf_op jit(solution)/shard_map/ppermute | solution.py:590
  35.8 1.4 %collective-permute-start.4 = (f32[16,1326]{1,0:T(8,128)S(1)}, f32[16,1326]{1,0:T(8,128)S(1)}, u32[]{:S(2)}, u32[]{:S(2)}) collective-permute-start(f32[16,1326]{1,0:T(8,128)S(1)} %forward.1), channel_id=1, source_target_pairs={{0,2},{2,0},{4,6},{6,4},{8,10},{10,8},{12,14},{14,12},{16,18},{18,... | collective-permute-start | bytes 254600 | tf_op jit(solution)/shard_map/ppermute | solution.py:595

commit v7 on v6

--- a/solution.py
+++ b/solution.py
@@ -9,6 +9,7 @@
 from jax.sharding import PartitionSpec as P
 
 LEAF = ("leaf_0", "leaf_1", "leaf_2", "leaf_3")
+LEAF_SIZES = (4, 4, 4, 2)
 DELTA = 0.05
 EPSILON = 1e-06
 
@@ -28,6 +29,17 @@
 VMEM = functools.partial(pl.BlockSpec, memory_space=pltpu.VMEM)
 
 
+def leaf_block():
+    index = 0
+    for axis, size in zip(LEAF, LEAF_SIZES):
+        index = index * size + lax.axis_index(axis)
+    return index
+
+
+def is_odd():
+    return lax.axis_index(LEAF[-1]) == 1
+
+
 def edge_rows(regrets_ref, chance_ref, edge_ref, last):
     at = OWN - 10 if last else 0
     edge_ref[0:10] = regrets_ref[at : at + 10]
@@ -39,29 +51,31 @@
     edge_ref[15:16] = jnp.zeros((1, HANDS), F32)
 
 
-def forward_kernel(place_ref, regrets_ref, chance_ref, after_ref, edge_ref):
-    @pl.when(place_ref[1] == 1)
+def forward_kernel(regrets_ref, chance_ref, after_ref, edge_ref):
+    odd = is_odd()
+
+    @pl.when(odd)
     def _():
         edge_rows(regrets_ref, chance_ref, edge_ref, False)
 
-    @pl.when(place_ref[1] != 1)
+    @pl.when(jnp.logical_not(odd))
     def _():
         edge_rows(regrets_ref, chance_ref, edge_ref, True)
 
 
-def forward(place, regrets, chance, after):
+def forward(regrets, chance, after):
     return pl.pallas_call(
         forward_kernel,
         out_shape=jax.ShapeDtypeStruct((16, HANDS), F32),
-        in_specs=[SMEM(), VMEM(), VMEM(), SMEM()],
+        in_specs=[VMEM()] * 3,
         out_specs=VMEM(),
         compiler_params=pltpu.CompilerParams(vmem_limit_bytes=SMALL),
         name="forward",
-    )(place, regrets, chance, after)
+    )(regrets, chance, after)
 
 
 def pack_kernel(
-    place_ref, boards_hbm, pot_hbm, regrets_hbm, chance_hbm, rank_hbm, cards_hbm, parent_hbm,
+    boards_hbm, pot_hbm, regrets_hbm, chance_hbm, rank_hbm, cards_hbm, parent_hbm,
     regrets_ref, chance_ref, even_ref, cross_ref, cross_other_ref,
     wide_rank_ref, free_ref, holding_ref, pots_ref, nodes_ref,
     board_cards_ref, pot_ref, rank_ref, cards_ref, parent_ref, all_chance_ref, sems,
@@ -103,7 +117,7 @@
     holding_ref[:, :HANDS] = jnp.where((deck == lower) | (deck == upper), 1.0, 0.0).astype(BF16)
 
     leaves = parent_ref.shape[0] * 128
-    begin = place_ref[0] * OWN - SIDE
+    begin = leaf_block() * OWN - SIDE
     line = (begin + 128) // 128 - 1
     held = [
         parent_ref[pl.ds(jnp.clip(line + j, 0, leaves // 128 - 1), 1), :].astype(F32)
@@ -120,6 +134,8 @@
     chance_ref[...] = all_chance_ref[0 : OWN - EARLY]
     regrets_ref[OWN + 1 :] = all_chance_ref[OWN - EARLY :]
 
+    odd = is_odd()
+
     def ends(ref, last):
         at = OWN - 15 if last else 0
         ref[0:15] = regrets_ref[at : at + 15]
@@ -133,13 +149,13 @@
         ref[29:30, 0:128] = pots_ref[0:1, :]
         ref[30:] = jnp.zeros((EDGE - 30, HANDS), F32)
 
-    @pl.when(place_ref[1] == 1)
+    @pl.when(odd)
     def _():
         ends(even_ref, False)
         ends(cross_ref, True)
         edge_rows(regrets_ref, chance_ref, cross_other_ref, True)
 
-    @pl.when(place_ref[1] != 1)
+    @pl.when(jnp.logical_not(odd))
     def _():
         ends(even_ref, True)
         ends(cross_ref, False)
@@ -149,7 +165,6 @@
     regrets_ref[OWN : OWN + 1, 0:128] = held
 
 
-SMEM = functools.partial(pl.BlockSpec, memory_space=pltpu.SMEM)
 HBM = functools.partial(pl.BlockSpec, memory_space=pltpu.HBM)
 
 
@@ -157,7 +172,7 @@
     return pltpu.with_memory_space_constraint(array, pltpu.HBM)
 
 
-def pack(place, board_cards, pot_row, regrets, chance, hand_rank, cards, parent):
+def pack(board_cards, pot_row, regrets, chance, hand_rank, cards, parent):
     shapes = (
         jax.ShapeDtypeStruct((OWN + 1 + EARLY, HANDS), F32),
         jax.ShapeDtypeStruct((OWN - EARLY, HANDS), F32),
@@ -174,7 +189,7 @@
     return pl.pallas_call(
         pack_kernel,
         out_shape=shapes,
-        in_specs=[SMEM()] + [HBM()] * len(large),
+        in_specs=[HBM()] * len(large),
         out_specs=[VMEM()] * len(shapes),
         scratch_shapes=[
             pltpu.SMEM((4, 5), jnp.int32),
@@ -187,11 +202,11 @@
         ],
         compiler_params=pltpu.CompilerParams(vmem_limit_bytes=SMALL),
         name="pack",
-    )(place, *map(in_hbm, large))
-
-
-def sides(place_ref, even_ref, cross_ref, rows):
-    odd = place_ref[1] == 1
+    )(*map(in_hbm, large))
+
+
+def sides(even_ref, cross_ref, rows):
+    odd = is_odd()
     even, cross = even_ref[rows], cross_ref[rows]
     return jnp.where(odd, even, cross), jnp.where(odd, cross, even)
 
@@ -248,12 +263,12 @@
 
 
 def build_side_kernel(
-    place_ref, even_ref, cross_ref, nodes_ref, regrets_other_ref, apart_ref,
-    near_ref, far_ref, token_ref, rank_ref, column_ref,
+    even_ref, cross_ref, nodes_ref, regrets_other_ref, apart_ref,
+    near_ref, far_ref, outer_ref, rank_ref, column_ref,
 ):
     outer = outer_boards(nodes_ref[0:1, :], regrets_other_ref[OWN : OWN + 1, 0:128])
-    token_ref[0] = outer.astype(jnp.int32)
-    left, right = sides(place_ref, even_ref, cross_ref, slice(25, 27))
+    outer_ref[...] = jnp.where(outer, jnp.ones_like(outer_ref), jnp.zeros_like(outer_ref))
+    left, right = sides(even_ref, cross_ref, slice(25, 27))
     rank_ref[...] = jnp.zeros_like(rank_ref)
     rank_ref[0:2, :HANDS] = left
     rank_ref[2:4, :HANDS] = right
@@ -286,21 +301,21 @@
     )(holding, ranks)
 
 
-def build_side(place, even, cross, nodes, regrets_other, apart):
+def build_side(even, cross, nodes, regrets_other, apart):
     return pl.pallas_call(
         build_side_kernel,
         out_shape=(
             matrices_shape(2),
             matrices_shape(2),
-            jax.ShapeDtypeStruct((1,), jnp.int32),
+            jax.ShapeDtypeStruct((8, 128), F32),
         ),
-        in_specs=[SMEM()] + [VMEM()] * 5,
-        out_specs=[VMEM(), VMEM(), SMEM()],
+        in_specs=[VMEM()] * 5,
+        out_specs=[VMEM()] * 3,
         scratch_shapes=[pltpu.VMEM((8, WIDE), F32), pltpu.VMEM((WIDE, 128), F32)],
         compiler_params=pltpu.CompilerParams(vmem_limit_bytes=LIMIT),
         cost_estimate=BUILD_COST,
         name="build_side",
-    )(place, even, cross, nodes, regrets_other, apart)
+    )(even, cross, nodes, regrets_other, apart)
 
 
 def node_totals(same, values):
@@ -344,7 +359,6 @@
 
 
 def first_kernel(
-    place_ref,
     outer_ref,
     regrets_ref,
     chance_ref,
@@ -371,8 +385,8 @@
     terms_ref,
     values_ref,
 ):
-    left, right = sides(place_ref, even_ref, cross_ref, slice(0, 30))
-    left_other, right_other = sides(place_ref, even_other_ref, cross_other_ref, slice(0, 15))
+    left, right = sides(even_ref, cross_ref, slice(0, 30))
+    left_other, right_other = sides(even_other_ref, cross_other_ref, slice(0, 15))
     same_ref[0] = same_node(nodes_ref[0:1, :])
     same_ref[1] = same_node(regrets_other_ref[OWN : OWN + 1, 0:128])
     free_ref[...] = jnp.zeros_like(free_ref)
@@ -426,12 +440,14 @@
     board(1, near_ref[0])
     board(6, near_ref[1])
 
-    @pl.when(outer_ref[0] == 1)
+    outer = jnp.max(outer_ref[0:1, :]) > 0.5
+
+    @pl.when(outer)
     def _():
         board(0, far_ref[0])
         board(7, far_ref[1])
 
-    @pl.when(outer_ref[0] != 1)
+    @pl.when(jnp.logical_not(outer))
     def _():
         for p in range(2):
             for b in (0, 7):
@@ -449,7 +465,7 @@
     sums_ref[...] = jnp.where(lane == 0, sums[0], jnp.where(lane == 1, sums[1], 0.0))
 
 
-def first(place, outer, arrays):
+def first(arrays):
     shapes = (
         jax.ShapeDtypeStruct((2, WINDOW, WIDE), F32),
         jax.ShapeDtypeStruct((WINDOW, WIDE), F32),
@@ -462,7 +478,7 @@
     return pl.pallas_call(
         first_kernel,
         out_shape=shapes,
-        in_specs=[SMEM(), SMEM()] + [VMEM()] * len(arrays),
+        in_specs=[VMEM()] * len(arrays),
         out_specs=[VMEM()] * len(shapes),
         scratch_shapes=[
             pltpu.VMEM((2, WINDOW, WIDE), F32),
@@ -471,7 +487,7 @@
         ],
         compiler_params=pltpu.CompilerParams(vmem_limit_bytes=LIMIT),
         name="first",
-    )(place, outer, *arrays)
+    )(*arrays)
 
 
 def second_kernel(
@@ -568,10 +584,8 @@
 
 
 def local(chance_reach, regrets_start, pot, parent, hand_cards, board_cards, hand_rank):
-    index = lax.axis_index(LEAF).astype(jnp.int32)
     devices = lax.axis_size(LEAF)
     leaf_count = parent.shape[1]
-    place = jnp.stack([index, lax.rem(index, 2)])
 
     even_pairs = [(i, i ^ 1) for i in range(devices)]
     cross_pairs = [(i, i + 1) for i in range(1, devices - 1, 2)]
@@ -580,7 +594,7 @@
     diagonal = [(2 * i + p, 2 * j + 1 - p) for i, j in cross_pairs for p in range(2)]
 
     regrets, chance, even, cross, cross_other, ranks, free, holding, pots, nodes = pack(
-        place, board_cards, pot[None], regrets_start[0], chance_reach[0], hand_rank,
+        board_cards, pot[None], regrets_start[0], chance_reach[0], hand_rank,
         hand_cards.T, parent.reshape(-1, 128),
     )
     cross = lax.ppermute(cross, LEAF, cross_pairs)
@@ -590,18 +604,17 @@
     cross_other = lax.ppermute(cross_other, LEAF + ("player",), diagonal)
 
     own_matrix, apart = build_own(holding, ranks)
-    near, far, outer = build_side(place, even, cross, nodes, regrets_other, apart)
-
-    even_other = lax.ppermute(forward(place, regrets_other, chance_other, outer), LEAF, even_pairs)
+    near, far, outer = build_side(even, cross, nodes, regrets_other, apart)
+
+    even_other = lax.ppermute(forward(regrets_other, chance_other, outer), LEAF, even_pairs)
 
     def gathered(sums):
         return lax.all_to_all(sums.reshape(devices, 1, 128), LEAF, 0, 0).reshape(128, 128)
 
     count = float(leaf_count * HANDS)
     window, reached, instant, sums, same, all_free, all_pot = first(
-        place,
-        outer,
-        (regrets, chance, even, cross, regrets_other, chance_other, even_other, cross_other)
+        (outer, regrets, chance, even, cross, regrets_other, chance_other, even_other)
+        + (cross_other,)
         + (nodes, free, pots, own_matrix, near, far),
     )
     values, moved, mine, sums = second(
@@ -614,8 +627,8 @@
 
 def solution(mesh):
     split = Mesh(
-        mesh.devices.reshape(4, 4, 4, 2, mesh.shape["player"]),
-        ("leaf_0", "leaf_1", "leaf_2", "leaf_3", "player"),
+        mesh.devices.reshape(*LEAF_SIZES, mesh.shape["player"]),
+        LEAF + ("player",),
     )
     placed = (
         P("player", LEAF, None),

time: 87.2 us -> 83.2 us (0.954)
  Pallas kernels: 25.9 us -> 22 us
    pallas_call x2, Pallas kernels: 7.89 us -> 6.18 us  [the longest x1 4.97 us: first(): pl.pallas_call(first_kernel, out_shape=shapes, in_specs=[VMEM()] * len(ar...]
    pallas_call x1, Pallas kernels: 1.21 us -> 0.03 us  [forward(): pl.pallas_call(forward_kernel, out_shape=jax.ShapeDtypeStruct((16, HANDS)...]
    pallas_call x1, Pallas kernels: 5.16 us -> 4.13 us  [build_side(): pl.pallas_call(build_side_kernel, out_shape=(matrices_shape(2), matrices_...]
  transfers between devices with their start and end apart: 6 -> 6, of which waited for: 2 -> 2; matrix products, arithmetic and copies ran while one was open for 0% -> 0% of each run, Pallas kernels for 15% -> 13%
where the time goes in v7:
time: 83.2 us; the launch traced here: 82.9 us
  blocking collectives  38.3 us (46%)
  Pallas kernels  22 us (26%)
  starting transfers between devices  19 us (23%)
  waiting for transfers between devices  2.99 us (4%)
    all_to_all x2, blocking collectives, gathered(): lax.all_to_all(sums.reshape(devices, 1, 128), LEAF, 0, 0).reshape(128, 128)  38.3 us
    ppermute x1, starting transfers between devices, local(): regrets_other = lax.ppermute(regrets, 'player', [(0, 1), (1, 0)])  7.83 us
    ppermute x1, starting transfers between devices, local(): cross_other = lax.ppermute(cross_other, LEAF + ('player',), diagonal)  7.47 us
    pallas_call x1, Pallas kernels, build_own(): pl.pallas_call(build_own_kernel, out_shape=(matrices_shape(4), jax.ShapeD...  6.32 us
    pallas_call x1, Pallas kernels, first(): pl.pallas_call(first_kernel, out_shape=shapes, in_specs=[VMEM()] * len(ar...  4.97 us
    pallas_call x1, Pallas kernels, second(): pl.pallas_call(functools.partial(second_kernel, count=count), out_shape=s...  4.52 us
    pallas_call x1, Pallas kernels, build_side(): pl.pallas_call(build_side_kernel, out_shape=(matrices_shape(2), matrices_...  4.13 us
    ppermute x1, starting transfers between devices, local(): cross = lax.ppermute(cross, LEAF, cross_pairs)  2.52 us
  transfers between devices with their start and end apart: 6, of which 2 were waited for; matrix products, arithmetic and copies ran while one was open for 0% of the time, Pallas kernels for 13%

profile of v7, /device:TPU:1, one launch (start us, length us, event | category | flops | bytes accessed | tf_op | source)
XLA Modules:
  0.0 82.9 jit_solution(13611129927208679540)
XLA Ops:
  0.6 1.2 %pack.1 = (f32[35,1326]{1,0:T(8,128)S(1)}, f32[30,1326]{1,0:T(8,128)S(1)}, f32[32,1326]{1,0:T(8,128)S(1)}, f32[32,1326]{1,0:T(8,128)S(1)}, f32[16,1326]{1,0:T(8,...) custom-call(s32[4,5]{1,0:T(4,128)} %boards_hbm.1, ...), custom_call_target="tpu_custom_call" | custom-call | tf_op jit(solution)/shard_map/pack/pallas_call | solution.py:189
  1.9 7.8 %collective-permute-start.2 = (f32[35,1326]{1,0:T(8,128)S(1)}, f32[35,1326]{1,0:T(8,128)S(1)}, u32[]{:S(2)}, u32[]{:S(2)}) collective-permute-start(f32[35,1326]{1,0:T(8,128)S(1)} %get-tuple-element.31.regrets_ref), channel_id=1, source_target_pairs={{0,1},{1,0},{2,3},{3,2},{4,5},{5,4},{6,7},{7,6},{8,9},{9,8},{10,11... | collective-permute-start | bytes 556928 | tf_op jit(solution)/shard_map/ppermute | solution.py:602
  9.7 0.9 %collective-permute-start = (f32[32,1326]{1,0:T(8,128)S(1)}, f32[32,1326]{1,0:T(8,128)S(1)}, u32[]{:S(2)}, u32[]{:S(2)}) collective-permute-start(f32[32,1326]{1,0:T(8,128)S(1)} %get-tuple-element.28), channel_id=1, source_target_pairs={{0,2},{2,0},{4,6},{6,4},{8,10},{10,8},{12,14},{14,12},{16,18},{18,... | collective-permute-start | bytes 509192 | tf_op jit(solution)/shard_map/ppermute | solution.py:601
  10.6 2.5 %collective-permute-start.1 = (f32[32,1326]{1,0:T(8,128)S(1)}, f32[32,1326]{1,0:T(8,128)S(1)}, u32[]{:S(2)}, u32[]{:S(2)}) collective-permute-start(f32[32,1326]{1,0:T(8,128)S(1)} %get-tuple-element.29), channel_id=1, source_target_pairs={{2,4},{6,8},{10,12},{14,16},{18,20},{22,24},{26,28},{30,32},{34,36... | collective-permute-start | bytes 509192 | tf_op jit(solution)/shard_map/ppermute | solution.py:600
  13.2 0.1 collective-permute-start.3
  13.3 7.5 %collective-permute-start.5 = (f32[16,1326]{1,0:T(8,128)S(1)}, f32[16,1326]{1,0:T(8,128)S(1)}, u32[]{:S(2)}, u32[]{:S(2)}) collective-permute-start(f32[16,1326]{1,0:T(8,128)S(1)} %get-tuple-element.37), channel_id=1, source_target_pairs={{2,5},{3,4},{6,9},{7,8},{10,13},{11,12},{14,17},{15,16},{18,21},{1... | collective-permute-start | bytes 254600 | tf_op jit(solution)/shard_map/ppermute | solution.py:604
  20.7 6.3 %build_own.1 = (bf16[4,1408,1408]{2,1,0:T(8,128)(2,1)S(1)}, bf16[1408,1408]{1,0:T(8,128)(2,1)S(1)}) custom-call(bf16[128,1408]{1,0:T(8,128)(2,1)S(1)} %get-tuple-element.32.holding_ref, f32[8,1408]{1,0:T(8,128)S(1)} %get-tuple-element.33.rank_ref), custom_call_target="tpu_custom_call" | custom-call | flops 63438848 | bytes 15859712 | tf_op jit(solution)/shard_map/build_own/pallas_call | solution.py:292
  27.1 0.0 collective-permute-done.even_ref
  27.1 1.7 %collective-permute-done.1.cross_ref = f32[32,1326]{1,0:T(8,128)S(1)} collective-permute-done((f32[32,1326]{1,0:T(8,128)S(1)}, f32[32,1326]{1,0:T(8,128)S(1)}, u32[]{:S(2)}, u32[]{:S(2)}) %collective-permute-start.1) | collective-permute-done | bytes 169760 | tf_op jit(solution)/shard_map/ppermute | solution.py:600
  28.8 0.0 collective-permute-done.2.regrets_other_ref.regrets_ref
  28.8 4.1 %build_side.1 = (bf16[2,1408,1408]{2,1,0:T(8,128)(2,1)S(1)}, bf16[2,1408,1408]{2,1,0:T(8,128)(2,1)S(1)}, f32[8,128]{1,0:T(8,128)S(1)}) custom-call(f32[32,1326]{1,0:T(8,128)S(1)} %collective-permute-done.even_ref, f32[32,1326]{1,0:T(8,128)S(1)} %collective-permute-done.1.cross_ref, f32[8,128]{1,0:T(8,128)S(1)} %get-tuple-element.30.nodes_ref, ...), custom_call_target="tpu_custom_call" | custom-call | flops 63438848 | bytes 15859712 | tf_op jit(solution)/shard_map/build_side/pallas_call | solution.py:305
  32.9 0.0 collective-permute-done.3.chance_ref.chance_other_ref
  33.0 0.1 collective-permute-start.4
  33.1 0.0 collective-permute-done.5.cross_other_ref
  33.1 1.3 %collective-permute-done.4.even_other_ref = f32[16,1326]{1,0:T(8,128)S(1)} collective-permute-done((f32[16,1326]{1,0:T(8,128)S(1)}, f32[16,1326]{1,0:T(8,128)S(1)}, u32[]{:S(2)}, u32[]{:S(2)}) %collective-permute-start.4) | collective-permute-done | bytes 84896 | tf_op jit(solution)/shard_map/ppermute | solution.py:609
  34.4 5.0 %first.1 = (f32[2,64,1408]{2,1,0:T(8,128)S(1)}, f32[64,1408]{1,0:T(8,128)S(1)}, f32[2,64,1408]{2,1,0:T(8,128)S(1)}, f32[128,128]{1,0:T(8,128)S(1)}, bf16[2,64,19...) custom-call(f32[8,128]{1,0:T(8,128)S(1)} %get-tuple-element.35.after_ref.outer_ref, ...), custom_call_target="tpu_custom_call" | custom-call | tf_op jit(solution)/shard_map/first/pallas_call | solution.py:478
  39.3 22.9 %all_to_all.10 = f32[128,1,128]{2,1,0:T(1,128)S(1)} all-to-all(f32[128,1,128]{2,1,0:T(1,128)S(1)} %bitcast.17), channel_id=1, replica_groups=mesh['leaf_0'=4,'leaf_1'=4,'leaf_2'=4,'leaf_3'=2,'player'=2] {'leaf_0','..., dimensions={0} | all-to-all | bytes 131072 | tf_op jit(solution)/shard_map/all_to_all | solution.py:612
  62.2 4.5 %second.1 = (f32[32,1326]{1,0:T(8,128)}, f32[32,1408]{1,0:T(8,128)S(1)}, f32[32,1408]{1,0:T(8,128)S(1)}, f32[128,128]{1,0:T(8,128)S(1)}) custom-call(f32[128,128]{1,0:T(8,128)S(1)} %bitcast.15, f32[2,64,1408]{2,1,0:T(8,128)S(1)} %get-tuple-element.44.window_ref, f32[64,1408]{1,0:T(8,128)S(1)} %get-tuple-element.45.reached_ref, ...), custom_call_target="tpu_custom_call" | custom-call | tf_op jit(solution)/shard_map/second/pallas_call | solution.py:554
  66.7 15.4 %all_to_all.11 = f32[128,1,128]{2,1,0:T(1,128)S(1)} all-to-all(f32[128,1,128]{2,1,0:T(1,128)S(1)} %bitcast.18), channel_id=1, replica_groups=mesh['leaf_0'=4,'leaf_1'=4,'leaf_2'=4,'leaf_3'=2,'player'=2] {'leaf_0','..., dimensions={0} | all-to-all | bytes 131072 | tf_op jit(solution)/shard_map/all_to_all | solution.py:612
  82.1 0.8 tail.1
  (1 shorter events, 0.0 us)
Async XLA Ops:
  1.9 26.9 %collective-permute-start.2 = (f32[35,1326]{1,0:T(8,128)S(1)}, f32[35,1326]{1,0:T(8,128)S(1)}, u32[]{:S(2)}, u32[]{:S(2)}) collective-permute-start(f32[35,1326]{1,0:T(8,128)S(1)} %get-tuple-element.31.regrets_ref), channel_id=1, source_target_pairs={{0,1},{1,0},{2,3},{3,2},{4,5},{5,4},{6,7},{7,6},{8,9},{9,8},{10,11... | collective-permute-start | bytes 556928 | tf_op jit(solution)/shard_map/ppermute | solution.py:602
  9.7 17.4 %collective-permute-start = (f32[32,1326]{1,0:T(8,128)S(1)}, f32[32,1326]{1,0:T(8,128)S(1)}, u32[]{:S(2)}, u32[]{:S(2)}) collective-permute-start(f32[32,1326]{1,0:T(8,128)S(1)} %get-tuple-element.28), channel_id=1, source_target_pairs={{0,2},{2,0},{4,6},{6,4},{8,10},{10,8},{12,14},{14,12},{16,18},{18,... | collective-permute-start | bytes 509192 | tf_op jit(solution)/shard_map/ppermute | solution.py:601
  10.6 18.2 %collective-permute-start.1 = (f32[32,1326]{1,0:T(8,128)S(1)}, f32[32,1326]{1,0:T(8,128)S(1)}, u32[]{:S(2)}, u32[]{:S(2)}) collective-permute-start(f32[32,1326]{1,0:T(8,128)S(1)} %get-tuple-element.29), channel_id=1, source_target_pairs={{2,4},{6,8},{10,12},{14,16},{18,20},{22,24},{26,28},{30,32},{34,36... | collective-permute-start | bytes 509192 | tf_op jit(solution)/shard_map/ppermute | solution.py:600
  13.2 19.8 %collective-permute-start.3 = (f32[30,1326]{1,0:T(8,128)S(1)}, f32[30,1326]{1,0:T(8,128)S(1)}, u32[]{:S(2)}, u32[]{:S(2)}) collective-permute-start(f32[30,1326]{1,0:T(8,128)S(1)} %get-tuple-element.36.chance_ref), channel_id=1, source_target_pairs={{0,1},{1,0},{2,3},{3,2},{4,5},{5,4},{6,7},{7,6},{8,9},{9,8},{10,11... | collective-permute-start | bytes 477368 | tf_op jit(solution)/shard_map/ppermute | solution.py:603
  13.3 19.8 %collective-permute-start.5 = (f32[16,1326]{1,0:T(8,128)S(1)}, f32[16,1326]{1,0:T(8,128)S(1)}, u32[]{:S(2)}, u32[]{:S(2)}) collective-permute-start(f32[16,1326]{1,0:T(8,128)S(1)} %get-tuple-element.37), channel_id=1, source_target_pairs={{2,5},{3,4},{6,9},{7,8},{10,13},{11,12},{14,17},{15,16},{18,21},{1... | collective-permute-start | bytes 254600 | tf_op jit(solution)/shard_map/ppermute | solution.py:604
  33.0 1.4 %collective-permute-start.4 = (f32[16,1326]{1,0:T(8,128)S(1)}, f32[16,1326]{1,0:T(8,128)S(1)}, u32[]{:S(2)}, u32[]{:S(2)}) collective-permute-start(f32[16,1326]{1,0:T(8,128)S(1)} %forward.1), channel_id=1, source_target_pairs={{0,2},{2,0},{4,6},{6,4},{8,10},{10,8},{12,14},{14,12},{16,18},{18,... | collective-permute-start | bytes 254600 | tf_op jit(solution)/shard_map/ppermute | solution.py:609

commit v8 on v7

--- a/solution.py
+++ b/solution.py
@@ -51,32 +51,9 @@
     edge_ref[15:16] = jnp.zeros((1, HANDS), F32)
 
 
-def forward_kernel(regrets_ref, chance_ref, after_ref, edge_ref):
-    odd = is_odd()
-
-    @pl.when(odd)
-    def _():
-        edge_rows(regrets_ref, chance_ref, edge_ref, False)
-
-    @pl.when(jnp.logical_not(odd))
-    def _():
-        edge_rows(regrets_ref, chance_ref, edge_ref, True)
-
-
-def forward(regrets, chance, after):
-    return pl.pallas_call(
-        forward_kernel,
-        out_shape=jax.ShapeDtypeStruct((16, HANDS), F32),
-        in_specs=[VMEM()] * 3,
-        out_specs=VMEM(),
-        compiler_params=pltpu.CompilerParams(vmem_limit_bytes=SMALL),
-        name="forward",
-    )(regrets, chance, after)
-
-
 def pack_kernel(
     boards_hbm, pot_hbm, regrets_hbm, chance_hbm, rank_hbm, cards_hbm, parent_hbm,
-    regrets_ref, chance_ref, even_ref, cross_ref, cross_other_ref,
+    regrets_ref, chance_ref, even_ref, cross_ref, even_other_ref, cross_other_ref,
     wide_rank_ref, free_ref, holding_ref, pots_ref, nodes_ref,
     board_cards_ref, pot_ref, rank_ref, cards_ref, parent_ref, all_chance_ref, sems,
 ):
@@ -153,12 +130,14 @@
     def _():
         ends(even_ref, False)
         ends(cross_ref, True)
+        edge_rows(regrets_ref, chance_ref, even_other_ref, False)
         edge_rows(regrets_ref, chance_ref, cross_other_ref, True)
 
     @pl.when(jnp.logical_not(odd))
     def _():
         ends(even_ref, True)
         ends(cross_ref, False)
+        edge_rows(regrets_ref, chance_ref, even_other_ref, True)
         edge_rows(regrets_ref, chance_ref, cross_other_ref, False)
 
     regrets_ref[OWN : OWN + 1] = jnp.zeros((1, HANDS), F32)
@@ -178,6 +157,7 @@
         jax.ShapeDtypeStruct((OWN - EARLY, HANDS), F32),
         jax.ShapeDtypeStruct((EDGE, HANDS), F32),
         jax.ShapeDtypeStruct((EDGE, HANDS), F32),
+        jax.ShapeDtypeStruct((16, HANDS), F32),
         jax.ShapeDtypeStruct((16, HANDS), F32),
         jax.ShapeDtypeStruct((8, WIDE), F32),
         jax.ShapeDtypeStruct((8, WIDE), F32),
@@ -211,21 +191,18 @@
     return jnp.where(odd, even, cross), jnp.where(odd, cross, even)
 
 
-ROWS = 128
-
-
-def fill(rank_ref, apart_ref, column_ref, targets):
+def fill(rank_ref, apart_ref, column_ref, targets, step):
     ranks = rank_ref[...]
     for t in range(WIDE // 128):
         lanes = slice(t * 128, (t + 1) * 128)
         tile = jnp.concatenate([ranks[:, lanes], jnp.zeros((120, 128), F32)], axis=0)
         column_ref[lanes, :] = tile.T
 
-    @pl.loop(0, WIDE // ROWS)
+    @pl.loop(0, WIDE // step)
     def _(i):
-        rows = pl.ds(pl.multiple_of(i * ROWS, ROWS), ROWS)
+        rows = pl.ds(pl.multiple_of(i * step, step), step)
         column = column_ref[rows, :]
-        own = [jnp.broadcast_to(column[:, b : b + 1], (ROWS, 128)) for b, _, _ in targets]
+        own = [jnp.broadcast_to(column[:, b : b + 1], (step, 128)) for b, _, _ in targets]
         for t in range(WIDE // 128):
             lanes = slice(t * 128, (t + 1) * 128)
             apart = apart_ref[rows, lanes]
@@ -241,7 +218,7 @@
     for rows in (slice(0, half), slice(half, WIDE)):
         shared = jnp.dot(holding.T[rows], holding, preferred_element_type=F32)
         apart_ref[rows, :] = (1.0 - jnp.minimum(shared, 1.0)).astype(BF16)
-    fill(rank_ref, apart_ref, column_ref, [(b, matrix_ref, b) for b in range(4)])
+    fill(rank_ref, apart_ref, column_ref, [(b, matrix_ref, b) for b in range(4)], 352)
 
 
 def outer_boards(mine, other):
@@ -272,11 +249,11 @@
     rank_ref[...] = jnp.zeros_like(rank_ref)
     rank_ref[0:2, :HANDS] = left
     rank_ref[2:4, :HANDS] = right
-    fill(rank_ref, apart_ref, column_ref, [(1, near_ref, 0), (2, near_ref, 1)])
+    fill(rank_ref, apart_ref, column_ref, [(1, near_ref, 0), (2, near_ref, 1)], 704)
 
     @pl.when(outer)
     def _():
-        fill(rank_ref, apart_ref, column_ref, [(0, far_ref, 0), (3, far_ref, 1)])
+        fill(rank_ref, apart_ref, column_ref, [(0, far_ref, 0), (3, far_ref, 1)], 704)
 
 
 BUILD_COST = pl.CostEstimate(
@@ -591,9 +568,10 @@
     cross_pairs = [(i, i + 1) for i in range(1, devices - 1, 2)]
     cross_pairs = cross_pairs + [(j, i) for i, j in cross_pairs]
 
-    diagonal = [(2 * i + p, 2 * j + 1 - p) for i, j in cross_pairs for p in range(2)]
-
-    regrets, chance, even, cross, cross_other, ranks, free, holding, pots, nodes = pack(
+    def diagonal(pairs):
+        return [(2 * i + p, 2 * j + 1 - p) for i, j in pairs for p in range(2)]
+
+    regrets, chance, even, cross, even_other, cross_other, ranks, free, holding, pots, nodes = pack(
         board_cards, pot[None], regrets_start[0], chance_reach[0], hand_rank,
         hand_cards.T, parent.reshape(-1, 128),
     )
@@ -601,12 +579,13 @@
     even = lax.ppermute(even, LEAF, even_pairs)
     regrets_other = lax.ppermute(regrets, "player", [(0, 1), (1, 0)])
     chance_other = lax.ppermute(chance, "player", [(0, 1), (1, 0)])
-    cross_other = lax.ppermute(cross_other, LEAF + ("player",), diagonal)
+    both = LEAF + ("player",)
+    even_other = lax.ppermute(even_other, both, diagonal(even_pairs))
+    cross_other = lax.ppermute(cross_other, both, diagonal(cross_pairs))
 
     own_matrix, apart = build_own(holding, ranks)
     near, far, outer = build_side(even, cross, nodes, regrets_other, apart)
 
-    even_other = lax.ppermute(forward(regrets_other, chance_other, outer), LEAF, even_pairs)
 
     def gathered(sums):
         return lax.all_to_all(sums.reshape(devices, 1, 128), LEAF, 0, 0).reshape(128, 128)

time: 83.2 us -> 85.4 us (1.026)
  blocking collectives: 38.3 us -> 41.7 us
  waiting for transfers between devices: 2.99 us -> 1.23 us
    all_to_all x2, blocking collectives: 38.3 us -> 41.7 us  [gathered(): lax.all_to_all(sums.reshape(devices, 1, 128), LEAF, 0, 0).reshape(128, 128)]
    ppermute x1, starting transfers between devices: 7.83 us -> 5.19 us  [local(): regrets_other = lax.ppermute(regrets, 'player', [(0, 1), (1, 0)])]
    ppermute x1, starting transfers between devices: 0.95 us -> 3.33 us  [local(): even = lax.ppermute(even, LEAF, even_pairs)]
    ppermute x2, waiting for transfers between devices: 1.27 us -> 0.01 us  [the longest x1 0.01 us: local(): even_other = lax.ppermute(even_other, both, diagonal(even_pairs))]
  transfers between devices with their start and end apart: 6 -> 6, of which waited for: 2 -> 1; matrix products, arithmetic and copies ran while one was open for 0% -> 0% of each run, Pallas kernels for 13% -> 12%
where the time goes in v8:
time: 85.4 us; the launch traced here: 84.6 us
  blocking collectives  41.7 us (49%)
  Pallas kernels  22 us (26%)
  starting transfers between devices  18.9 us (22%)
  waiting for transfers between devices  1.23 us (1%)
    all_to_all x2, blocking collectives, gathered(): lax.all_to_all(sums.reshape(devices, 1, 128), LEAF, 0, 0).reshape(128, 128)  41.7 us
    pallas_call x1, Pallas kernels, build_own(): pl.pallas_call(build_own_kernel, out_shape=(matrices_shape(4), jax.ShapeD...  6.16 us
    ppermute x1, starting transfers between devices, local(): regrets_other = lax.ppermute(regrets, 'player', [(0, 1), (1, 0)])  5.19 us
    pallas_call x1, Pallas kernels, first(): pl.pallas_call(first_kernel, out_shape=shapes, in_specs=[VMEM()] * len(ar...  4.98 us
    pallas_call x1, Pallas kernels, second(): pl.pallas_call(functools.partial(second_kernel, count=count), out_shape=s...  4.52 us
    pallas_call x1, Pallas kernels, build_side(): pl.pallas_call(build_side_kernel, out_shape=(matrices_shape(2), matrices_...  4.37 us
    ppermute x1, starting transfers between devices, local(): cross_other = lax.ppermute(cross_other, both, diagonal(cross_pairs))  3.7 us
    ppermute x1, starting transfers between devices, local(): even_other = lax.ppermute(even_other, both, diagonal(even_pairs))  3.67 us
  transfers between devices with their start and end apart: 6, of which 1 were waited for; matrix products, arithmetic and copies ran while one was open for 0% of the time, Pallas kernels for 12%

profile of v8, /device:TPU:1, one launch (start us, length us, event | category | flops | bytes accessed | tf_op | source)
XLA Modules:
  0.0 84.6 jit_solution(441255977020692700)
XLA Ops:
  0.6 1.2 %pack.1 = (f32[35,1326]{1,0:T(8,128)S(1)}, f32[30,1326]{1,0:T(8,128)S(1)}, f32[32,1326]{1,0:T(8,128)S(1)}, f32[32,1326]{1,0:T(8,128)S(1)}, f32[16,1326]{1,0:T(8,...) custom-call(s32[4,5]{1,0:T(4,128)} %boards_hbm.1, ...), custom_call_target="tpu_custom_call" | custom-call | tf_op jit(solution)/shard_map/pack/pallas_call | solution.py:169
  1.9 3.3 %collective-permute-start = (f32[32,1326]{1,0:T(8,128)S(1)}, f32[32,1326]{1,0:T(8,128)S(1)}, u32[]{:S(2)}, u32[]{:S(2)}) collective-permute-start(f32[32,1326]{1,0:T(8,128)S(1)} %get-tuple-element.29), channel_id=1, source_target_pairs={{0,2},{2,0},{4,6},{6,4},{8,10},{10,8},{12,14},{14,12},{16,18},{18,... | collective-permute-start | bytes 509192 | tf_op jit(solution)/shard_map/ppermute | solution.py:579
  5.2 5.2 %collective-permute-start.2 = (f32[35,1326]{1,0:T(8,128)S(1)}, f32[35,1326]{1,0:T(8,128)S(1)}, u32[]{:S(2)}, u32[]{:S(2)}) collective-permute-start(f32[35,1326]{1,0:T(8,128)S(1)} %get-tuple-element.32.regrets_ref), channel_id=1, source_target_pairs={{0,1},{1,0},{2,3},{3,2},{4,5},{5,4},{6,7},{7,6},{8,9},{9,8},{10,11... | collective-permute-start | bytes 556928 | tf_op jit(solution)/shard_map/ppermute | solution.py:580
  10.4 2.9 %collective-permute-start.1 = (f32[32,1326]{1,0:T(8,128)S(1)}, f32[32,1326]{1,0:T(8,128)S(1)}, u32[]{:S(2)}, u32[]{:S(2)}) collective-permute-start(f32[32,1326]{1,0:T(8,128)S(1)} %get-tuple-element.30), channel_id=1, source_target_pairs={{2,4},{6,8},{10,12},{14,16},{18,20},{22,24},{26,28},{30,32},{34,36... | collective-permute-start | bytes 509192 | tf_op jit(solution)/shard_map/ppermute | solution.py:578
  13.3 0.1 collective-permute-start.3
  13.4 3.7 %collective-permute-start.4 = (f32[16,1326]{1,0:T(8,128)S(1)}, f32[16,1326]{1,0:T(8,128)S(1)}, u32[]{:S(2)}, u32[]{:S(2)}) collective-permute-start(f32[16,1326]{1,0:T(8,128)S(1)} %get-tuple-element.38), channel_id=1, source_target_pairs={{0,3},{1,2},{2,1},{3,0},{4,7},{5,6},{6,5},{7,4},{8,11},{9,10},{10,... | collective-permute-start | bytes 254600 | tf_op jit(solution)/shard_map/ppermute | solution.py:583
  17.0 0.0 collective-permute-done.even_ref
  17.1 3.7 %collective-permute-start.5 = (f32[16,1326]{1,0:T(8,128)S(1)}, f32[16,1326]{1,0:T(8,128)S(1)}, u32[]{:S(2)}, u32[]{:S(2)}) collective-permute-start(f32[16,1326]{1,0:T(8,128)S(1)} %get-tuple-element.39), channel_id=1, source_target_pairs={{2,5},{3,4},{6,9},{7,8},{10,13},{11,12},{14,17},{15,16},{18,21},{1... | collective-permute-start | bytes 254600 | tf_op jit(solution)/shard_map/ppermute | solution.py:584
  20.8 6.2 %build_own.1 = (bf16[4,1408,1408]{2,1,0:T(8,128)(2,1)S(1)}, bf16[1408,1408]{1,0:T(8,128)(2,1)S(1)}) custom-call(bf16[128,1408]{1,0:T(8,128)(2,1)S(1)} %get-tuple-element.33.holding_ref, f32[8,1408]{1,0:T(8,128)S(1)} %get-tuple-element.34.rank_ref), custom_call_target="tpu_custom_call" | custom-call | flops 63438848 | bytes 15859712 | tf_op jit(solution)/shard_map/build_own/pallas_call | solution.py:269
  26.9 1.2 %collective-permute-done.1.cross_ref = f32[32,1326]{1,0:T(8,128)S(1)} collective-permute-done((f32[32,1326]{1,0:T(8,128)S(1)}, f32[32,1326]{1,0:T(8,128)S(1)}, u32[]{:S(2)}, u32[]{:S(2)}) %collective-permute-start.1) | collective-permute-done | bytes 169760 | tf_op jit(solution)/shard_map/ppermute | solution.py:578
  28.1 0.0 collective-permute-done.2.regrets_other_ref
  28.1 4.4 %build_side.1 = (bf16[2,1408,1408]{2,1,0:T(8,128)(2,1)S(1)}, bf16[2,1408,1408]{2,1,0:T(8,128)(2,1)S(1)}, f32[8,128]{1,0:T(8,128)S(1)}) custom-call(f32[32,1326]{1,0:T(8,128)S(1)} %collective-permute-done.even_ref, f32[32,1326]{1,0:T(8,128)S(1)} %collective-permute-done.1.cross_ref, f32[8,128]{1,0:T(8,128)S(1)} %get-tuple-element.31.nodes_ref, ...), custom_call_target="tpu_custom_call" | custom-call | flops 63438848 | bytes 15859712 | tf_op jit(solution)/shard_map/build_side/pallas_call | solution.py:282
  32.5 0.0 collective-permute-done.4.even_other_ref
  32.5 0.0 collective-permute-done.5.cross_other_ref
  32.5 0.0 collective-permute-done.3.chance_other_ref
  32.6 5.0 %first.1 = (f32[2,64,1408]{2,1,0:T(8,128)S(1)}, f32[64,1408]{1,0:T(8,128)S(1)}, f32[2,64,1408]{2,1,0:T(8,128)S(1)}, f32[128,128]{1,0:T(8,128)S(1)}, bf16[2,64,19...) custom-call(f32[8,128]{1,0:T(8,128)S(1)} %get-tuple-element.36.outer_ref, ...), custom_call_target="tpu_custom_call" | custom-call | tf_op jit(solution)/shard_map/first/pallas_call | solution.py:455
  37.5 26.3 %all_to_all.10 = f32[128,1,128]{2,1,0:T(1,128)S(1)} all-to-all(f32[128,1,128]{2,1,0:T(1,128)S(1)} %bitcast.17), channel_id=1, replica_groups=mesh['leaf_0'=4,'leaf_1'=4,'leaf_2'=4,'leaf_3'=2,'player'=2] {'leaf_0','..., dimensions={0} | all-to-all | bytes 131072 | tf_op jit(solution)/shard_map/all_to_all | solution.py:591
  63.9 4.5 %second.1 = (f32[32,1326]{1,0:T(8,128)}, f32[32,1408]{1,0:T(8,128)S(1)}, f32[32,1408]{1,0:T(8,128)S(1)}, f32[128,128]{1,0:T(8,128)S(1)}) custom-call(f32[128,128]{1,0:T(8,128)S(1)} %bitcast.15, f32[2,64,1408]{2,1,0:T(8,128)S(1)} %get-tuple-element.46.window_ref, f32[64,1408]{1,0:T(8,128)S(1)} %get-tuple-element.47.reached_ref, ...), custom_call_target="tpu_custom_call" | custom-call | tf_op jit(solution)/shard_map/second/pallas_call | solution.py:531
  68.4 15.4 %all_to_all.11 = f32[128,1,128]{2,1,0:T(1,128)S(1)} all-to-all(f32[128,1,128]{2,1,0:T(1,128)S(1)} %bitcast.18), channel_id=1, replica_groups=mesh['leaf_0'=4,'leaf_1'=4,'leaf_2'=4,'leaf_3'=2,'player'=2] {'leaf_0','..., dimensions={0} | all-to-all | bytes 131072 | tf_op jit(solution)/shard_map/all_to_all | solution.py:591
  83.8 0.8 tail.1
Async XLA Ops:
  1.9 15.2 %collective-permute-start = (f32[32,1326]{1,0:T(8,128)S(1)}, f32[32,1326]{1,0:T(8,128)S(1)}, u32[]{:S(2)}, u32[]{:S(2)}) collective-permute-start(f32[32,1326]{1,0:T(8,128)S(1)} %get-tuple-element.29), channel_id=1, source_target_pairs={{0,2},{2,0},{4,6},{6,4},{8,10},{10,8},{12,14},{14,12},{16,18},{18,... | collective-permute-start | bytes 509192 | tf_op jit(solution)/shard_map/ppermute | solution.py:579
  5.2 22.9 %collective-permute-start.2 = (f32[35,1326]{1,0:T(8,128)S(1)}, f32[35,1326]{1,0:T(8,128)S(1)}, u32[]{:S(2)}, u32[]{:S(2)}) collective-permute-start(f32[35,1326]{1,0:T(8,128)S(1)} %get-tuple-element.32.regrets_ref), channel_id=1, source_target_pairs={{0,1},{1,0},{2,3},{3,2},{4,5},{5,4},{6,7},{7,6},{8,9},{9,8},{10,11... | collective-permute-start | bytes 556928 | tf_op jit(solution)/shard_map/ppermute | solution.py:580
  10.4 17.7 %collective-permute-start.1 = (f32[32,1326]{1,0:T(8,128)S(1)}, f32[32,1326]{1,0:T(8,128)S(1)}, u32[]{:S(2)}, u32[]{:S(2)}) collective-permute-start(f32[32,1326]{1,0:T(8,128)S(1)} %get-tuple-element.30), channel_id=1, source_target_pairs={{2,4},{6,8},{10,12},{14,16},{18,20},{22,24},{26,28},{30,32},{34,36... | collective-permute-start | bytes 509192 | tf_op jit(solution)/shard_map/ppermute | solution.py:578
  13.3 19.3 %collective-permute-start.3 = (f32[30,1326]{1,0:T(8,128)S(1)}, f32[30,1326]{1,0:T(8,128)S(1)}, u32[]{:S(2)}, u32[]{:S(2)}) collective-permute-start(f32[30,1326]{1,0:T(8,128)S(1)} %get-tuple-element.37.chance_ref), channel_id=1, source_target_pairs={{0,1},{1,0},{2,3},{3,2},{4,5},{5,4},{6,7},{7,6},{8,9},{9,8},{10,11... | collective-permute-start | bytes 477368 | tf_op jit(solution)/shard_map/ppermute | solution.py:581
  13.4 19.1 %collective-permute-start.4 = (f32[16,1326]{1,0:T(8,128)S(1)}, f32[16,1326]{1,0:T(8,128)S(1)}, u32[]{:S(2)}, u32[]{:S(2)}) collective-permute-start(f32[16,1326]{1,0:T(8,128)S(1)} %get-tuple-element.38), channel_id=1, source_target_pairs={{0,3},{1,2},{2,1},{3,0},{4,7},{5,6},{6,5},{7,4},{8,11},{9,10},{10,... | collective-permute-start | bytes 254600 | tf_op jit(solution)/shard_map/ppermute | solution.py:583
  17.1 15.5 %collective-permute-start.5 = (f32[16,1326]{1,0:T(8,128)S(1)}, f32[16,1326]{1,0:T(8,128)S(1)}, u32[]{:S(2)}, u32[]{:S(2)}) collective-permute-start(f32[16,1326]{1,0:T(8,128)S(1)} %get-tuple-element.39), channel_id=1, source_target_pairs={{2,5},{3,4},{6,9},{7,8},{10,13},{11,12},{14,17},{15,16},{18,21},{1... | collective-permute-start | bytes 254600 | tf_op jit(solution)/shard_map/ppermute | solution.py:584

commit v9 on v7

--- a/solution.py
+++ b/solution.py
@@ -21,7 +21,7 @@
 BOARD_LEAVES = 8
 EDGE = 32
 EARLY = 2
-LIMIT = 10 << 20
+LIMIT = 7 << 20
 SMALL = 6 << 20
 PIECES = 2
 BF16 = jnp.bfloat16
@@ -211,21 +211,18 @@
     return jnp.where(odd, even, cross), jnp.where(odd, cross, even)
 
 
-ROWS = 128
-
-
-def fill(rank_ref, apart_ref, column_ref, targets):
+def fill(rank_ref, apart_ref, column_ref, targets, step):
     ranks = rank_ref[...]
     for t in range(WIDE // 128):
         lanes = slice(t * 128, (t + 1) * 128)
         tile = jnp.concatenate([ranks[:, lanes], jnp.zeros((120, 128), F32)], axis=0)
         column_ref[lanes, :] = tile.T
 
-    @pl.loop(0, WIDE // ROWS)
+    @pl.loop(0, WIDE // step)
     def _(i):
-        rows = pl.ds(pl.multiple_of(i * ROWS, ROWS), ROWS)
+        rows = pl.ds(pl.multiple_of(i * step, step), step)
         column = column_ref[rows, :]
-        own = [jnp.broadcast_to(column[:, b : b + 1], (ROWS, 128)) for b, _, _ in targets]
+        own = [jnp.broadcast_to(column[:, b : b + 1], (step, 128)) for b, _, _ in targets]
         for t in range(WIDE // 128):
             lanes = slice(t * 128, (t + 1) * 128)
             apart = apart_ref[rows, lanes]
@@ -241,7 +238,7 @@
     for rows in (slice(0, half), slice(half, WIDE)):
         shared = jnp.dot(holding.T[rows], holding, preferred_element_type=F32)
         apart_ref[rows, :] = (1.0 - jnp.minimum(shared, 1.0)).astype(BF16)
-    fill(rank_ref, apart_ref, column_ref, [(b, matrix_ref, b) for b in range(4)])
+    fill(rank_ref, apart_ref, column_ref, [(b, matrix_ref, b) for b in range(4)], 352)
 
 
 def outer_boards(mine, other):
@@ -262,21 +259,32 @@
     return (begin < BOARD_LEAVES) | (end >= WINDOW - BOARD_LEAVES)
 
 
-def build_side_kernel(
-    even_ref, cross_ref, nodes_ref, regrets_other_ref, apart_ref,
-    near_ref, far_ref, outer_ref, rank_ref, column_ref,
-):
-    outer = outer_boards(nodes_ref[0:1, :], regrets_other_ref[OWN : OWN + 1, 0:128])
-    outer_ref[...] = jnp.where(outer, jnp.ones_like(outer_ref), jnp.zeros_like(outer_ref))
+def side_ranks(even_ref, cross_ref, rank_ref):
     left, right = sides(even_ref, cross_ref, slice(25, 27))
     rank_ref[...] = jnp.zeros_like(rank_ref)
     rank_ref[0:2, :HANDS] = left
     rank_ref[2:4, :HANDS] = right
-    fill(rank_ref, apart_ref, column_ref, [(1, near_ref, 0), (2, near_ref, 1)])
+
+
+def build_near_kernel(
+    even_ref, cross_ref, apart_ref, near_ref, token_ref, rank_ref, column_ref
+):
+    token_ref[...] = jnp.zeros_like(token_ref)
+    side_ranks(even_ref, cross_ref, rank_ref)
+    fill(rank_ref, apart_ref, column_ref, [(1, near_ref, 0), (2, near_ref, 1)], 128)
+
+
+def build_far_kernel(
+    even_ref, cross_ref, nodes_ref, regrets_other_ref, apart_ref, after_ref,
+    far_ref, outer_ref, rank_ref, column_ref,
+):
+    outer = outer_boards(nodes_ref[0:1, :], regrets_other_ref[OWN : OWN + 1, 0:128])
+    outer_ref[...] = jnp.where(outer, jnp.ones_like(outer_ref), jnp.zeros_like(outer_ref))
 
     @pl.when(outer)
     def _():
-        fill(rank_ref, apart_ref, column_ref, [(0, far_ref, 0), (3, far_ref, 1)])
+        side_ranks(even_ref, cross_ref, rank_ref)
+        fill(rank_ref, apart_ref, column_ref, [(0, far_ref, 0), (3, far_ref, 1)], 128)
 
 
 BUILD_COST = pl.CostEstimate(
@@ -301,21 +309,17 @@
     )(holding, ranks)
 
 
-def build_side(even, cross, nodes, regrets_other, apart):
+def build_pair(kernel, name, arrays):
     return pl.pallas_call(
-        build_side_kernel,
-        out_shape=(
-            matrices_shape(2),
-            matrices_shape(2),
-            jax.ShapeDtypeStruct((8, 128), F32),
-        ),
-        in_specs=[VMEM()] * 5,
-        out_specs=[VMEM()] * 3,
+        kernel,
+        out_shape=(matrices_shape(2), jax.ShapeDtypeStruct((8, 128), F32)),
+        in_specs=[VMEM()] * len(arrays),
+        out_specs=[VMEM()] * 2,
         scratch_shapes=[pltpu.VMEM((8, WIDE), F32), pltpu.VMEM((WIDE, 128), F32)],
         compiler_params=pltpu.CompilerParams(vmem_limit_bytes=LIMIT),
         cost_estimate=BUILD_COST,
-        name="build_side",
-    )(even, cross, nodes, regrets_other, apart)
+        name=name,
+    )(*arrays)
 
 
 def node_totals(same, values):
@@ -604,9 +608,12 @@
     cross_other = lax.ppermute(cross_other, LEAF + ("player",), diagonal)
 
     own_matrix, apart = build_own(holding, ranks)
-    near, far, outer = build_side(even, cross, nodes, regrets_other, apart)
-
-    even_other = lax.ppermute(forward(regrets_other, chance_other, outer), LEAF, even_pairs)
+    near, built = build_pair(build_near_kernel, "build_near", (even, cross, apart))
+    rows = forward(regrets_other, chance_other, built)
+    even_other = lax.ppermute(rows, LEAF, even_pairs)
+    far, outer = build_pair(
+        build_far_kernel, "build_far", (even, cross, nodes, regrets_other, apart, rows)
+    )
 
     def gathered(sums):
         return lax.all_to_all(sums.reshape(devices, 1, 128), LEAF, 0, 0).reshape(128, 128)

time: 83.2 us -> 82.5 us (level)
  waiting for transfers between devices: 2.99 us -> 1.98 us
    ppermute x1, waiting for transfers between devices: 1.27 us -> 0.14 us  [local(): even_other = lax.ppermute(rows, LEAF, even_pairs)]
    pallas_call x1 -> x2, Pallas kernels: 4.13 us -> 4.35 us  [build_pair(): pl.pallas_call(kernel, out_shape=(matrices_shape(2), jax.ShapeDtypeStruct...]
where the time goes in v9:
time: 82.5 us; the launch traced here: 82.3 us
  blocking collectives  38.5 us (47%)
  Pallas kernels  22.1 us (27%)
  starting transfers between devices  19 us (23%)
  waiting for transfers between devices  1.98 us (2%)
    all_to_all x2, blocking collectives, gathered(): lax.all_to_all(sums.reshape(devices, 1, 128), LEAF, 0, 0).reshape(128, 128)  38.5 us
    ppermute x1, starting transfers between devices, local(): regrets_other = lax.ppermute(regrets, 'player', [(0, 1), (1, 0)])  7.83 us
    ppermute x1, starting transfers between devices, local(): cross_other = lax.ppermute(cross_other, LEAF + ('player',), diagonal)  7.47 us
    pallas_call x1, Pallas kernels, build_own(): pl.pallas_call(build_own_kernel, out_shape=(matrices_shape(4), jax.ShapeD...  6.2 us
    pallas_call x1, Pallas kernels, first(): pl.pallas_call(first_kernel, out_shape=shapes, in_specs=[VMEM()] * len(ar...  4.99 us
    pallas_call x1, Pallas kernels, second(): pl.pallas_call(functools.partial(second_kernel, count=count), out_shape=s...  4.54 us
    pallas_call x2, Pallas kernels, build_pair(): pl.pallas_call(kernel, out_shape=(matrices_shape(2), jax.ShapeDtypeStruct...  4.35 us
    ppermute x1, starting transfers between devices, local(): cross = lax.ppermute(cross, LEAF, cross_pairs)  2.52 us
  transfers between devices with their start and end apart: 6, of which 2 were waited for; matrix products, arithmetic and copies ran while one was open for 0% of the time, Pallas kernels for 13%

profile of v9, /device:TPU:1, one launch (start us, length us, event | category | flops | bytes accessed | tf_op | source)
XLA Modules:
  0.0 82.3 jit_solution(5167709372783511874)
XLA Ops:
  0.6 1.2 %pack.1 = (f32[35,1326]{1,0:T(8,128)S(1)}, f32[30,1326]{1,0:T(8,128)S(1)}, f32[32,1326]{1,0:T(8,128)S(1)}, f32[32,1326]{1,0:T(8,128)S(1)}, f32[16,1326]{1,0:T(8,...) custom-call(s32[4,5]{1,0:T(4,128)} %boards_hbm.1, ...), custom_call_target="tpu_custom_call" | custom-call | tf_op jit(solution)/shard_map/pack/pallas_call | solution.py:189
  1.9 7.8 %collective-permute-start.2 = (f32[35,1326]{1,0:T(8,128)S(1)}, f32[35,1326]{1,0:T(8,128)S(1)}, u32[]{:S(2)}, u32[]{:S(2)}) collective-permute-start(f32[35,1326]{1,0:T(8,128)S(1)} %get-tuple-element.32.regrets_ref), channel_id=1, source_target_pairs={{0,1},{1,0},{2,3},{3,2},{4,5},{5,4},{6,7},{7,6},{8,9},{9,8},{10,11... | collective-permute-start | bytes 556928 | tf_op jit(solution)/shard_map/ppermute | solution.py:606
  9.7 0.9 %collective-permute-start = (f32[32,1326]{1,0:T(8,128)S(1)}, f32[32,1326]{1,0:T(8,128)S(1)}, u32[]{:S(2)}, u32[]{:S(2)}) collective-permute-start(f32[32,1326]{1,0:T(8,128)S(1)} %get-tuple-element.29), channel_id=1, source_target_pairs={{0,2},{2,0},{4,6},{6,4},{8,10},{10,8},{12,14},{14,12},{16,18},{18,... | collective-permute-start | bytes 509192 | tf_op jit(solution)/shard_map/ppermute | solution.py:605
  10.6 2.5 %collective-permute-start.1 = (f32[32,1326]{1,0:T(8,128)S(1)}, f32[32,1326]{1,0:T(8,128)S(1)}, u32[]{:S(2)}, u32[]{:S(2)}) collective-permute-start(f32[32,1326]{1,0:T(8,128)S(1)} %get-tuple-element.30), channel_id=1, source_target_pairs={{2,4},{6,8},{10,12},{14,16},{18,20},{22,24},{26,28},{30,32},{34,36... | collective-permute-start | bytes 509192 | tf_op jit(solution)/shard_map/ppermute | solution.py:604
  13.2 0.1 collective-permute-start.3
  13.3 7.5 %collective-permute-start.5 = (f32[16,1326]{1,0:T(8,128)S(1)}, f32[16,1326]{1,0:T(8,128)S(1)}, u32[]{:S(2)}, u32[]{:S(2)}) collective-permute-start(f32[16,1326]{1,0:T(8,128)S(1)} %get-tuple-element.39), channel_id=1, source_target_pairs={{2,5},{3,4},{6,9},{7,8},{10,13},{11,12},{14,17},{15,16},{18,21},{1... | collective-permute-start | bytes 254600 | tf_op jit(solution)/shard_map/ppermute | solution.py:608
  20.7 6.2 %build_own.1 = (bf16[4,1408,1408]{2,1,0:T(8,128)(2,1)S(1)}, bf16[1408,1408]{1,0:T(8,128)(2,1)S(1)}) custom-call(bf16[128,1408]{1,0:T(8,128)(2,1)S(1)} %get-tuple-element.33.holding_ref, f32[8,1408]{1,0:T(8,128)S(1)} %get-tuple-element.34.rank_ref), custom_call_target="tpu_custom_call" | custom-call | flops 63438848 | bytes 15859712 | tf_op jit(solution)/shard_map/build_own/pallas_call | solution.py:300
  26.9 0.0 collective-permute-done.even_ref
  27.0 1.8 %collective-permute-done.1.cross_ref = f32[32,1326]{1,0:T(8,128)S(1)} collective-permute-done((f32[32,1326]{1,0:T(8,128)S(1)}, f32[32,1326]{1,0:T(8,128)S(1)}, u32[]{:S(2)}, u32[]{:S(2)}) %collective-permute-start.1) | collective-permute-done | bytes 169760 | tf_op jit(solution)/shard_map/ppermute | solution.py:604
  28.8 3.2 %build_near.1 = (bf16[2,1408,1408]{2,1,0:T(8,128)(2,1)S(1)}, f32[8,128]{1,0:T(8,128)S(1)}) custom-call(f32[32,1326]{1,0:T(8,128)S(1)} %collective-permute-done.even_ref, f32[32,1326]{1,0:T(8,128)S(1)} %collective-permute-done.1.cross_ref, bf16[1408,1408]{1,0:T(8,128)(2,1)S(1)} %get-tuple-element.35.apart_ref), custom_call_target="tpu_custom_call" | custom-call | flops 63438848 | bytes 15859712 | tf_op jit(solution)/shard_map/build_near/pallas_call | solution.py:313
  32.0 0.0 collective-permute-done.3.chance_ref.chance_other_ref
  32.0 0.0 collective-permute-done.2.regrets_ref.regrets_other_ref
  32.1 0.1 collective-permute-start.4
  32.2 1.1 %build_far.1 = (bf16[2,1408,1408]{2,1,0:T(8,128)(2,1)S(1)}, f32[8,128]{1,0:T(8,128)S(1)}) custom-call(f32[32,1326]{1,0:T(8,128)S(1)} %collective-permute-done.even_ref, f32[32,1326]{1,0:T(8,128)S(1)} %collective-permute-done.1.cross_ref, f32[8,128]{1,0:T(8,128)S(1)} %get-tuple-element.31.nodes_ref, ...), custom_call_target="tpu_custom_call" | custom-call | flops 63438848 | bytes 15859712 | tf_op jit(solution)/shard_map/build_far/pallas_call | solution.py:313
  33.3 0.0 collective-permute-done.5.cross_other_ref
  33.3 0.1 collective-permute-done.4.even_other_ref
  33.5 5.0 %first.1 = (f32[2,64,1408]{2,1,0:T(8,128)S(1)}, f32[64,1408]{1,0:T(8,128)S(1)}, f32[2,64,1408]{2,1,0:T(8,128)S(1)}, f32[128,128]{1,0:T(8,128)S(1)}, bf16[2,64,19...) custom-call(f32[8,128]{1,0:T(8,128)S(1)} %get-tuple-element.38.outer_ref, ...), custom_call_target="tpu_custom_call" | custom-call | tf_op jit(solution)/shard_map/first/pallas_call | solution.py:482
  38.5 23.1 %all_to_all.10 = f32[128,1,128]{2,1,0:T(1,128)S(1)} all-to-all(f32[128,1,128]{2,1,0:T(1,128)S(1)} %bitcast.17), channel_id=1, replica_groups=mesh['leaf_0'=4,'leaf_1'=4,'leaf_2'=4,'leaf_3'=2,'player'=2] {'leaf_0','..., dimensions={0} | all-to-all | bytes 131072 | tf_op jit(solution)/shard_map/all_to_all | solution.py:619
  61.5 4.5 %second.1 = (f32[32,1326]{1,0:T(8,128)}, f32[32,1408]{1,0:T(8,128)S(1)}, f32[32,1408]{1,0:T(8,128)S(1)}, f32[128,128]{1,0:T(8,128)S(1)}) custom-call(f32[128,128]{1,0:T(8,128)S(1)} %bitcast.15, f32[2,64,1408]{2,1,0:T(8,128)S(1)} %get-tuple-element.46.window_ref, f32[64,1408]{1,0:T(8,128)S(1)} %get-tuple-element.47.reached_ref, ...), custom_call_target="tpu_custom_call" | custom-call | tf_op jit(solution)/shard_map/second/pallas_call | solution.py:558
  66.1 15.4 %all_to_all.11 = f32[128,1,128]{2,1,0:T(1,128)S(1)} all-to-all(f32[128,1,128]{2,1,0:T(1,128)S(1)} %bitcast.18), channel_id=1, replica_groups=mesh['leaf_0'=4,'leaf_1'=4,'leaf_2'=4,'leaf_3'=2,'player'=2] {'leaf_0','..., dimensions={0} | all-to-all | bytes 131072 | tf_op jit(solution)/shard_map/all_to_all | solution.py:619
  81.5 0.8 tail.1
  (1 shorter events, 0.0 us)
Async XLA Ops:
  1.9 30.2 %collective-permute-start.2 = (f32[35,1326]{1,0:T(8,128)S(1)}, f32[35,1326]{1,0:T(8,128)S(1)}, u32[]{:S(2)}, u32[]{:S(2)}) collective-permute-start(f32[35,1326]{1,0:T(8,128)S(1)} %get-tuple-element.32.regrets_ref), channel_id=1, source_target_pairs={{0,1},{1,0},{2,3},{3,2},{4,5},{5,4},{6,7},{7,6},{8,9},{9,8},{10,11... | collective-permute-start | bytes 556928 | tf_op jit(solution)/shard_map/ppermute | solution.py:606
  9.7 17.3 %collective-permute-start = (f32[32,1326]{1,0:T(8,128)S(1)}, f32[32,1326]{1,0:T(8,128)S(1)}, u32[]{:S(2)}, u32[]{:S(2)}) collective-permute-start(f32[32,1326]{1,0:T(8,128)S(1)} %get-tuple-element.29), channel_id=1, source_target_pairs={{0,2},{2,0},{4,6},{6,4},{8,10},{10,8},{12,14},{14,12},{16,18},{18,... | collective-permute-start | bytes 509192 | tf_op jit(solution)/shard_map/ppermute | solution.py:605
  10.6 18.2 %collective-permute-start.1 = (f32[32,1326]{1,0:T(8,128)S(1)}, f32[32,1326]{1,0:T(8,128)S(1)}, u32[]{:S(2)}, u32[]{:S(2)}) collective-permute-start(f32[32,1326]{1,0:T(8,128)S(1)} %get-tuple-element.30), channel_id=1, source_target_pairs={{2,4},{6,8},{10,12},{14,16},{18,20},{22,24},{26,28},{30,32},{34,36... | collective-permute-start | bytes 509192 | tf_op jit(solution)/shard_map/ppermute | solution.py:604
  13.2 18.9 %collective-permute-start.3 = (f32[30,1326]{1,0:T(8,128)S(1)}, f32[30,1326]{1,0:T(8,128)S(1)}, u32[]{:S(2)}, u32[]{:S(2)}) collective-permute-start(f32[30,1326]{1,0:T(8,128)S(1)} %get-tuple-element.36.chance_ref), channel_id=1, source_target_pairs={{0,1},{1,0},{2,3},{3,2},{4,5},{5,4},{6,7},{7,6},{8,9},{9,8},{10,11... | collective-permute-start | bytes 477368 | tf_op jit(solution)/shard_map/ppermute | solution.py:607
  13.3 20.1 %collective-permute-start.5 = (f32[16,1326]{1,0:T(8,128)S(1)}, f32[16,1326]{1,0:T(8,128)S(1)}, u32[]{:S(2)}, u32[]{:S(2)}) collective-permute-start(f32[16,1326]{1,0:T(8,128)S(1)} %get-tuple-element.39), channel_id=1, source_target_pairs={{2,5},{3,4},{6,9},{7,8},{10,13},{11,12},{14,17},{15,16},{18,21},{1... | collective-permute-start | bytes 254600 | tf_op jit(solution)/shard_map/ppermute | solution.py:608
  32.1 1.4 %collective-permute-start.4 = (f32[16,1326]{1,0:T(8,128)S(1)}, f32[16,1326]{1,0:T(8,128)S(1)}, u32[]{:S(2)}, u32[]{:S(2)}) collective-permute-start(f32[16,1326]{1,0:T(8,128)S(1)} %forward.1.after_ref), channel_id=1, source_target_pairs={{0,2},{2,0},{4,6},{6,4},{8,10},{10,8},{12,14},{14,12},{16,18},{18,... | collective-permute-start | bytes 254600 | tf_op jit(solution)/shard_map/ppermute | solution.py:613

commit v10 on v9

--- a/solution.py
+++ b/solution.py
@@ -19,7 +19,7 @@
 SIDE = 16
 WINDOW = OWN + 2 * SIDE
 BOARD_LEAVES = 8
-EDGE = 32
+EDGE = 31
 EARLY = 2
 LIMIT = 7 << 20
 SMALL = 6 << 20
@@ -48,7 +48,6 @@
         edge_ref[15 - EARLY : 15] = regrets_ref[OWN + 1 :]
     else:
         edge_ref[10:15] = chance_ref[0:5]
-    edge_ref[15:16] = jnp.zeros((1, HANDS), F32)
 
 
 def forward_kernel(regrets_ref, chance_ref, after_ref, edge_ref):
@@ -66,7 +65,7 @@
 def forward(regrets, chance, after):
     return pl.pallas_call(
         forward_kernel,
-        out_shape=jax.ShapeDtypeStruct((16, HANDS), F32),
+        out_shape=jax.ShapeDtypeStruct((15, HANDS), F32),
         in_specs=[VMEM()] * 3,
         out_specs=VMEM(),
         compiler_params=pltpu.CompilerParams(vmem_limit_bytes=SMALL),
@@ -178,7 +177,7 @@
         jax.ShapeDtypeStruct((OWN - EARLY, HANDS), F32),
         jax.ShapeDtypeStruct((EDGE, HANDS), F32),
         jax.ShapeDtypeStruct((EDGE, HANDS), F32),
-        jax.ShapeDtypeStruct((16, HANDS), F32),
+        jax.ShapeDtypeStruct((15, HANDS), F32),
         jax.ShapeDtypeStruct((8, WIDE), F32),
         jax.ShapeDtypeStruct((8, WIDE), F32),
         jax.ShapeDtypeStruct((128, WIDE), BF16),
@@ -325,9 +324,7 @@
 def node_totals(same, values):
     high = values.astype(BF16)
     rest = values - high.astype(F32)
-    middle = rest.astype(BF16)
-    low = (rest - middle.astype(F32)).astype(BF16)
-    parts = jnp.concatenate([high, middle, low], axis=0)
+    parts = jnp.concatenate([high, rest.astype(BF16)], axis=0)
     return jnp.dot(same, parts, preferred_element_type=F32)
 
 
@@ -353,7 +350,7 @@
 def same_node(row):
     equal = jnp.where(jnp.broadcast_to(row, (128, 128)) == column_of(row), 1.0, 0.0)
     equal = equal[:WINDOW, :WINDOW]
-    return jnp.concatenate([equal, equal, equal], axis=1).astype(BF16)
+    return jnp.concatenate([equal, equal], axis=1).astype(BF16)
 
 
 def board_rows(free, boards):
@@ -475,7 +472,7 @@
         jax.ShapeDtypeStruct((WINDOW, WIDE), F32),
         jax.ShapeDtypeStruct((2, WINDOW, WIDE), F32),
         jax.ShapeDtypeStruct((128, 128), F32),
-        jax.ShapeDtypeStruct((2, WINDOW, 3 * WINDOW), BF16),
+        jax.ShapeDtypeStruct((2, WINDOW, 2 * WINDOW), BF16),
         jax.ShapeDtypeStruct((8, WIDE), F32),
         jax.ShapeDtypeStruct((WINDOW, 128), F32),
     )

time: 82.5 us -> 82.3 us (level)
  no operation moved by 1% of the time
where the time goes in v10:
time: 82.3 us; the launch traced here: 82 us
  blocking collectives  38.5 us (47%)
  Pallas kernels  21.9 us (27%)
  starting transfers between devices  19 us (23%)
  waiting for transfers between devices  1.98 us (2%)
    all_to_all x2, blocking collectives, gathered(): lax.all_to_all(sums.reshape(devices, 1, 128), LEAF, 0, 0).reshape(128, 128)  38.5 us
    ppermute x1, starting transfers between devices, local(): regrets_other = lax.ppermute(regrets, 'player', [(0, 1), (1, 0)])  7.83 us
    ppermute x1, starting transfers between devices, local(): cross_other = lax.ppermute(cross_other, LEAF + ('player',), diagonal)  7.47 us
    pallas_call x1, Pallas kernels, build_own(): pl.pallas_call(build_own_kernel, out_shape=(matrices_shape(4), jax.ShapeD...  6.2 us
    pallas_call x1, Pallas kernels, first(): pl.pallas_call(first_kernel, out_shape=shapes, in_specs=[VMEM()] * len(ar...  4.8 us
    pallas_call x1, Pallas kernels, second(): pl.pallas_call(functools.partial(second_kernel, count=count), out_shape=s...  4.47 us
    pallas_call x2, Pallas kernels, build_pair(): pl.pallas_call(kernel, out_shape=(matrices_shape(2), jax.ShapeDtypeStruct...  4.35 us
    ppermute x1, starting transfers between devices, local(): cross = lax.ppermute(cross, LEAF, cross_pairs)  2.52 us
  transfers between devices with their start and end apart: 6, of which 2 were waited for; matrix products, arithmetic and copies ran while one was open for 0% of the time, Pallas kernels for 13%

profile of v10, /device:TPU:1, one launch (start us, length us, event | category | flops | bytes accessed | tf_op | source)
XLA Modules:
  0.0 82.0 jit_solution(14693490810965806349)
XLA Ops:
  0.6 1.2 %pack.1 = (f32[35,1326]{1,0:T(8,128)S(1)}, f32[30,1326]{1,0:T(8,128)S(1)}, f32[31,1326]{1,0:T(8,128)S(1)}, f32[31,1326]{1,0:T(8,128)S(1)}, f32[15,1326]{1,0:T(8,...) custom-call(s32[4,5]{1,0:T(4,128)} %boards_hbm.1, ...), custom_call_target="tpu_custom_call" | custom-call | tf_op jit(solution)/shard_map/pack/pallas_call | solution.py:188
  1.9 7.8 %collective-permute-start.2 = (f32[35,1326]{1,0:T(8,128)S(1)}, f32[35,1326]{1,0:T(8,128)S(1)}, u32[]{:S(2)}, u32[]{:S(2)}) collective-permute-start(f32[35,1326]{1,0:T(8,128)S(1)} %get-tuple-element.32.regrets_ref), channel_id=1, source_target_pairs={{0,1},{1,0},{2,3},{3,2},{4,5},{5,4},{6,7},{7,6},{8,9},{9,8},{10,11... | collective-permute-start | bytes 556928 | tf_op jit(solution)/shard_map/ppermute | solution.py:603
  9.7 1.0 %collective-permute-start = (f32[31,1326]{1,0:T(8,128)S(1)}, f32[31,1326]{1,0:T(8,128)S(1)}, u32[]{:S(2)}, u32[]{:S(2)}) collective-permute-start(f32[31,1326]{1,0:T(8,128)S(1)} %get-tuple-element.29), channel_id=1, source_target_pairs={{0,2},{2,0},{4,6},{6,4},{8,10},{10,8},{12,14},{14,12},{16,18},{18,... | collective-permute-start | bytes 493280 | tf_op jit(solution)/shard_map/ppermute | solution.py:602
  10.6 2.5 %collective-permute-start.1 = (f32[31,1326]{1,0:T(8,128)S(1)}, f32[31,1326]{1,0:T(8,128)S(1)}, u32[]{:S(2)}, u32[]{:S(2)}) collective-permute-start(f32[31,1326]{1,0:T(8,128)S(1)} %get-tuple-element.30), channel_id=1, source_target_pairs={{2,4},{6,8},{10,12},{14,16},{18,20},{22,24},{26,28},{30,32},{34,36... | collective-permute-start | bytes 493280 | tf_op jit(solution)/shard_map/ppermute | solution.py:601
  13.2 0.1 collective-permute-start.3
  13.3 7.5 %collective-permute-start.5 = (f32[15,1326]{1,0:T(8,128)S(1)}, f32[15,1326]{1,0:T(8,128)S(1)}, u32[]{:S(2)}, u32[]{:S(2)}) collective-permute-start(f32[15,1326]{1,0:T(8,128)S(1)} %get-tuple-element.39), channel_id=1, source_target_pairs={{2,5},{3,4},{6,9},{7,8},{10,13},{11,12},{14,17},{15,16},{18,21},{1... | collective-permute-start | bytes 238688 | tf_op jit(solution)/shard_map/ppermute | solution.py:605
  20.7 6.2 %build_own.1 = (bf16[4,1408,1408]{2,1,0:T(8,128)(2,1)S(1)}, bf16[1408,1408]{1,0:T(8,128)(2,1)S(1)}) custom-call(bf16[128,1408]{1,0:T(8,128)(2,1)S(1)} %get-tuple-element.33.holding_ref, f32[8,1408]{1,0:T(8,128)S(1)} %get-tuple-element.34.rank_ref), custom_call_target="tpu_custom_call" | custom-call | flops 63438848 | bytes 15859712 | tf_op jit(solution)/shard_map/build_own/pallas_call | solution.py:299
  26.9 0.0 collective-permute-done.even_ref
  27.0 1.8 %collective-permute-done.1.cross_ref = f32[31,1326]{1,0:T(8,128)S(1)} collective-permute-done((f32[31,1326]{1,0:T(8,128)S(1)}, f32[31,1326]{1,0:T(8,128)S(1)}, u32[]{:S(2)}, u32[]{:S(2)}) %collective-permute-start.1) | collective-permute-done | bytes 164456 | tf_op jit(solution)/shard_map/ppermute | solution.py:601
  28.8 3.2 %build_near.1 = (bf16[2,1408,1408]{2,1,0:T(8,128)(2,1)S(1)}, f32[8,128]{1,0:T(8,128)S(1)}) custom-call(f32[31,1326]{1,0:T(8,128)S(1)} %collective-permute-done.even_ref, f32[31,1326]{1,0:T(8,128)S(1)} %collective-permute-done.1.cross_ref, bf16[1408,1408]{1,0:T(8,128)(2,1)S(1)} %get-tuple-element.35.apart_ref), custom_call_target="tpu_custom_call" | custom-call | flops 63438848 | bytes 15859712 | tf_op jit(solution)/shard_map/build_near/pallas_call | solution.py:312
  32.0 0.0 collective-permute-done.3.chance_ref.chance_other_ref
  32.0 0.0 collective-permute-done.2.regrets_ref.regrets_other_ref
  32.1 0.1 collective-permute-start.4
  32.2 1.1 %build_far.1 = (bf16[2,1408,1408]{2,1,0:T(8,128)(2,1)S(1)}, f32[8,128]{1,0:T(8,128)S(1)}) custom-call(f32[31,1326]{1,0:T(8,128)S(1)} %collective-permute-done.even_ref, f32[31,1326]{1,0:T(8,128)S(1)} %collective-permute-done.1.cross_ref, f32[8,128]{1,0:T(8,128)S(1)} %get-tuple-element.31.nodes_ref, ...), custom_call_target="tpu_custom_call" | custom-call | flops 63438848 | bytes 15859712 | tf_op jit(solution)/shard_map/build_far/pallas_call | solution.py:312
  33.3 0.0 collective-permute-done.5.cross_other_ref
  33.3 0.1 collective-permute-done.4.even_other_ref
  33.5 4.8 %first.1 = (f32[2,64,1408]{2,1,0:T(8,128)S(1)}, f32[64,1408]{1,0:T(8,128)S(1)}, f32[2,64,1408]{2,1,0:T(8,128)S(1)}, f32[128,128]{1,0:T(8,128)S(1)}, bf16[2,64,12...) custom-call(f32[8,128]{1,0:T(8,128)S(1)} %get-tuple-element.38.outer_ref, ...), custom_call_target="tpu_custom_call" | custom-call | tf_op jit(solution)/shard_map/first/pallas_call | solution.py:479
  38.3 23.1 %all_to_all.10 = f32[128,1,128]{2,1,0:T(1,128)S(1)} all-to-all(f32[128,1,128]{2,1,0:T(1,128)S(1)} %bitcast.17), channel_id=1, replica_groups=mesh['leaf_0'=4,'leaf_1'=4,'leaf_2'=4,'leaf_3'=2,'player'=2] {'leaf_0','..., dimensions={0} | all-to-all | bytes 131072 | tf_op jit(solution)/shard_map/all_to_all | solution.py:616
  61.4 4.5 %second.1 = (f32[32,1326]{1,0:T(8,128)}, f32[32,1408]{1,0:T(8,128)S(1)}, f32[32,1408]{1,0:T(8,128)S(1)}, f32[128,128]{1,0:T(8,128)S(1)}) custom-call(f32[128,128]{1,0:T(8,128)S(1)} %bitcast.15, f32[2,64,1408]{2,1,0:T(8,128)S(1)} %get-tuple-element.46.window_ref, f32[64,1408]{1,0:T(8,128)S(1)} %get-tuple-element.47.reached_ref, ...), custom_call_target="tpu_custom_call" | custom-call | tf_op jit(solution)/shard_map/second/pallas_call | solution.py:555
  65.8 15.4 %all_to_all.11 = f32[128,1,128]{2,1,0:T(1,128)S(1)} all-to-all(f32[128,1,128]{2,1,0:T(1,128)S(1)} %bitcast.18), channel_id=1, replica_groups=mesh['leaf_0'=4,'leaf_1'=4,'leaf_2'=4,'leaf_3'=2,'player'=2] {'leaf_0','..., dimensions={0} | all-to-all | bytes 131072 | tf_op jit(solution)/shard_map/all_to_all | solution.py:616
  81.2 0.8 tail.1
  (1 shorter events, 0.0 us)
Async XLA Ops:
  1.9 30.2 %collective-permute-start.2 = (f32[35,1326]{1,0:T(8,128)S(1)}, f32[35,1326]{1,0:T(8,128)S(1)}, u32[]{:S(2)}, u32[]{:S(2)}) collective-permute-start(f32[35,1326]{1,0:T(8,128)S(1)} %get-tuple-element.32.regrets_ref), channel_id=1, source_target_pairs={{0,1},{1,0},{2,3},{3,2},{4,5},{5,4},{6,7},{7,6},{8,9},{9,8},{10,11... | collective-permute-start | bytes 556928 | tf_op jit(solution)/shard_map/ppermute | solution.py:603
  9.7 17.3 %collective-permute-start = (f32[31,1326]{1,0:T(8,128)S(1)}, f32[31,1326]{1,0:T(8,128)S(1)}, u32[]{:S(2)}, u32[]{:S(2)}) collective-permute-start(f32[31,1326]{1,0:T(8,128)S(1)} %get-tuple-element.29), channel_id=1, source_target_pairs={{0,2},{2,0},{4,6},{6,4},{8,10},{10,8},{12,14},{14,12},{16,18},{18,... | collective-permute-start | bytes 493280 | tf_op jit(solution)/shard_map/ppermute | solution.py:602
  10.6 18.2 %collective-permute-start.1 = (f32[31,1326]{1,0:T(8,128)S(1)}, f32[31,1326]{1,0:T(8,128)S(1)}, u32[]{:S(2)}, u32[]{:S(2)}) collective-permute-start(f32[31,1326]{1,0:T(8,128)S(1)} %get-tuple-element.30), channel_id=1, source_target_pairs={{2,4},{6,8},{10,12},{14,16},{18,20},{22,24},{26,28},{30,32},{34,36... | collective-permute-start | bytes 493280 | tf_op jit(solution)/shard_map/ppermute | solution.py:601
  13.2 18.9 %collective-permute-start.3 = (f32[30,1326]{1,0:T(8,128)S(1)}, f32[30,1326]{1,0:T(8,128)S(1)}, u32[]{:S(2)}, u32[]{:S(2)}) collective-permute-start(f32[30,1326]{1,0:T(8,128)S(1)} %get-tuple-element.36.chance_ref), channel_id=1, source_target_pairs={{0,1},{1,0},{2,3},{3,2},{4,5},{5,4},{6,7},{7,6},{8,9},{9,8},{10,11... | collective-permute-start | bytes 477368 | tf_op jit(solution)/shard_map/ppermute | solution.py:604
  13.3 20.1 %collective-permute-start.5 = (f32[15,1326]{1,0:T(8,128)S(1)}, f32[15,1326]{1,0:T(8,128)S(1)}, u32[]{:S(2)}, u32[]{:S(2)}) collective-permute-start(f32[15,1326]{1,0:T(8,128)S(1)} %get-tuple-element.39), channel_id=1, source_target_pairs={{2,5},{3,4},{6,9},{7,8},{10,13},{11,12},{14,17},{15,16},{18,21},{1... | collective-permute-start | bytes 238688 | tf_op jit(solution)/shard_map/ppermute | solution.py:605
  32.1 1.4 %collective-permute-start.4 = (f32[15,1326]{1,0:T(8,128)S(1)}, f32[15,1326]{1,0:T(8,128)S(1)}, u32[]{:S(2)}, u32[]{:S(2)}) collective-permute-start(f32[15,1326]{1,0:T(8,128)S(1)} %forward.1.after_ref), channel_id=1, source_target_pairs={{0,2},{2,0},{4,6},{6,4},{8,10},{10,8},{12,14},{14,12},{16,18},{18,... | collective-permute-start | bytes 238688 | tf_op jit(solution)/shard_map/ppermute | solution.py:610
